TPU v7x, 512 devices: a whole 4x4x16 slice. The times are simulated.
512 devices in a mesh: rx: 32 (over x, z_lo), ry: 16 (over z_hi, y, core).
Axes of the slice: x: 4, y: 4, z: 16 (z_hi: 2, z_lo: 8; z = z_hi * 8 + z_lo), core: 2. Of those that a mesh axis runs over, the one named last changes fastest.
Arguments:
- cell_input: bfloat16 [128, 64, 64, 128], P('rx', 'ry'), may hold values from -6 to 6
- w_filter: bfloat16 [2, 32, 32], replicated, may hold values from -0.75 to 0.75
- w_gate: bfloat16 [2, 32, 32], replicated, may hold values from -0.75 to 0.75
- bias_filter: float32 [32], replicated, may hold values from -3 to 3
- bias_gate: float32 [32], replicated, may hold values from -3 to 3
- adjacency: bfloat16 [128, 64, 5, 4096], P('rx', 'ry'), may hold values from -0.3125 to 0.3125
- out_block: int32 [32, 16, 48], P('rx', 'ry'), may hold values from 0 to 15
- out_dev: int32 [32, 16, 48, 1], P('rx', 'ry'), may hold values from 0 to 31; in each aligned block of 48 rows (0 to 47, 48 to 95, ..., all dimensions but the last counted through in order) at most 2 rows name the same one
- out_target: int32 [32, 16, 48], P('rx', 'ry'), may hold values from 0 to 15
- out_tiles: bfloat16 [32, 16, 48, 4096], P('rx', 'ry'), may hold values from -0.75 to 0.75
- w_mix: bfloat16 [3, 32, 32], replicated, may hold values from -0.625 to 0.625
- bias_mix: float32 [32], replicated, may hold values from -3 to 3
Outputs:
- layer_output: bfloat16 [128, 64, 64, 128], P('rx', 'ry')
Inputs may be any that keep to these rules, and one draw needn't show every extreme that they name: `out_dev`: among the 48 edges of one region no destination region row appears more than 2 times, and in some regions one appears exactly 2 times.
All inputs are finite; a program needn't handle non-finite values.
Results may differ from a plain program's by a relative error of at most 0.0045.
Values may be sent and summed in bfloat16 or wider, within the bound.
No kernel may reach another device: no remote copies, remote signals or barrier semaphores. Data moves between devices by JAX's collectives and lax.ppermute only.
A program may use at most 64 MiB of HBM per device.

v0:
```python
import jax
import jax.numpy as jnp
from jax import lax
from jax.sharding import PartitionSpec as P

DILATION_STEP = 2
CAP = 2


def with_halo(array, sides, width):
    for axis, dim in sides:
        size, length = (lax.axis_size(axis), array.shape[dim])
        up = [(i, (i + 1) % size) for i in range(size - 1)]
        down = [(j, i) for i, j in up]
        last = lax.slice_in_dim(array, length - width, length, axis=dim)
        leading = lax.slice_in_dim(array, 0, width, axis=dim)
        before = lax.ppermute(last, axis, up)
        after = lax.ppermute(leading, axis, down)
        array = jnp.concatenate([before, array, after], axis=dim)
    return array


def group_eye(channels):
    group_members = 128 // channels
    input_signals = jnp.arange(group_members, dtype=jnp.int32)[:, None]
    output_signals = jnp.arange(group_members, dtype=jnp.int32)[None, :]
    return (input_signals, output_signals)


def time_tables(w_filter, w_gate, channels):
    group_members = 128 // channels
    input_signals, output_signals = group_eye(channels)
    diagonal = (input_signals == output_signals).astype(jnp.float32)
    within_group = (input_signals == output_signals - DILATION_STEP).astype(jnp.float32)
    across_groups = (input_signals == output_signals - DILATION_STEP + group_members).astype(
        jnp.float32
    )
    filter_taps = w_filter.astype(jnp.float32)
    gate_taps = w_gate.astype(jnp.float32)
    current_tab = jnp.concatenate(
        [
            jnp.kron(diagonal, filter_taps[1]) + jnp.kron(within_group, filter_taps[0]),
            jnp.kron(diagonal, gate_taps[1]) + jnp.kron(within_group, gate_taps[0]),
        ],
        axis=1,
    )
    earlier_tab = jnp.concatenate(
        [jnp.kron(across_groups, filter_taps[0]), jnp.kron(across_groups, gate_taps[0])], axis=1
    )
    return (current_tab.astype(jnp.bfloat16), earlier_tab.astype(jnp.bfloat16))


def gated_units(cell_input, current_tab, earlier_tab, bias_filter, bias_gate):
    block_rows, block_cols, block_size, features = cell_input.shape
    group_members = 128 // bias_filter.shape[0]
    grouped = cell_input.reshape(block_rows * block_cols * block_size, features // 128, 128)
    shifted = jnp.concatenate([jnp.zeros_like(grouped), grouped[:, :-1]], axis=1)
    pre_both = jnp.einsum("ngk,kj->ngj", grouped, current_tab, preferred_element_type=jnp.float32)
    pre_both = pre_both + jnp.einsum(
        "ngk,kj->ngj", shifted, earlier_tab, preferred_element_type=jnp.float32
    )
    filter_bias = jnp.tile(bias_filter, group_members)
    gate_bias = jnp.tile(bias_gate, group_members)
    gated = jnp.tanh(pre_both[..., :128] + filter_bias) * jax.nn.sigmoid(
        pre_both[..., 128:] + gate_bias
    )
    return gated.astype(jnp.bfloat16).reshape(cell_input.shape)


def block_stencil(padded, tiles):
    neighbours = (
        padded[1:-1, 1:-1],
        padded[:-2, 1:-1],
        padded[2:, 1:-1],
        padded[1:-1, :-2],
        padded[1:-1, 2:],
    )
    stencil_sum = jnp.einsum(
        "ijab,ijbf->ijaf", tiles[:, :, 0], neighbours[0], preferred_element_type=jnp.float32
    )
    for offset in range(1, 5):
        stencil_sum = stencil_sum + jnp.einsum(
            "ijab,ijbf->ijaf",
            tiles[:, :, offset],
            neighbours[offset],
            preferred_element_type=jnp.float32,
        )
    return stencil_sum


def fetch_border(signal):
    return with_halo(signal, (("rx", 0), ("ry", 1)), 1)


def local_terms(signal, adjacency):
    block_size = signal.shape[2]
    tiles = adjacency.reshape(adjacency.shape[0], adjacency.shape[1], 5, block_size, block_size)
    bordered = fetch_border(signal)
    stencil_sum = block_stencil(bordered, tiles)
    return stencil_sum


def send_layout(out_block, out_dev, out_target, out_tiles, senders):
    destinations = out_dev.reshape(-1)
    sources = out_block.reshape(-1)
    targets = out_target.reshape(-1)
    edge_count = destinations.shape[0]
    edge_tiles = out_tiles.reshape(edge_count, out_tiles.shape[-1])
    owners = jnp.arange(senders, dtype=jnp.int32)
    dest_hits = (destinations[:, None] == owners[None, :]).astype(jnp.int32)
    edge_ranks = jnp.sum((jnp.cumsum(dest_hits, axis=0) - 1) * dest_hits, axis=1)
    slot_ids = jnp.arange(CAP, dtype=jnp.int32)
    select = dest_hits[:, :, None] * (edge_ranks[:, None, None] == slot_ids[None, None, :]).astype(
        jnp.int32
    )
    select = select.astype(jnp.bfloat16)
    tile_buf = jnp.einsum(
        "edc,ek->dck", select, edge_tiles, preferred_element_type=jnp.float32
    ).astype(jnp.bfloat16)
    target_buf = (
        jnp.einsum("edc,e->dc", select.astype(jnp.float32), (targets + 1).astype(jnp.float32)) - 1.0
    )
    return (select, sources, tile_buf, target_buf.astype(jnp.bfloat16))


def diffuse(signal, adjacency, layout):
    select, sources, tile_buf, target_buf = layout
    block_rows, block_cols, block_size, features = signal.shape
    nblocks = block_rows * block_cols
    near_sum = local_terms(signal, adjacency)
    flat_blocks = signal.reshape(nblocks, block_size, features)
    picked = flat_blocks[sources]
    block_buf = jnp.einsum(
        "edc,eaf->dcaf", select, picked, preferred_element_type=jnp.float32
    ).astype(jnp.bfloat16)
    recv_blocks, recv_tiles, recv_targets = (
        lax.all_to_all(block_buf, "rx", split_axis=0, concat_axis=0, tiled=True),
        lax.all_to_all(tile_buf, "rx", split_axis=0, concat_axis=0, tiled=True),
        lax.all_to_all(target_buf, "rx", split_axis=0, concat_axis=0, tiled=True),
    )
    square_tiles = recv_tiles.reshape(
        recv_tiles.shape[0], recv_tiles.shape[1], block_size, block_size
    )
    products = jnp.einsum(
        "scab,scbf->scaf", square_tiles, recv_blocks, preferred_element_type=jnp.float32
    )
    block_ids = jnp.arange(nblocks, dtype=jnp.int32).astype(jnp.float32)
    onehot = (recv_targets.astype(jnp.float32)[None, :, :] == block_ids[:, None, None]).astype(
        jnp.float32
    )
    far_sum = jnp.einsum("nsc,scaf->naf", onehot, products, precision=lax.Precision.HIGHEST)
    return near_sum + far_sum.reshape(signal.shape)


def local(
    cell_input,
    w_filter,
    w_gate,
    bias_filter,
    bias_gate,
    adjacency,
    out_block,
    out_dev,
    out_target,
    out_tiles,
    w_mix,
    bias_mix,
):
    channels = w_filter.shape[1]
    current_tab, earlier_tab = time_tables(w_filter, w_gate, channels)
    gated = gated_units(cell_input, current_tab, earlier_tab, bias_filter, bias_gate)
    layout = send_layout(out_block, out_dev, out_target, out_tiles, lax.axis_size("rx"))
    first_hop = diffuse(gated, adjacency, layout).astype(jnp.bfloat16)
    second_hop = diffuse(first_hop, adjacency, layout)
    input_signals, output_signals = group_eye(channels)
    diagonal = (input_signals == output_signals).astype(jnp.float32)
    mix_weights = w_mix.astype(jnp.float32)
    table_zero = jnp.kron(diagonal, mix_weights[0]).astype(jnp.bfloat16)
    table_one = jnp.kron(diagonal, mix_weights[1]).astype(jnp.bfloat16)
    table_two = jnp.kron(diagonal, mix_weights[2])
    block_rows, block_cols, block_size, features = cell_input.shape
    grouped_shape = (block_rows * block_cols * block_size, features // 128, 128)
    mixture = jnp.einsum(
        "ngk,kj->ngj", gated.reshape(grouped_shape), table_zero, preferred_element_type=jnp.float32
    )
    mixture = mixture + jnp.einsum(
        "ngk,kj->ngj",
        first_hop.reshape(grouped_shape),
        table_one,
        preferred_element_type=jnp.float32,
    )
    mixture = mixture + jnp.einsum(
        "ngk,kj->ngj", second_hop.reshape(grouped_shape), table_two, precision=lax.Precision.HIGHEST
    )
    mixture = mixture + jnp.tile(bias_mix, 128 // channels)
    output_sum = cell_input.astype(jnp.float32) + mixture.reshape(cell_input.shape)
    return output_sum.astype(jnp.bfloat16)


def solution(mesh):
    in_specs = (
        P("rx", "ry", None, None),
        P(),
        P(),
        P(),
        P(),
        P("rx", "ry", None, None),
        P("rx", "ry", None),
        P("rx", "ry", None, None),
        P("rx", "ry", None),
        P("rx", "ry", None, None),
        P(),
        P(),
    )
    out_specs = P("rx", "ry", None, None)
    return jax.shard_map(local, mesh=mesh, in_specs=in_specs, out_specs=out_specs, check_vma=False)
```

profile of v0, /device:TPU:354, one launch (start us, length us, event | category | flops | bytes accessed | tf_op | source)
XLA Modules:
  0.0 227.8 jit_solution(9777863136488515252)
XLA Ops:
  3.3 9.5 %all-to-all-start = ((bf16[32,1,2]{2,1,0:T(2,128)(2,1)}), bf16[32,1,2]{2,1,0:T(2,128)(2,1)S(1)}, u32[]{:S(2)}, u32[]{:S(2)}) async-start(bf16[32,1,2]{2,1,0:T(2,128)(2,1)} %copy.92), calls=%async_computation | async-start | bytes 32768 | tf_op jit(solution)/shard_map/all_to_all | solution.py:139
  15.4 1.3 copy.94
  16.7 4.7 %all-to-all-done = bf16[32,1,2]{2,1,0:T(2,128)(2,1)S(1)} async-done(((bf16[32,1,2]{2,1,0:T(2,128)(2,1)}), bf16[32,1,2]{2,1,0:T(2,128)(2,1)S(1)}, u32[]{:S(2)}, u32[]{:S(2)}) %all-to-all-start) | async-done | bytes 160 | tf_op jit(solution)/shard_map/all_to_all | solution.py:139
  21.4 7.9 %all-to-all-start.1 = ((bf16[32,2,4096]{2,1,0:T(2,128)(2,1)}), bf16[32,2,4096]{2,1,0:T(2,128)(2,1)S(1)}, u32[]{:S(2)}, u32[]{:S(2)}) async-start(bf16[32,2,4096]{2,1,0:T(2,128)(2,1)} %copy.94), calls=%async_computation.1 | async-start | bytes 1048576 | tf_op jit(solution)/shard_map/all_to_all | solution.py:138
  29.4 1.2 add_convert_fusion.1
  34.1 1.4 copy.97
  35.6 18.2 %all-to-all-done.1 = bf16[32,2,4096]{2,1,0:T(2,128)(2,1)S(1)} async-done(((bf16[32,2,4096]{2,1,0:T(2,128)(2,1)}), bf16[32,2,4096]{2,1,0:T(2,128)(2,1)S(1)}, u32[]{:S(2)}, u32[]{:S(2)}) %all-to-all-start.1) | async-done | bytes 524320 | tf_op jit(solution)/shard_map/all_to_all | solution.py:138
  53.8 10.5 %all-to-all-start.2 = ((bf16[32,2,64,128]{3,2,1,0:T(8,128)(2,1)}), bf16[32,2,64,128]{3,2,1,0:T(8,128)(2,1)}, u32[]{:S(2)}, u32[]{:S(2)}) async-start(bf16[32,2,64,128]{3,2,1,0:T(8,128)(2,1)} %copy.97), calls=%async_computation.2 | async-start | bytes 2097152 | tf_op jit(solution)/shard_map/all_to_all | solution.py:137
  64.5 2.5 %collective-permute-start.1 = (bf16[1,4,64,128]{3,2,1,0:T(8,128)(2,1)S(1)}, bf16[1,4,64,128]{3,2,1,0:T(8,128)(2,1)S(1)}, u32[]{:S(2)}, u32[]{:S(2)}) collective-permute-start(bf16[1,4,64,128]{3,2,1,0:T(8,128)(2,1)S(1)} %bitcast.140), channel_id=1, source_target_pairs={{16,0},{32,16},{48,32},{64,48},{80,64},{96,80},{112,96},{128,112},... | collective-permute-start | bytes 196616 | tf_op jit(solution)/shard_map/ppermute | solution.py:18
  67.1 4.6 %collective-permute-start = (bf16[1,4,64,128]{3,2,1,0:T(8,128)(2,1)S(1)}, bf16[1,4,64,128]{3,2,1,0:T(8,128)(2,1)S(1)}, u32[]{:S(2)}, u32[]{:S(2)}) collective-permute-start(bf16[1,4,64,128]{3,2,1,0:T(8,128)(2,1)S(1)} %bitcast.141), channel_id=1, source_target_pairs={{0,16},{16,32},{32,48},{48,64},{64,80},{80,96},{96,112},{112,128},... | collective-permute-start | bytes 196616 | tf_op jit(solution)/shard_map/ppermute | solution.py:17
  73.4 41.9 %collective-permute-done.1 = bf16[1,4,64,128]{3,2,1,0:T(8,128)(2,1)S(1)} collective-permute-done((bf16[1,4,64,128]{3,2,1,0:T(8,128)(2,1)S(1)}, bf16[1,4,64,128]{3,2,1,0:T(8,128)(2,1)S(1)}, u32[]{:S(2)}, u32[]{:S(2)}) %collective-permute-start.1) | collective-permute-done | bytes 65568 | tf_op jit(solution)/shard_map/ppermute | solution.py:18
  115.3 7.2 %collective-permute-start.3 = (bf16[6,1,64,128]{3,2,1,0:T(8,128)(2,1)S(1)}, bf16[6,1,64,128]{3,2,1,0:T(8,128)(2,1)S(1)}, u32[]{:S(2)}, u32[]{:S(2)}) collective-permute-start(bf16[6,1,64,128]{3,2,1,0:T(8,128)(2,1)S(1)} %get-tuple-element.8), channel_id=1, source_target_pairs={{1,0},{2,1},{3,2},{4,3},{5,4},{6,5},{7,6},{8,7},{9,8},{10,9},{11,1... | collective-permute-start | bytes 294920 | tf_op jit(solution)/shard_map/ppermute | solution.py:18
  122.5 2.1 collective-permute-start.2
  126.7 12.6 %collective-permute-done.2 = bf16[6,1,64,128]{3,2,1,0:T(8,128)(2,1)S(1)} collective-permute-done((bf16[6,1,64,128]{3,2,1,0:T(8,128)(2,1)S(1)}, bf16[6,1,64,128]{3,2,1,0:T(8,128)(2,1)S(1)}, u32[]{:S(2)}, u32[]{:S(2)}) %collective-permute-start.2) | collective-permute-done | bytes 98336 | tf_op jit(solution)/shard_map/ppermute | solution.py:17
  140.3 2.3 %reshape.314 = bf16[32,2,64,64]{3,2,1,0:T(8,128)(2,1)S(1)} reshape(bf16[32,2,4096]{2,1,0:T(2,128)(2,1)} %copy-done.1) | data formatting | bytes 1048576 | tf_op jit(solution)/shard_map/reshape | solution.py:141
  142.6 1.6 fusion.102
  144.3 2.0 fusion.6
  146.7 1.7 gather_fusion.1
  148.4 1.9 convolution_convert_fusion.1
  150.3 1.4 copy.101
  151.7 8.1 %all-to-all-start.3 = ((bf16[32,2,64,128]{3,2,1,0:T(8,128)(2,1)}), bf16[32,2,64,128]{3,2,1,0:T(8,128)(2,1)}, u32[]{:S(2)}, u32[]{:S(2)}) async-start(bf16[32,2,64,128]{3,2,1,0:T(8,128)(2,1)} %copy.101), calls=%async_computation.3 | async-start | bytes 2097152 | tf_op jit(solution)/shard_map/all_to_all | solution.py:137
  159.9 1.7 convert_element_type.148
  161.5 1.7 convert_element_type.162
  165.1 2.5 %collective-permute-start.5 = (bf16[1,4,64,128]{3,2,1,0:T(8,128)(2,1)S(1)}, bf16[1,4,64,128]{3,2,1,0:T(8,128)(2,1)S(1)}, u32[]{:S(2)}, u32[]{:S(2)}) collective-permute-start(bf16[1,4,64,128]{3,2,1,0:T(8,128)(2,1)S(1)} %get-tuple-element.10), channel_id=1, source_target_pairs={{16,0},{32,16},{48,32},{64,48},{80,64},{96,80},{112,96},{128,112},... | collective-permute-start | bytes 196616 | tf_op jit(solution)/shard_map/ppermute | solution.py:18
  167.6 4.6 %collective-permute-start.4 = (bf16[1,4,64,128]{3,2,1,0:T(8,128)(2,1)S(1)}, bf16[1,4,64,128]{3,2,1,0:T(8,128)(2,1)S(1)}, u32[]{:S(2)}, u32[]{:S(2)}) collective-permute-start(bf16[1,4,64,128]{3,2,1,0:T(8,128)(2,1)S(1)} %get-tuple-element.9), channel_id=1, source_target_pairs={{0,16},{16,32},{32,48},{48,64},{64,80},{80,96},{96,112},{112,128},... | collective-permute-start | bytes 196616 | tf_op jit(solution)/shard_map/ppermute | solution.py:17
  172.2 1.8 convolution_add_fusion
  174.1 24.0 %collective-permute-done.5 = bf16[1,4,64,128]{3,2,1,0:T(8,128)(2,1)S(1)} collective-permute-done((bf16[1,4,64,128]{3,2,1,0:T(8,128)(2,1)S(1)}, bf16[1,4,64,128]{3,2,1,0:T(8,128)(2,1)S(1)}, u32[]{:S(2)}, u32[]{:S(2)}) %collective-permute-start.5) | collective-permute-done | bytes 65568 | tf_op jit(solution)/shard_map/ppermute | solution.py:18
  198.2 5.6 %collective-permute-start.7 = (bf16[6,1,64,128]{3,2,1,0:T(8,128)(2,1)S(1)}, bf16[6,1,64,128]{3,2,1,0:T(8,128)(2,1)S(1)}, u32[]{:S(2)}, u32[]{:S(2)}) collective-permute-start(bf16[6,1,64,128]{3,2,1,0:T(8,128)(2,1)S(1)} %get-tuple-element.6), channel_id=1, source_target_pairs={{1,0},{2,1},{3,2},{4,3},{5,4},{6,5},{7,6},{8,7},{9,8},{10,9},{11,1... | collective-permute-start | bytes 294920 | tf_op jit(solution)/shard_map/ppermute | solution.py:18
  203.7 1.9 collective-permute-start.6
  206.9 13.5 %collective-permute-done.6 = bf16[6,1,64,128]{3,2,1,0:T(8,128)(2,1)S(1)} collective-permute-done((bf16[6,1,64,128]{3,2,1,0:T(8,128)(2,1)S(1)}, bf16[6,1,64,128]{3,2,1,0:T(8,128)(2,1)S(1)}, u32[]{:S(2)}, u32[]{:S(2)}) %collective-permute-start.6) | collective-permute-done | bytes 98336 | tf_op jit(solution)/shard_map/ppermute | solution.py:17
  221.5 1.6 fusion.103
  223.2 2.0 fusion.9
  (125 shorter events, 21.6 us)
Async XLA Ops:
  0.0 12.9 %copy-start = (bf16[1,1,48,4096]{3,2,1,0:T(8,128)(2,1)S(1)}, bf16[1,1,48,4096]{3,2,1,0:T(8,128)(2,1)}, u32[]{:S(2)}) copy-start(bf16[1,1,48,4096]{3,2,1,0:T(8,128)(2,1)} %param.21) | copy-start | bytes 1179652
  1.8 31.6 %copy-start.17 = (s32[48,2]{0,1:T(2,128)}, s32[48,2]{0,1:T(2,128)S(1)}, u32[]{:S(2)}) copy-start(s32[48,2]{0,1:T(2,128)S(1)} %compare_convert_fusion) | copy-start | bytes 1156
  3.3 18.1 %all-to-all-start = ((bf16[32,1,2]{2,1,0:T(2,128)(2,1)}), bf16[32,1,2]{2,1,0:T(2,128)(2,1)S(1)}, u32[]{:S(2)}, u32[]{:S(2)}) async-start(bf16[32,1,2]{2,1,0:T(2,128)(2,1)} %copy.92), calls=%async_computation | async-start | bytes 32768 | tf_op jit(solution)/shard_map/all_to_all | solution.py:139
  16.7 14.4 %copy-start.24 = (f32[32]{0:T(128)S(1)}, f32[32]{0:T(128)}, u32[]{:S(2)}) copy-start(f32[32]{0:T(128)} %param.16) | copy-start | bytes 388
  16.7 14.5 %copy-start.25 = (f32[32]{0:T(128)S(1)}, f32[32]{0:T(128)}, u32[]{:S(2)}) copy-start(f32[32]{0:T(128)} %param.15) | copy-start | bytes 388
  21.4 32.4 %all-to-all-start.1 = ((bf16[32,2,4096]{2,1,0:T(2,128)(2,1)}), bf16[32,2,4096]{2,1,0:T(2,128)(2,1)S(1)}, u32[]{:S(2)}, u32[]{:S(2)}) async-start(bf16[32,2,4096]{2,1,0:T(2,128)(2,1)} %copy.94), calls=%async_computation.1 | async-start | bytes 1048576 | tf_op jit(solution)/shard_map/all_to_all | solution.py:138
  29.4 2.2 copy-start.4
  35.6 36.1 %copy-start.7 = (bf16[4,4,5,4096]{3,1,2,0:T(4,128)(2,1)S(1)}, bf16[4,4,5,4096]{3,1,2,0:T(4,128)(2,1)}, u32[]{:S(2)}) copy-start(bf16[4,4,5,4096]{3,1,2,0:T(4,128)(2,1)} %param.17) | copy-start | bytes 1966084
  53.8 13.3 %copy-start.1 = (bf16[32,2,4096]{2,1,0:T(2,128)(2,1)}, bf16[32,2,4096]{2,1,0:T(2,128)(2,1)S(1)}, u32[]{:S(2)}) copy-start(bf16[32,2,4096]{2,1,0:T(2,128)(2,1)S(1)} %all-to-all-done.1) | copy-start | bytes 1572868
  53.8 88.8 %all-to-all-start.2 = ((bf16[32,2,64,128]{3,2,1,0:T(8,128)(2,1)}), bf16[32,2,64,128]{3,2,1,0:T(8,128)(2,1)}, u32[]{:S(2)}, u32[]{:S(2)}) async-start(bf16[32,2,64,128]{3,2,1,0:T(8,128)(2,1)} %copy.97), calls=%async_computation.2 | async-start | bytes 2097152 | tf_op jit(solution)/shard_map/all_to_all | solution.py:137
  64.5 50.8 %collective-permute-start.1 = (bf16[1,4,64,128]{3,2,1,0:T(8,128)(2,1)S(1)}, bf16[1,4,64,128]{3,2,1,0:T(8,128)(2,1)S(1)}, u32[]{:S(2)}, u32[]{:S(2)}) collective-permute-start(bf16[1,4,64,128]{3,2,1,0:T(8,128)(2,1)S(1)} %bitcast.140), channel_id=1, source_target_pairs={{16,0},{32,16},{48,32},{64,48},{80,64},{96,80},{112,96},{128,112},... | collective-permute-start | bytes 196616 | tf_op jit(solution)/shard_map/ppermute | solution.py:18
  67.1 48.2 %collective-permute-start = (bf16[1,4,64,128]{3,2,1,0:T(8,128)(2,1)S(1)}, bf16[1,4,64,128]{3,2,1,0:T(8,128)(2,1)S(1)}, u32[]{:S(2)}, u32[]{:S(2)}) collective-permute-start(bf16[1,4,64,128]{3,2,1,0:T(8,128)(2,1)S(1)} %bitcast.141), channel_id=1, source_target_pairs={{0,16},{16,32},{32,48},{48,64},{64,80},{80,96},{96,112},{112,128},... | collective-permute-start | bytes 196616 | tf_op jit(solution)/shard_map/ppermute | solution.py:17
  73.0 71.2 %copy-start.22 = (f32[16]{0:T(128)}, f32[16]{0:T(128)S(1)}, u32[]{:S(2)}) copy-start(f32[16]{0:T(128)S(1)} %iota_convert_fusion) | copy-start | bytes 196
  73.4 70.9 %copy-start.20 = (f32[32,2]{0,1:T(2,128)}, f32[32,2]{0,1:T(2,128)S(1)}, u32[]{:S(2)}) copy-start(f32[32,2]{0,1:T(2,128)S(1)} %bitcast_convert_fusion) | copy-start | bytes 772
  115.2 24.0 %copy-start.13 = (bf16[1,4,64,128]{3,2,1,0:T(8,128)(2,1)}, bf16[1,4,64,128]{3,2,1,0:T(8,128)(2,1)S(1)}, u32[]{:S(2)}) copy-start(bf16[1,4,64,128]{3,2,1,0:T(8,128)(2,1)S(1)} %collective-permute-done.1) | copy-start | bytes 196612
  115.3 10.4 %collective-permute-start.3 = (bf16[6,1,64,128]{3,2,1,0:T(8,128)(2,1)S(1)}, bf16[6,1,64,128]{3,2,1,0:T(8,128)(2,1)S(1)}, u32[]{:S(2)}, u32[]{:S(2)}) collective-permute-start(bf16[6,1,64,128]{3,2,1,0:T(8,128)(2,1)S(1)} %get-tuple-element.8), channel_id=1, source_target_pairs={{1,0},{2,1},{3,2},{4,3},{5,4},{6,5},{7,6},{8,7},{9,8},{10,9},{11,1... | collective-permute-start | bytes 294920 | tf_op jit(solution)/shard_map/ppermute | solution.py:18
  122.5 16.8 %collective-permute-start.2 = (bf16[6,1,64,128]{3,2,1,0:T(8,128)(2,1)S(1)}, bf16[6,1,64,128]{3,2,1,0:T(8,128)(2,1)S(1)}, u32[]{:S(2)}, u32[]{:S(2)}) collective-permute-start(bf16[6,1,64,128]{3,2,1,0:T(8,128)(2,1)S(1)} %get-tuple-element.7), channel_id=1, source_target_pairs={{0,1},{1,2},{2,3},{3,4},{4,5},{5,6},{6,7},{7,8},{8,9},{9,10},{10,1... | collective-permute-start | bytes 294920 | tf_op jit(solution)/shard_map/ppermute | solution.py:17
  144.2 2.2 copy-start.2
  144.3 2.2 copy-start.10
  144.3 2.2 copy-start.11
  144.3 2.2 copy-start.14
  151.7 11.5 %copy-start.6 = (f32[4,32,4,32]{3,2,1,0:T(4,128)S(1)}, f32[4,32,4,32]{3,2,1,0:T(4,128)}, u32[]{:S(2)}) copy-start(f32[4,32,4,32]{3,2,1,0:T(4,128)} %get-tuple-element.26) | copy-start | bytes 196612
  151.7 12.3 %copy-start.26 = (f32[32]{0:T(128)S(1)}, f32[32]{0:T(128)}, u32[]{:S(2)}) copy-start(f32[32]{0:T(128)} %param.23) | copy-start | bytes 388
  151.7 69.8 %all-to-all-start.3 = ((bf16[32,2,64,128]{3,2,1,0:T(8,128)(2,1)}), bf16[32,2,64,128]{3,2,1,0:T(8,128)(2,1)}, u32[]{:S(2)}, u32[]{:S(2)}) async-start(bf16[32,2,64,128]{3,2,1,0:T(8,128)(2,1)} %copy.101), calls=%async_computation.3 | async-start | bytes 2097152 | tf_op jit(solution)/shard_map/all_to_all | solution.py:137
  165.1 33.0 %collective-permute-start.5 = (bf16[1,4,64,128]{3,2,1,0:T(8,128)(2,1)S(1)}, bf16[1,4,64,128]{3,2,1,0:T(8,128)(2,1)S(1)}, u32[]{:S(2)}, u32[]{:S(2)}) collective-permute-start(bf16[1,4,64,128]{3,2,1,0:T(8,128)(2,1)S(1)} %get-tuple-element.10), channel_id=1, source_target_pairs={{16,0},{32,16},{48,32},{64,48},{80,64},{96,80},{112,96},{128,112},... | collective-permute-start | bytes 196616 | tf_op jit(solution)/shard_map/ppermute | solution.py:18
  167.6 30.6 %collective-permute-start.4 = (bf16[1,4,64,128]{3,2,1,0:T(8,128)(2,1)S(1)}, bf16[1,4,64,128]{3,2,1,0:T(8,128)(2,1)S(1)}, u32[]{:S(2)}, u32[]{:S(2)}) collective-permute-start(bf16[1,4,64,128]{3,2,1,0:T(8,128)(2,1)S(1)} %get-tuple-element.9), channel_id=1, source_target_pairs={{0,16},{16,32},{32,48},{48,64},{64,80},{80,96},{96,112},{112,128},... | collective-permute-start | bytes 196616 | tf_op jit(solution)/shard_map/ppermute | solution.py:17
  198.1 22.4 %copy-start.15 = (bf16[1,4,64,128]{3,2,1,0:T(8,128)(2,1)}, bf16[1,4,64,128]{3,2,1,0:T(8,128)(2,1)S(1)}, u32[]{:S(2)}) copy-start(bf16[1,4,64,128]{3,2,1,0:T(8,128)(2,1)S(1)} %collective-permute-done.5) | copy-start | bytes 196612
  198.2 7.8 %collective-permute-start.7 = (bf16[6,1,64,128]{3,2,1,0:T(8,128)(2,1)S(1)}, bf16[6,1,64,128]{3,2,1,0:T(8,128)(2,1)S(1)}, u32[]{:S(2)}, u32[]{:S(2)}) collective-permute-start(bf16[6,1,64,128]{3,2,1,0:T(8,128)(2,1)S(1)} %get-tuple-element.6), channel_id=1, source_target_pairs={{1,0},{2,1},{3,2},{4,3},{5,4},{6,5},{7,6},{8,7},{9,8},{10,9},{11,1... | collective-permute-start | bytes 294920 | tf_op jit(solution)/shard_map/ppermute | solution.py:18
  203.7 16.8 %collective-permute-start.6 = (bf16[6,1,64,128]{3,2,1,0:T(8,128)(2,1)S(1)}, bf16[6,1,64,128]{3,2,1,0:T(8,128)(2,1)S(1)}, u32[]{:S(2)}, u32[]{:S(2)}) collective-permute-start(bf16[6,1,64,128]{3,2,1,0:T(8,128)(2,1)S(1)} %get-tuple-element.5), channel_id=1, source_target_pairs={{0,1},{1,2},{2,3},{3,4},{4,5},{5,6},{6,7},{7,8},{8,9},{9,10},{10,1... | collective-permute-start | bytes 294920 | tf_op jit(solution)/shard_map/ppermute | solution.py:17
  223.2 2.2 copy-start.8
  223.2 2.2 copy-start.9
  223.2 2.2 copy-start.16
  (8 other events, 10.6 us)
where the time goes:
time: 229 us; the launch traced here: 228 us
  waiting for transfers between devices  115 us (50%)
  starting transfers between devices  67 us (29%)
  matrix products  21.1 us (9%)
  local copies, waits for them, and re-layouts  17.7 us (8%)
  other arithmetic  6.27 us (3%)
    ppermute x4, waiting for transfers between devices, with_halo(): after = lax.ppermute(leading, axis, down)  65.9 us
    ppermute x4, waiting for transfers between devices, with_halo(): before = lax.ppermute(last, axis, up)  26.2 us
    all_to_all x2, starting transfers between devices, diffuse(): lax.all_to_all(block_buf, 'rx', split_axis=0, concat_axis=0, tiled=True)  18.7 us
    all_to_all x1, waiting for transfers between devices, diffuse(): lax.all_to_all(tile_buf, 'rx', split_axis=0, concat_axis=0, tiled=True)  18.2 us
    ppermute x4, starting transfers between devices, with_halo(): after = lax.ppermute(leading, axis, down)  17.7 us
    ppermute x4, starting transfers between devices, with_halo(): before = lax.ppermute(last, axis, up)  13.2 us
    all_to_all x1, starting transfers between devices, diffuse(): lax.all_to_all(target_buf, 'rx', split_axis=0, concat_axis=0, tiled=True)  9.51 us
    all_to_all x1, starting transfers between devices, diffuse(): lax.all_to_all(tile_buf, 'rx', split_axis=0, concat_axis=0, tiled=True)  7.91 us
  transfers between devices with their start and end apart: 12, of which 6 were waited for; matrix products, arithmetic and copies ran while one was open for 12% of the time, Pallas kernels for 0%

commit v1 on v0

v1 whole, which is shorter than its diff:
```python
import jax
import jax.numpy as jnp
from jax import lax
from jax.sharding import PartitionSpec as P

DILATION_STEP = 2
CAP = 2


def group_eye(channels):
    group_members = 128 // channels
    input_signals = jnp.arange(group_members, dtype=jnp.int32)[:, None]
    output_signals = jnp.arange(group_members, dtype=jnp.int32)[None, :]
    return (input_signals, output_signals)


def time_tables(w_filter, w_gate, channels):
    group_members = 128 // channels
    input_signals, output_signals = group_eye(channels)
    diagonal = (input_signals == output_signals).astype(jnp.float32)
    within_group = (input_signals == output_signals - DILATION_STEP).astype(jnp.float32)
    across_groups = (input_signals == output_signals - DILATION_STEP + group_members).astype(
        jnp.float32
    )
    filter_taps = w_filter.astype(jnp.float32)
    gate_taps = w_gate.astype(jnp.float32)
    current_tab = jnp.concatenate(
        [
            jnp.kron(diagonal, filter_taps[1]) + jnp.kron(within_group, filter_taps[0]),
            jnp.kron(diagonal, gate_taps[1]) + jnp.kron(within_group, gate_taps[0]),
        ],
        axis=1,
    )
    earlier_tab = jnp.concatenate(
        [jnp.kron(across_groups, filter_taps[0]), jnp.kron(across_groups, gate_taps[0])], axis=1
    )
    return (current_tab.astype(jnp.bfloat16), earlier_tab.astype(jnp.bfloat16))


def gated_units(cell_input, current_tab, earlier_tab, bias_filter, bias_gate):
    block_rows, block_cols, block_size, features = cell_input.shape
    group_members = 128 // bias_filter.shape[0]
    grouped = cell_input.reshape(block_rows * block_cols * block_size, features // 128, 128)
    shifted = jnp.concatenate([jnp.zeros_like(grouped), grouped[:, :-1]], axis=1)
    pre_both = jnp.einsum("ngk,kj->ngj", grouped, current_tab, preferred_element_type=jnp.float32)
    pre_both = pre_both + jnp.einsum(
        "ngk,kj->ngj", shifted, earlier_tab, preferred_element_type=jnp.float32
    )
    filter_bias = jnp.tile(bias_filter, group_members)
    gate_bias = jnp.tile(bias_gate, group_members)
    gated = jnp.tanh(pre_both[..., :128] + filter_bias) * jax.nn.sigmoid(
        pre_both[..., 128:] + gate_bias
    )
    return gated.astype(jnp.bfloat16).reshape(cell_input.shape)


def shift_pairs(size, step):
    if step > 0:
        return [(i, i + 1) for i in range(size - 1)]
    return [(i + 1, i) for i in range(size - 1)]


def fetch_halo(signal):
    n_rx, n_ry = lax.axis_size("rx"), lax.axis_size("ry")
    above = lax.ppermute(signal[-1:], "rx", shift_pairs(n_rx, 1))
    below = lax.ppermute(signal[:1], "rx", shift_pairs(n_rx, -1))
    left = lax.ppermute(signal[:, -1:], "ry", shift_pairs(n_ry, 1))
    right = lax.ppermute(signal[:, :1], "ry", shift_pairs(n_ry, -1))
    return above, below, left, right


def local_terms(signal, tiles, halo):
    above, below, left, right = halo
    neighbours = (
        signal,
        jnp.concatenate([above, signal[:-1]], axis=0),
        jnp.concatenate([signal[1:], below], axis=0),
        jnp.concatenate([left, signal[:, :-1]], axis=1),
        jnp.concatenate([signal[:, 1:], right], axis=1),
    )
    stencil_sum = jnp.einsum(
        "ijab,ijbf->ijaf", tiles[:, :, 0], neighbours[0], preferred_element_type=jnp.float32
    )
    for offset in range(1, 5):
        stencil_sum = stencil_sum + jnp.einsum(
            "ijab,ijbf->ijaf",
            tiles[:, :, offset],
            neighbours[offset],
            preferred_element_type=jnp.float32,
        )
    return stencil_sum


def edge_select(out_dev, senders):
    destinations = out_dev.reshape(-1)
    owners = jnp.arange(senders, dtype=jnp.int32)
    dest_hits = (destinations[:, None] == owners[None, :]).astype(jnp.int32)
    edge_ranks = jnp.sum((jnp.cumsum(dest_hits, axis=0) - 1) * dest_hits, axis=1)
    slot_ids = jnp.arange(CAP, dtype=jnp.int32)
    select = dest_hits[:, :, None] * (edge_ranks[:, None, None] == slot_ids[None, None, :]).astype(
        jnp.int32
    )
    return select.reshape(select.shape[0], -1).astype(jnp.bfloat16)


def far_terms(recv_blocks, recv_tiles, recv_targets, nblocks):
    products = jnp.einsum(
        "sab,sbf->saf", recv_tiles, recv_blocks, preferred_element_type=jnp.float32
    )
    block_ids = jnp.arange(nblocks, dtype=jnp.float32)
    onehot = (recv_targets[None, :] == block_ids[:, None]).astype(jnp.float32)
    return jnp.einsum("ns,saf->naf", onehot, products, precision=lax.Precision.HIGHEST)


def local(
    cell_input,
    w_filter,
    w_gate,
    bias_filter,
    bias_gate,
    adjacency,
    out_block,
    out_dev,
    out_target,
    out_tiles,
    w_mix,
    bias_mix,
):
    channels = w_filter.shape[1]
    block_rows, block_cols, block_size, features = cell_input.shape
    nblocks = block_rows * block_cols
    n_rx = lax.axis_size("rx")
    tiles = adjacency.reshape(block_rows, block_cols, 5, block_size, block_size)
    current_tab, earlier_tab = time_tables(w_filter, w_gate, channels)
    gated = gated_units(cell_input, current_tab, earlier_tab, bias_filter, bias_gate)

    select = edge_select(out_dev, n_rx)
    sources = out_block.reshape(-1)
    edge_count = sources.shape[0]
    block_len = block_size * features
    tile_len = out_tiles.shape[-1]

    flat_gated = gated.reshape(nblocks, block_len)
    target_col = jnp.zeros((edge_count, 128), jnp.bfloat16).at[:, 0].set(
        (out_target.reshape(-1) + 1).astype(jnp.bfloat16)
    )
    payload = jnp.concatenate(
        [flat_gated[sources], out_tiles.reshape(edge_count, tile_len), target_col], axis=1
    )
    send_one = jnp.einsum(
        "es,ek->sk", select, payload, preferred_element_type=jnp.float32
    ).astype(jnp.bfloat16)
    send_one = send_one.reshape(n_rx, CAP, -1)
    halo_one = fetch_halo(gated)
    recv_one = lax.all_to_all(send_one, "rx", split_axis=0, concat_axis=0, tiled=True)
    recv_one = recv_one.reshape(n_rx * CAP, -1)
    recv_blocks = recv_one[:, :block_len].reshape(-1, block_size, features)
    recv_tiles = recv_one[:, block_len : block_len + tile_len].reshape(-1, block_size, block_size)
    recv_targets = recv_one[:, block_len + tile_len].astype(jnp.float32) - 1.0

    near_one = local_terms(gated, tiles, halo_one)
    far_one = far_terms(recv_blocks, recv_tiles, recv_targets, nblocks)
    first_hop = (near_one + far_one.reshape(gated.shape)).astype(jnp.bfloat16)

    flat_first = first_hop.reshape(nblocks, block_len)
    send_two = jnp.einsum(
        "es,ek->sk", select, flat_first[sources], preferred_element_type=jnp.float32
    ).astype(jnp.bfloat16)
    send_two = send_two.reshape(n_rx, CAP, block_size, features)
    halo_two = fetch_halo(first_hop)
    recv_two = lax.all_to_all(send_two, "rx", split_axis=0, concat_axis=0, tiled=True)
    recv_two = recv_two.reshape(n_rx * CAP, block_size, features)
    near_two = local_terms(first_hop, tiles, halo_two)
    far_two = far_terms(recv_two, recv_tiles, recv_targets, nblocks)
    second_hop = near_two + far_two.reshape(gated.shape)

    input_signals, output_signals = group_eye(channels)
    diagonal = (input_signals == output_signals).astype(jnp.float32)
    mix_weights = w_mix.astype(jnp.float32)
    table_zero = jnp.kron(diagonal, mix_weights[0]).astype(jnp.bfloat16)
    table_one = jnp.kron(diagonal, mix_weights[1]).astype(jnp.bfloat16)
    table_two = jnp.kron(diagonal, mix_weights[2])
    grouped_shape = (nblocks * block_size, features // 128, 128)
    mixture = jnp.einsum(
        "ngk,kj->ngj", gated.reshape(grouped_shape), table_zero, preferred_element_type=jnp.float32
    )
    mixture = mixture + jnp.einsum(
        "ngk,kj->ngj",
        first_hop.reshape(grouped_shape),
        table_one,
        preferred_element_type=jnp.float32,
    )
    mixture = mixture + jnp.einsum(
        "ngk,kj->ngj", second_hop.reshape(grouped_shape), table_two, precision=lax.Precision.HIGHEST
    )
    mixture = mixture + jnp.tile(bias_mix, 128 // channels)
    output_sum = cell_input.astype(jnp.float32) + mixture.reshape(cell_input.shape)
    return output_sum.astype(jnp.bfloat16)


def solution(mesh):
    in_specs = (
        P("rx", "ry", None, None),
        P(),
        P(),
        P(),
        P(),
        P("rx", "ry", None, None),
        P("rx", "ry", None),
        P("rx", "ry", None, None),
        P("rx", "ry", None),
        P("rx", "ry", None, None),
        P(),
        P(),
    )
    out_specs = P("rx", "ry", None, None)
    return jax.shard_map(local, mesh=mesh, in_specs=in_specs, out_specs=out_specs, check_vma=False)
```

time: 229 us -> 194 us (0.85)
  the two profiles are of different devices: /device:TPU:354 before, /device:TPU:57 now
where the time goes in v1:
time: 194 us; the launch traced here: 193 us
  starting transfers between devices  72.7 us (37%)
  waiting for transfers between devices  70.2 us (36%)
  local copies, waits for them, and re-layouts  22.3 us (11%)
  matrix products  20.2 us (10%)
  other arithmetic  6.86 us (4%)
    ppermute x2, waiting for transfers between devices, fetch_halo(): above = lax.ppermute(signal[-1:], 'rx', shift_pairs(n_rx, 1))  29.8 us
    ppermute x2, starting transfers between devices, fetch_halo(): left = lax.ppermute(signal[:, -1:], 'ry', shift_pairs(n_ry, 1))  27.7 us
    all_to_all x1, waiting for transfers between devices, local(): lax.all_to_all(send_one, 'rx', split_axis=0, concat_axis=0, tiled=True)  20.8 us
    all_to_all x1, waiting for transfers between devices, local(): lax.all_to_all(send_two, 'rx', split_axis=0, concat_axis=0, tiled=True)  19.5 us
    all_to_all x1, starting transfers between devices, local(): lax.all_to_all(send_one, 'rx', split_axis=0, concat_axis=0, tiled=True)  14.9 us
    all_to_all x1, starting transfers between devices, local(): lax.all_to_all(send_two, 'rx', split_axis=0, concat_axis=0, tiled=True)  13.6 us
    dot_general x8, matrix products, local_terms(): jnp.einsum('ijab,ijbf->ijaf', tiles[:, :, offset], neighbours[offset], pr...  8.28 us
    ppermute x2, starting transfers between devices, fetch_halo(): above = lax.ppermute(signal[-1:], 'rx', shift_pairs(n_rx, 1))  6.17 us
  transfers between devices with their start and end apart: 10, of which 4 were waited for; matrix products, arithmetic and copies ran while one was open for 16% of the time, Pallas kernels for 0%

profile of v1, /device:TPU:57, one launch (start us, length us, event | category | flops | bytes accessed | tf_op | source)
XLA Modules:
  0.0 193.0 jit_solution(10736032318690984412)
XLA Ops:
  2.9 1.2 add_convert_fusion.1
  7.4 1.0 gather_fusion
  8.5 1.6 convolution_convert_fusion
  10.0 1.5 reshape.374
  11.6 14.9 %all-to-all-start = ((bf16[32,2,12416]{2,1,0:T(2,128)(2,1)}), bf16[32,2,12416]{2,1,0:T(2,128)(2,1)}, u32[]{:S(2)}, u32[]{:S(2)}) async-start(bf16[32,2,12416]{2,1,0:T(2,128)(2,1)} %reshape.374), calls=%async_computation | async-start | bytes 3178496 | tf_op jit(solution)/shard_map/all_to_all | solution.py:155
  27.1 3.1 %collective-permute-start.3 = (bf16[4,1,64,128]{3,2,1,0:T(8,128)(2,1)}, bf16[4,1,64,128]{3,2,1,0:T(8,128)(2,1)}, u32[]{:S(2)}, u32[]{:S(2)}) collective-permute-start(bf16[4,1,64,128]{3,2,1,0:T(8,128)(2,1)} %get-tuple-element.30), channel_id=1, source_target_pairs={{1,0},{2,1},{3,2},{4,3},{5,4},{6,5},{7,6},{8,7},{9,8},{10,9},{11,1... | collective-permute-start | bytes 196616 | tf_op jit(solution)/shard_map/ppermute | solution.py:68
  30.2 13.2 %collective-permute-start.2 = (bf16[4,1,64,128]{3,2,1,0:T(8,128)(2,1)}, bf16[4,1,64,128]{3,2,1,0:T(8,128)(2,1)}, u32[]{:S(2)}, u32[]{:S(2)}) collective-permute-start(bf16[4,1,64,128]{3,2,1,0:T(8,128)(2,1)} %get-tuple-element.29), channel_id=1, source_target_pairs={{0,1},{1,2},{2,3},{3,4},{4,5},{5,6},{6,7},{7,8},{8,9},{9,10},{10,1... | collective-permute-start | bytes 196616 | tf_op jit(solution)/shard_map/ppermute | solution.py:67
  44.2 3.1 %collective-permute-start = (bf16[1,4,64,128]{3,2,1,0:T(8,128)(2,1)}, bf16[1,4,64,128]{3,2,1,0:T(8,128)(2,1)}, u32[]{:S(2)}, u32[]{:S(2)}) collective-permute-start(bf16[1,4,64,128]{3,2,1,0:T(8,128)(2,1)} %bitcast.11), channel_id=1, source_target_pairs={{0,16},{16,32},{32,48},{48,64},{64,80},{80,96},{96,112},{112,128},... | collective-permute-start | bytes 196616 | tf_op jit(solution)/shard_map/ppermute | solution.py:65
  48.1 3.0 %collective-permute-start.1 = (bf16[1,4,64,128]{3,2,1,0:T(8,128)(2,1)}, bf16[1,4,64,128]{3,2,1,0:T(8,128)(2,1)S(1)}, u32[]{:S(2)}, u32[]{:S(2)}) collective-permute-start(bf16[1,4,64,128]{3,2,1,0:T(8,128)(2,1)} %bitcast.15), channel_id=1, source_target_pairs={{16,0},{32,16},{48,32},{64,48},{80,64},{96,80},{112,96},{128,112},... | collective-permute-start | bytes 196616 | tf_op jit(solution)/shard_map/ppermute | solution.py:66
  53.1 1.8 fusion.43
  54.9 1.9 fusion.39
  56.8 23.5 %collective-permute-done = bf16[1,4,64,128]{3,2,1,0:T(8,128)(2,1)} collective-permute-done((bf16[1,4,64,128]{3,2,1,0:T(8,128)(2,1)}, bf16[1,4,64,128]{3,2,1,0:T(8,128)(2,1)}, u32[]{:S(2)}, u32[]{:S(2)}) %collective-permute-start) | collective-permute-done | bytes 65568 | tf_op jit(solution)/shard_map/ppermute | solution.py:65
  80.3 1.9 convolution_add_fusion.4
  82.1 20.8 %all-to-all-done = bf16[32,2,12416]{2,1,0:T(2,128)(2,1)} async-done(((bf16[32,2,12416]{2,1,0:T(2,128)(2,1)}), bf16[32,2,12416]{2,1,0:T(2,128)(2,1)}, u32[]{:S(2)}, u32[]{:S(2)}) %all-to-all-start) | async-done | bytes 1589280 | tf_op jit(solution)/shard_map/all_to_all | solution.py:155
  103.0 3.6 %reshape.375 = bf16[64,12416]{1,0:T(8,128)(2,1)S(1)} reshape(bf16[32,2,12416]{2,1,0:T(2,128)(2,1)} %all-to-all-done) | data formatting | bytes 3178496 | tf_op jit(solution)/shard_map/reshape | solution.py:156
  107.4 1.1 slice_bitcast_fusion
  109.2 2.1 %reshape.376 = bf16[64,64,64]{2,1,0:T(8,128)(2,1)S(1)} reshape(bf16[64,4096]{1,0:T(8,128)(2,1)} %slice.194) | data formatting | bytes 1048576 | tf_op jit(solution)/shard_map/reshape | solution.py:158
  111.2 1.5 copy.55
  113.4 2.0 %fusion.3 = f32[16,64,128]{2,0,1:T(8,128)S(1)} fusion(f32[64,64,128]{2,1,0:T(8,128)S(1)} %fusion.106, f32[64]{0:T(128)S(1)} %copy-done.14), kind=kOutput, calls=%fused_computation.8 | convolution fusion | flops 100664320 | bytes 2621696 | tf_op jit(solution)/shard_map/ns,saf->naf/dot_general | solution.py:112
  116.0 2.2 %gather_fusion.1 = bf16[48,8192]{1,0:T(8,128)(2,1)} fusion(bf16[16,8192]{1,0:T(8,128)(2,1)S(1)} %bitcast.111, s32[1024]{0:T(1024)} %copy-done.13), kind=kCustom, calls=%fused_computation.1 | custom fusion | bytes 1573056 | tf_op jit(solution)/shard_map/gather | solution.py:167
  118.2 1.5 fusion.5
  119.8 1.3 copy.57
  121.0 13.6 %all-to-all-start.1 = ((bf16[32,2,64,128]{3,2,1,0:T(8,128)(2,1)}), bf16[32,2,64,128]{3,2,1,0:T(8,128)(2,1)}, u32[]{:S(2)}, u32[]{:S(2)}) async-start(bf16[32,2,64,128]{3,2,1,0:T(8,128)(2,1)} %bitcast.117), calls=%async_computation.1 | async-start | bytes 2097152 | tf_op jit(solution)/shard_map/all_to_all | solution.py:171
  135.4 1.9 collective-permute-start.7
  137.4 14.5 %collective-permute-start.6 = (bf16[4,1,64,128]{3,2,1,0:T(8,128)(2,1)S(1)}, bf16[4,1,64,128]{3,2,1,0:T(8,128)(2,1)S(1)}, u32[]{:S(2)}, u32[]{:S(2)}) collective-permute-start(bf16[4,1,64,128]{3,2,1,0:T(8,128)(2,1)S(1)} %get-tuple-element.21), channel_id=1, source_target_pairs={{0,1},{1,2},{2,3},{3,4},{4,5},{5,6},{6,7},{7,8},{8,9},{9,10},{10,1... | collective-permute-start | bytes 196616 | tf_op jit(solution)/shard_map/ppermute | solution.py:67
  151.8 3.1 %collective-permute-start.4 = (bf16[1,4,64,128]{3,2,1,0:T(8,128)(2,1)S(1)}, bf16[1,4,64,128]{3,2,1,0:T(8,128)(2,1)S(1)}, u32[]{:S(2)}, u32[]{:S(2)}) collective-permute-start(bf16[1,4,64,128]{3,2,1,0:T(8,128)(2,1)S(1)} %get-tuple-element.20), channel_id=1, source_target_pairs={{0,16},{16,32},{32,48},{48,64},{64,80},{80,96},{96,112},{112,128},... | collective-permute-start | bytes 196616 | tf_op jit(solution)/shard_map/ppermute | solution.py:65
  154.9 2.4 %collective-permute-start.5 = (bf16[1,4,64,128]{3,2,1,0:T(8,128)(2,1)S(1)}, bf16[1,4,64,128]{3,2,1,0:T(8,128)(2,1)S(1)}, u32[]{:S(2)}, u32[]{:S(2)}) collective-permute-start(bf16[1,4,64,128]{3,2,1,0:T(8,128)(2,1)S(1)} %get-tuple-element.19), channel_id=1, source_target_pairs={{16,0},{32,16},{48,32},{64,48},{80,64},{96,80},{112,96},{128,112},... | collective-permute-start | bytes 196616 | tf_op jit(solution)/shard_map/ppermute | solution.py:66
  157.6 1.0 convolution_add_fusion
  160.7 6.3 %collective-permute-done.4 = bf16[1,4,64,128]{3,2,1,0:T(8,128)(2,1)S(1)} collective-permute-done((bf16[1,4,64,128]{3,2,1,0:T(8,128)(2,1)S(1)}, bf16[1,4,64,128]{3,2,1,0:T(8,128)(2,1)S(1)}, u32[]{:S(2)}, u32[]{:S(2)}) %collective-permute-start.4) | collective-permute-done | bytes 65568 | tf_op jit(solution)/shard_map/ppermute | solution.py:65
  167.2 19.5 %all-to-all-done.1 = bf16[32,2,64,128]{3,2,1,0:T(8,128)(2,1)} async-done(((bf16[32,2,64,128]{3,2,1,0:T(8,128)(2,1)}), bf16[32,2,64,128]{3,2,1,0:T(8,128)(2,1)}, u32[]{:S(2)}, u32[]{:S(2)}) %all-to-all-start.1) | async-done | bytes 1048608 | tf_op jit(solution)/shard_map/all_to_all | solution.py:171
  186.8 1.6 fusion.107
  188.5 2.0 %fusion.1 = f32[16,64,128]{2,0,1:T(8,128)S(1)} fusion(f32[64,64,128]{2,1,0:T(8,128)S(1)} %fusion.107, f32[64]{0:T(128)S(1)} %copy-done.15), kind=kOutput, calls=%fused_computation.6 | convolution fusion | flops 100664320 | bytes 2621696 | tf_op jit(solution)/shard_map/ns,saf->naf/dot_general | solution.py:112
  (118 shorter events, 18.7 us)
Async XLA Ops:
  0.0 4.7 %copy-start.17 = (f32[32]{0:T(128)S(1)}, f32[32]{0:T(128)}, u32[]{:S(2)}) copy-start(f32[32]{0:T(128)} %param.18) | copy-start | bytes 388
  0.0 4.8 %copy-start.18 = (f32[32]{0:T(128)S(1)}, f32[32]{0:T(128)}, u32[]{:S(2)}) copy-start(f32[32]{0:T(128)} %param.17) | copy-start | bytes 388
  0.0 4.9 %copy-start.16 = (s32[1,1,48,1]{2,3,1,0:T(1,128)S(1)}, s32[1,1,48,1]{2,3,1,0:T(1,128)}, u32[]{:S(2)}) copy-start(s32[1,1,48,1]{2,3,1,0:T(1,128)} %param.21) | copy-start | bytes 580
  0.0 5.3 %copy-start.20 = (s32[1,1,48]{2,1,0:T(1,128)S(1)}, s32[1,1,48]{2,1,0:T(1,128)}, u32[]{:S(2)}) copy-start(s32[1,1,48]{2,1,0:T(1,128)} %param.22) | copy-start | bytes 580
  2.9 3.4 %copy-start.6 = (bf16[4,4,64,128]{3,2,1,0:T(8,128)(2,1)S(1)}, bf16[4,4,64,128]{3,2,1,0:T(8,128)(2,1)}, u32[]{:S(2)}) copy-start(bf16[4,4,64,128]{3,2,1,0:T(8,128)(2,1)} %param.14) | copy-start | bytes 786436
  6.7 0.7 copy-start.21
  7.4 1.1 copy-start.13
  7.4 1.1 copy-start.11
  11.5 39.5 %copy-start.9 = (bf16[4,4,5,4096]{3,1,2,0:T(4,128)(2,1)S(1)}, bf16[4,4,5,4096]{3,1,2,0:T(4,128)(2,1)}, u32[]{:S(2)}) copy-start(bf16[4,4,5,4096]{3,1,2,0:T(4,128)(2,1)} %param.19) | copy-start | bytes 1966084
  11.6 91.4 %all-to-all-start = ((bf16[32,2,12416]{2,1,0:T(2,128)(2,1)}), bf16[32,2,12416]{2,1,0:T(2,128)(2,1)}, u32[]{:S(2)}, u32[]{:S(2)}) async-start(bf16[32,2,12416]{2,1,0:T(2,128)(2,1)} %reshape.374), calls=%async_computation | async-start | bytes 3178496 | tf_op jit(solution)/shard_map/all_to_all | solution.py:155
  27.1 26.0 %collective-permute-start.3 = (bf16[4,1,64,128]{3,2,1,0:T(8,128)(2,1)}, bf16[4,1,64,128]{3,2,1,0:T(8,128)(2,1)}, u32[]{:S(2)}, u32[]{:S(2)}) collective-permute-start(bf16[4,1,64,128]{3,2,1,0:T(8,128)(2,1)} %get-tuple-element.30), channel_id=1, source_target_pairs={{1,0},{2,1},{3,2},{4,3},{5,4},{6,5},{7,6},{8,7},{9,8},{10,9},{11,1... | collective-permute-start | bytes 196616 | tf_op jit(solution)/shard_map/ppermute | solution.py:68
  30.2 24.7 %collective-permute-start.2 = (bf16[4,1,64,128]{3,2,1,0:T(8,128)(2,1)}, bf16[4,1,64,128]{3,2,1,0:T(8,128)(2,1)}, u32[]{:S(2)}, u32[]{:S(2)}) collective-permute-start(bf16[4,1,64,128]{3,2,1,0:T(8,128)(2,1)} %get-tuple-element.29), channel_id=1, source_target_pairs={{0,1},{1,2},{2,3},{3,4},{4,5},{5,6},{6,7},{7,8},{8,9},{9,10},{10,1... | collective-permute-start | bytes 196616 | tf_op jit(solution)/shard_map/ppermute | solution.py:67
  44.2 36.0 %collective-permute-start = (bf16[1,4,64,128]{3,2,1,0:T(8,128)(2,1)}, bf16[1,4,64,128]{3,2,1,0:T(8,128)(2,1)}, u32[]{:S(2)}, u32[]{:S(2)}) collective-permute-start(bf16[1,4,64,128]{3,2,1,0:T(8,128)(2,1)} %bitcast.11), channel_id=1, source_target_pairs={{0,16},{16,32},{32,48},{48,64},{64,80},{80,96},{96,112},{112,128},... | collective-permute-start | bytes 196616 | tf_op jit(solution)/shard_map/ppermute | solution.py:65
  48.1 67.5 %collective-permute-start.1 = (bf16[1,4,64,128]{3,2,1,0:T(8,128)(2,1)}, bf16[1,4,64,128]{3,2,1,0:T(8,128)(2,1)S(1)}, u32[]{:S(2)}, u32[]{:S(2)}) collective-permute-start(bf16[1,4,64,128]{3,2,1,0:T(8,128)(2,1)} %bitcast.15), channel_id=1, source_target_pairs={{16,0},{32,16},{48,32},{64,48},{80,64},{96,80},{112,96},{128,112},... | collective-permute-start | bytes 196616 | tf_op jit(solution)/shard_map/ppermute | solution.py:66
  112.7 0.7 copy-start.14
  113.4 2.2 %copy-start = (f32[4,4,128,64]{2,3,1,0:T(8,128)S(1)}, f32[4,4,128,64]{2,3,1,0:T(8,128)}, u32[]{:S(2)}) copy-start(f32[4,4,128,64]{2,3,1,0:T(8,128)} %convolution_add_fusion.4) | copy-start | bytes 1572868
  113.4 2.2 %copy-start.2 = (f32[4,4,128,64]{2,3,1,0:T(8,128)S(1)}, f32[4,4,128,64]{2,3,1,0:T(8,128)}, u32[]{:S(2)}) copy-start(f32[4,4,128,64]{2,3,1,0:T(8,128)} %fusion.43) | copy-start | bytes 1572868
  113.4 2.2 %copy-start.4 = (f32[4,4,128,64]{2,3,1,0:T(8,128)S(1)}, f32[4,4,128,64]{2,3,1,0:T(8,128)}, u32[]{:S(2)}) copy-start(f32[4,4,128,64]{2,3,1,0:T(8,128)} %fusion.39) | copy-start | bytes 1572868
  116.0 2.2 %copy-start.12 = (bf16[48,32,2]{0,2,1:T(2,128)(2,1)S(1)}, bf16[48,32,2]{0,2,1:T(2,128)(2,1)}, u32[]{:S(2)}) copy-start(bf16[48,32,2]{0,2,1:T(2,128)(2,1)} %copy-done.11) | copy-start | bytes 18436
  119.8 14.8 %copy-start.10 = (bf16[4,32,4,32]{3,2,1,0:T(4,128)(2,1)S(1)}, bf16[4,32,4,32]{3,2,1,0:T(4,128)(2,1)}, u32[]{:S(2)}) copy-start(bf16[4,32,4,32]{3,2,1,0:T(4,128)(2,1)} %get-tuple-element.48) | copy-start | bytes 98308
  121.0 13.8 %copy-start.8 = (f32[4,32,4,32]{3,2,1,0:T(4,128)S(1)}, f32[4,32,4,32]{3,2,1,0:T(4,128)}, u32[]{:S(2)}) copy-start(f32[4,32,4,32]{3,2,1,0:T(4,128)} %get-tuple-element.46) | copy-start | bytes 196612
  121.0 14.0 %copy-start.19 = (f32[32]{0:T(128)S(1)}, f32[32]{0:T(128)}, u32[]{:S(2)}) copy-start(f32[32]{0:T(128)} %param.25) | copy-start | bytes 388
  121.0 65.8 %all-to-all-start.1 = ((bf16[32,2,64,128]{3,2,1,0:T(8,128)(2,1)}), bf16[32,2,64,128]{3,2,1,0:T(8,128)(2,1)}, u32[]{:S(2)}, u32[]{:S(2)}) async-start(bf16[32,2,64,128]{3,2,1,0:T(8,128)(2,1)} %bitcast.117), calls=%async_computation.1 | async-start | bytes 2097152 | tf_op jit(solution)/shard_map/all_to_all | solution.py:171
  135.4 23.3 %collective-permute-start.7 = (bf16[4,1,64,128]{3,2,1,0:T(8,128)(2,1)S(1)}, bf16[4,1,64,128]{3,2,1,0:T(8,128)(2,1)S(1)}, u32[]{:S(2)}, u32[]{:S(2)}) collective-permute-start(bf16[4,1,64,128]{3,2,1,0:T(8,128)(2,1)S(1)} %get-tuple-element.22), channel_id=1, source_target_pairs={{1,0},{2,1},{3,2},{4,3},{5,4},{6,5},{7,6},{8,7},{9,8},{10,9},{11,1... | collective-permute-start | bytes 196616 | tf_op jit(solution)/shard_map/ppermute | solution.py:68
  137.4 22.4 %collective-permute-start.6 = (bf16[4,1,64,128]{3,2,1,0:T(8,128)(2,1)S(1)}, bf16[4,1,64,128]{3,2,1,0:T(8,128)(2,1)S(1)}, u32[]{:S(2)}, u32[]{:S(2)}) collective-permute-start(bf16[4,1,64,128]{3,2,1,0:T(8,128)(2,1)S(1)} %get-tuple-element.21), channel_id=1, source_target_pairs={{0,1},{1,2},{2,3},{3,4},{4,5},{5,6},{6,7},{7,8},{8,9},{9,10},{10,1... | collective-permute-start | bytes 196616 | tf_op jit(solution)/shard_map/ppermute | solution.py:67
  151.8 15.2 %collective-permute-start.4 = (bf16[1,4,64,128]{3,2,1,0:T(8,128)(2,1)S(1)}, bf16[1,4,64,128]{3,2,1,0:T(8,128)(2,1)S(1)}, u32[]{:S(2)}, u32[]{:S(2)}) collective-permute-start(bf16[1,4,64,128]{3,2,1,0:T(8,128)(2,1)S(1)} %get-tuple-element.20), channel_id=1, source_target_pairs={{0,16},{16,32},{32,48},{48,64},{64,80},{80,96},{96,112},{112,128},... | collective-permute-start | bytes 196616 | tf_op jit(solution)/shard_map/ppermute | solution.py:65
  154.9 35.7 %collective-permute-start.5 = (bf16[1,4,64,128]{3,2,1,0:T(8,128)(2,1)S(1)}, bf16[1,4,64,128]{3,2,1,0:T(8,128)(2,1)S(1)}, u32[]{:S(2)}, u32[]{:S(2)}) collective-permute-start(bf16[1,4,64,128]{3,2,1,0:T(8,128)(2,1)S(1)} %get-tuple-element.19), channel_id=1, source_target_pairs={{16,0},{32,16},{48,32},{64,48},{80,64},{96,80},{112,96},{128,112},... | collective-permute-start | bytes 196616 | tf_op jit(solution)/shard_map/ppermute | solution.py:66
  186.8 1.7 copy-start.15
  188.5 2.2 %copy-start.3 = (f32[4,4,128,64]{2,3,1,0:T(8,128)S(1)}, f32[4,4,128,64]{2,3,1,0:T(8,128)}, u32[]{:S(2)}) copy-start(f32[4,4,128,64]{2,3,1,0:T(8,128)} %fusion.57) | copy-start | bytes 1572868
  188.5 2.2 %copy-start.5 = (f32[4,4,128,64]{2,3,1,0:T(8,128)S(1)}, f32[4,4,128,64]{2,3,1,0:T(8,128)}, u32[]{:S(2)}) copy-start(f32[4,4,128,64]{2,3,1,0:T(8,128)} %fusion.53) | copy-start | bytes 1572868
  190.6 1.0 copy-start.1
  190.9 1.3 copy-start.7

commit v2 on v1

--- a/solution.py
+++ b/solution.py
@@ -103,13 +103,36 @@
     return select.reshape(select.shape[0], -1).astype(jnp.bfloat16)
 
 
-def far_terms(recv_blocks, recv_tiles, recv_targets, nblocks):
+def slot_targets(out_dev, out_target, cap):
+    me = lax.axis_index("rx")
+    info = jnp.stack([out_dev.reshape(-1), out_target.reshape(-1)], axis=0)
+    every = lax.all_gather(info, "rx")
+    hits = (every[:, 0] == me).astype(jnp.int32)
+    ranks = jnp.cumsum(hits, axis=1) - 1
+    slot_ids = jnp.arange(cap, dtype=jnp.int32)
+    picks = hits[:, :, None] * (ranks[:, :, None] == slot_ids[None, None, :]).astype(jnp.int32)
+    found = jnp.sum(picks * (every[:, 1, :, None] + 1), axis=1) - 1
+    return found.reshape(-1)
+
+
+def send_products(signal, edge_tiles, sources, select):
+    block_rows, block_cols, block_size, features = signal.shape
+    flat = signal.reshape(block_rows * block_cols, block_size, features)
     products = jnp.einsum(
-        "sab,sbf->saf", recv_tiles, recv_blocks, preferred_element_type=jnp.float32
-    )
-    block_ids = jnp.arange(nblocks, dtype=jnp.float32)
-    onehot = (recv_targets[None, :] == block_ids[:, None]).astype(jnp.float32)
-    return jnp.einsum("ns,saf->naf", onehot, products, precision=lax.Precision.HIGHEST)
+        "eab,ebf->eaf", edge_tiles, flat[sources], preferred_element_type=jnp.float32
+    ).astype(jnp.bfloat16)
+    slots = jnp.einsum(
+        "es,eaf->saf", select, products, preferred_element_type=jnp.float32
+    ).astype(jnp.bfloat16)
+    return slots.reshape(lax.axis_size("rx"), CAP, block_size, features)
+
+
+def far_terms(received, targets, nblocks):
+    received = received.reshape(targets.shape[0], -1)
+    onehot = (targets[None, :] == jnp.arange(nblocks, dtype=jnp.int32)[:, None]).astype(
+        jnp.bfloat16
+    )
+    return jnp.einsum("ns,sk->nk", onehot, received, preferred_element_type=jnp.float32)
 
 
 def local(
@@ -136,42 +159,21 @@
 
     select = edge_select(out_dev, n_rx)
     sources = out_block.reshape(-1)
-    edge_count = sources.shape[0]
-    block_len = block_size * features
-    tile_len = out_tiles.shape[-1]
-
-    flat_gated = gated.reshape(nblocks, block_len)
-    target_col = jnp.zeros((edge_count, 128), jnp.bfloat16).at[:, 0].set(
-        (out_target.reshape(-1) + 1).astype(jnp.bfloat16)
-    )
-    payload = jnp.concatenate(
-        [flat_gated[sources], out_tiles.reshape(edge_count, tile_len), target_col], axis=1
-    )
-    send_one = jnp.einsum(
-        "es,ek->sk", select, payload, preferred_element_type=jnp.float32
-    ).astype(jnp.bfloat16)
-    send_one = send_one.reshape(n_rx, CAP, -1)
+    edge_tiles = out_tiles.reshape(-1, block_size, block_size)
+    targets = slot_targets(out_dev, out_target, CAP)
+
+    send_one = send_products(gated, edge_tiles, sources, select)
     halo_one = fetch_halo(gated)
     recv_one = lax.all_to_all(send_one, "rx", split_axis=0, concat_axis=0, tiled=True)
-    recv_one = recv_one.reshape(n_rx * CAP, -1)
-    recv_blocks = recv_one[:, :block_len].reshape(-1, block_size, features)
-    recv_tiles = recv_one[:, block_len : block_len + tile_len].reshape(-1, block_size, block_size)
-    recv_targets = recv_one[:, block_len + tile_len].astype(jnp.float32) - 1.0
-
     near_one = local_terms(gated, tiles, halo_one)
-    far_one = far_terms(recv_blocks, recv_tiles, recv_targets, nblocks)
+    far_one = far_terms(recv_one, targets, nblocks)
     first_hop = (near_one + far_one.reshape(gated.shape)).astype(jnp.bfloat16)
 
-    flat_first = first_hop.reshape(nblocks, block_len)
-    send_two = jnp.einsum(
-        "es,ek->sk", select, flat_first[sources], preferred_element_type=jnp.float32
-    ).astype(jnp.bfloat16)
-    send_two = send_two.reshape(n_rx, CAP, block_size, features)
+    send_two = send_products(first_hop, edge_tiles, sources, select)
     halo_two = fetch_halo(first_hop)
     recv_two = lax.all_to_all(send_two, "rx", split_axis=0, concat_axis=0, tiled=True)
-    recv_two = recv_two.reshape(n_rx * CAP, block_size, features)
     near_two = local_terms(first_hop, tiles, halo_two)
-    far_two = far_terms(recv_two, recv_tiles, recv_targets, nblocks)
+    far_two = far_terms(recv_two, targets, nblocks)
     second_hop = near_two + far_two.reshape(gated.shape)
 
     input_signals, output_signals = group_eye(channels)

time: 194 us -> 244 us (1.26)
  the two profiles are of different devices: /device:TPU:57 before, /device:TPU:56 now
where the time goes in v2:
time: 244 us; the launch traced here: 242 us
  blocking collectives  125 us (51%)
  starting transfers between devices  48.7 us (20%)
  waiting for transfers between devices  27 us (11%)
  matrix products  18.1 us (7%)
  local copies, waits for them, and re-layouts  15.5 us (6%)
  other arithmetic  7.21 us (3%)
    all_gather x1, blocking collectives, slot_targets(): every = lax.all_gather(info, 'rx')  125 us
    all_to_all x1, waiting for transfers between devices, local(): lax.all_to_all(send_two, 'rx', split_axis=0, concat_axis=0, tiled=True)  19.7 us
    all_to_all x1, starting transfers between devices, local(): lax.all_to_all(send_one, 'rx', split_axis=0, concat_axis=0, tiled=True)  15.4 us
    dot_general x8, matrix products, local_terms(): jnp.einsum('ijab,ijbf->ijaf', tiles[:, :, offset], neighbours[offset], pr...  9.93 us
    all_to_all x1, starting transfers between devices, local(): lax.all_to_all(send_two, 'rx', split_axis=0, concat_axis=0, tiled=True)  9.92 us
    ppermute x2, starting transfers between devices, fetch_halo(): right = lax.ppermute(signal[:, :1], 'ry', shift_pairs(n_ry, -1))  7.29 us
    ppermute x2, waiting for transfers between devices, fetch_halo(): above = lax.ppermute(signal[-1:], 'rx', shift_pairs(n_rx, 1))  7.21 us
    ppermute x2, starting transfers between devices, fetch_halo(): above = lax.ppermute(signal[-1:], 'rx', shift_pairs(n_rx, 1))  6.87 us
  transfers between devices with their start and end apart: 10, of which 3 were waited for; matrix products, arithmetic and copies ran while one was open for 7% of the time, Pallas kernels for 0%

profile of v2, /device:TPU:56, one launch (start us, length us, event | category | flops | bytes accessed | tf_op | source)
XLA Modules:
  0.0 242.4 jit_solution(15346031603362001588)
XLA Ops:
  3.1 0.8 select_reduce_fusion
  6.1 1.8 reshape.373
  7.9 1.2 add_convert_fusion.1
  11.8 0.8 convolution_convert_fusion.1
  12.6 2.2 copy.74
  14.8 15.4 %all-to-all-start = ((bf16[32,2,64,128]{3,2,1,0:T(8,128)(2,1)}), bf16[32,2,64,128]{3,2,1,0:T(8,128)(2,1)}, u32[]{:S(2)}, u32[]{:S(2)}) async-start(bf16[32,2,64,128]{3,2,1,0:T(8,128)(2,1)} %copy.74), calls=%async_computation | async-start | bytes 2097152 | tf_op jit(solution)/shard_map/all_to_all | solution.py:167
  31.0 3.4 %collective-permute-start = (bf16[1,4,64,128]{3,2,1,0:T(8,128)(2,1)}, bf16[1,4,64,128]{3,2,1,0:T(8,128)(2,1)}, u32[]{:S(2)}, u32[]{:S(2)}) collective-permute-start(bf16[1,4,64,128]{3,2,1,0:T(8,128)(2,1)} %bitcast.11), channel_id=1, source_target_pairs={{0,16},{16,32},{32,48},{48,64},{64,80},{80,96},{96,112},{112,128},... | collective-permute-start | bytes 196616 | tf_op jit(solution)/shard_map/ppermute | solution.py:65
  35.1 3.1 %collective-permute-start.1 = (bf16[1,4,64,128]{3,2,1,0:T(8,128)(2,1)}, bf16[1,4,64,128]{3,2,1,0:T(8,128)(2,1)}, u32[]{:S(2)}, u32[]{:S(2)}) collective-permute-start(bf16[1,4,64,128]{3,2,1,0:T(8,128)(2,1)} %bitcast.15), channel_id=1, source_target_pairs={{16,0},{32,16},{48,32},{64,48},{80,64},{96,80},{112,96},{128,112},... | collective-permute-start | bytes 196616 | tf_op jit(solution)/shard_map/ppermute | solution.py:66
  38.8 1.9 collective-permute-start.2
  40.7 3.6 %collective-permute-start.3 = (bf16[4,1,64,128]{3,2,1,0:T(8,128)(2,1)}, bf16[4,1,64,128]{3,2,1,0:T(8,128)(2,1)}, u32[]{:S(2)}, u32[]{:S(2)}) collective-permute-start(bf16[4,1,64,128]{3,2,1,0:T(8,128)(2,1)} %get-tuple-element.18), channel_id=1, source_target_pairs={{1,0},{2,1},{3,2},{4,3},{5,4},{6,5},{7,6},{8,7},{9,8},{10,9},{11,1... | collective-permute-start | bytes 196616 | tf_op jit(solution)/shard_map/ppermute | solution.py:68
  44.4 125.3 %all-gather.1 = s32[32,2,48]{2,1,0:T(2,128)S(1)} all-gather(s32[1,2,48]{2,1,0:T(2,128)S(1)} %add_bitcast_fusion), channel_id=2, replica_groups=mesh['rx'=32,'ry'=16] {'rx'}, dimensions={0}, use_global_device_ids=true | all-gather | bytes 12672 | tf_op jit(solution)/shard_map/all_gather | solution.py:109
  171.2 1.0 reshape.371
  172.9 1.9 fusion.33
  174.8 1.9 fusion.37
  176.7 1.1 convolution_add_fusion.4
  177.8 1.9 fusion.16
  179.7 1.5 fusion.13
  181.2 0.8 gather_fusion.1
  182.4 0.8 convolution_convert_fusion
  183.1 2.2 copy.79
  185.3 9.9 %all-to-all-start.1 = ((bf16[32,2,64,128]{3,2,1,0:T(8,128)(2,1)}), bf16[32,2,64,128]{3,2,1,0:T(8,128)(2,1)}, u32[]{:S(2)}, u32[]{:S(2)}) async-start(bf16[32,2,64,128]{3,2,1,0:T(8,128)(2,1)} %copy.79), calls=%async_computation.1 | async-start | bytes 2097152 | tf_op jit(solution)/shard_map/all_to_all | solution.py:174
  196.1 1.9 collective-permute-start.6
  198.0 3.6 %collective-permute-start.7 = (bf16[4,1,64,128]{3,2,1,0:T(8,128)(2,1)S(1)}, bf16[4,1,64,128]{3,2,1,0:T(8,128)(2,1)S(1)}, u32[]{:S(2)}, u32[]{:S(2)}) collective-permute-start(bf16[4,1,64,128]{3,2,1,0:T(8,128)(2,1)S(1)} %get-tuple-element.10), channel_id=1, source_target_pairs={{1,0},{2,1},{3,2},{4,3},{5,4},{6,5},{7,6},{8,7},{9,8},{10,9},{11,1... | collective-permute-start | bytes 196616 | tf_op jit(solution)/shard_map/ppermute | solution.py:68
  201.7 2.3 collective-permute-start.5
  204.0 3.5 %collective-permute-start.4 = (bf16[1,4,64,128]{3,2,1,0:T(8,128)(2,1)S(1)}, bf16[1,4,64,128]{3,2,1,0:T(8,128)(2,1)S(1)}, u32[]{:S(2)}, u32[]{:S(2)}) collective-permute-start(bf16[1,4,64,128]{3,2,1,0:T(8,128)(2,1)S(1)} %get-tuple-element.8), channel_id=1, source_target_pairs={{0,16},{16,32},{32,48},{48,64},{64,80},{80,96},{96,112},{112,128},... | collective-permute-start | bytes 196616 | tf_op jit(solution)/shard_map/ppermute | solution.py:65
  208.1 1.0 fusion.47
  209.2 1.0 fusion.51
  210.3 7.2 %collective-permute-done.4 = bf16[1,4,64,128]{3,2,1,0:T(8,128)(2,1)S(1)} collective-permute-done((bf16[1,4,64,128]{3,2,1,0:T(8,128)(2,1)S(1)}, bf16[1,4,64,128]{3,2,1,0:T(8,128)(2,1)S(1)}, u32[]{:S(2)}, u32[]{:S(2)}) %collective-permute-start.4) | collective-permute-done | bytes 65568 | tf_op jit(solution)/shard_map/ppermute | solution.py:65
  217.7 19.7 %all-to-all-done.1 = bf16[32,2,64,128]{3,2,1,0:T(8,128)(2,1)} async-done(((bf16[32,2,64,128]{3,2,1,0:T(8,128)(2,1)}), bf16[32,2,64,128]{3,2,1,0:T(8,128)(2,1)}, u32[]{:S(2)}, u32[]{:S(2)}) %all-to-all-start.1) | async-done | bytes 1048608 | tf_op jit(solution)/shard_map/all_to_all | solution.py:174
  237.3 1.9 fusion.14
  239.3 1.4 fusion.7
  241.7 0.8 add_convert_fusion
  (101 shorter events, 15.0 us)
Async XLA Ops:
  2.2 8.6 %copy-start.8 = (s32[1024]{0:T(1024)}, s32[1024]{0:T(1024)S(1)}, u32[]{:S(2)}) copy-start(s32[1024]{0:T(1024)S(1)} %pad_clamp_fusion) | copy-start | bytes 12292
  7.9 2.0 copy-start
  14.8 29.6 %copy-start.11 = (s32[1,1,48,1]{2,3,1,0:T(1,128)S(1)}, s32[1,1,48,1]{2,3,1,0:T(1,128)}, u32[]{:S(2)}) copy-start(s32[1,1,48,1]{2,3,1,0:T(1,128)} %param.19) | copy-start | bytes 580
  14.8 29.6 %copy-start.13 = (s32[1,1,48]{2,1,0:T(1,128)S(1)}, s32[1,1,48]{2,1,0:T(1,128)}, u32[]{:S(2)}) copy-start(s32[1,1,48]{2,1,0:T(1,128)} %param.20) | copy-start | bytes 580
  14.8 156.1 %copy-start.3 = (bf16[4,4,5,4096]{3,1,2,0:T(4,128)(2,1)S(1)}, bf16[4,4,5,4096]{3,1,2,0:T(4,128)(2,1)}, u32[]{:S(2)}) copy-start(bf16[4,4,5,4096]{3,1,2,0:T(4,128)(2,1)} %param.17) | copy-start | bytes 1966084
  14.8 162.9 %all-to-all-start = ((bf16[32,2,64,128]{3,2,1,0:T(8,128)(2,1)}), bf16[32,2,64,128]{3,2,1,0:T(8,128)(2,1)}, u32[]{:S(2)}, u32[]{:S(2)}) async-start(bf16[32,2,64,128]{3,2,1,0:T(8,128)(2,1)} %copy.74), calls=%async_computation | async-start | bytes 2097152 | tf_op jit(solution)/shard_map/all_to_all | solution.py:167
  31.0 145.7 %collective-permute-start = (bf16[1,4,64,128]{3,2,1,0:T(8,128)(2,1)}, bf16[1,4,64,128]{3,2,1,0:T(8,128)(2,1)}, u32[]{:S(2)}, u32[]{:S(2)}) collective-permute-start(bf16[1,4,64,128]{3,2,1,0:T(8,128)(2,1)} %bitcast.11), channel_id=1, source_target_pairs={{0,16},{16,32},{32,48},{48,64},{64,80},{80,96},{96,112},{112,128},... | collective-permute-start | bytes 196616 | tf_op jit(solution)/shard_map/ppermute | solution.py:65
  35.1 144.6 %collective-permute-start.1 = (bf16[1,4,64,128]{3,2,1,0:T(8,128)(2,1)}, bf16[1,4,64,128]{3,2,1,0:T(8,128)(2,1)}, u32[]{:S(2)}, u32[]{:S(2)}) collective-permute-start(bf16[1,4,64,128]{3,2,1,0:T(8,128)(2,1)} %bitcast.15), channel_id=1, source_target_pairs={{16,0},{32,16},{48,32},{64,48},{80,64},{96,80},{112,96},{128,112},... | collective-permute-start | bytes 196616 | tf_op jit(solution)/shard_map/ppermute | solution.py:66
  38.8 134.1 %collective-permute-start.2 = (bf16[4,1,64,128]{3,2,1,0:T(8,128)(2,1)}, bf16[4,1,64,128]{3,2,1,0:T(8,128)(2,1)}, u32[]{:S(2)}, u32[]{:S(2)}) collective-permute-start(bf16[4,1,64,128]{3,2,1,0:T(8,128)(2,1)} %get-tuple-element.17), channel_id=1, source_target_pairs={{0,1},{1,2},{2,3},{3,4},{4,5},{5,6},{6,7},{7,8},{8,9},{9,10},{10,1... | collective-permute-start | bytes 196616 | tf_op jit(solution)/shard_map/ppermute | solution.py:67
  40.7 134.1 %collective-permute-start.3 = (bf16[4,1,64,128]{3,2,1,0:T(8,128)(2,1)}, bf16[4,1,64,128]{3,2,1,0:T(8,128)(2,1)}, u32[]{:S(2)}, u32[]{:S(2)}) collective-permute-start(bf16[4,1,64,128]{3,2,1,0:T(8,128)(2,1)} %get-tuple-element.18), channel_id=1, source_target_pairs={{1,0},{2,1},{3,2},{4,3},{5,4},{6,5},{7,6},{8,7},{9,8},{10,9},{11,1... | collective-permute-start | bytes 196616 | tf_op jit(solution)/shard_map/ppermute | solution.py:68
  172.9 4.8 %copy-start.6 = (s32[4,4]{1,0:T(4,128)}, s32[4,4]{1,0:T(4,128)S(1)}, u32[]{:S(2)}) copy-start(s32[4,4]{1,0:T(4,128)S(1)} %multiply_add_fusion) | copy-start | bytes 196
  174.8 2.9 %copy-start.9 = (s32[64]{0:T(128)S(1)}, s32[64]{0:T(128)}, u32[]{:S(2)}) copy-start(s32[64]{0:T(128)} %sub.23) | copy-start | bytes 772
  185.3 9.9 %copy-start.12 = (f32[32]{0:T(128)S(1)}, f32[32]{0:T(128)}, u32[]{:S(2)}) copy-start(f32[32]{0:T(128)} %param.23) | copy-start | bytes 388
  185.3 10.0 %copy-start.5 = (bf16[4,32,4,32]{3,2,1,0:T(4,128)(2,1)S(1)}, bf16[4,32,4,32]{3,2,1,0:T(4,128)(2,1)}, u32[]{:S(2)}) copy-start(bf16[4,32,4,32]{3,2,1,0:T(4,128)(2,1)} %get-tuple-element.35) | copy-start | bytes 98308
  185.3 10.2 %copy-start.4 = (bf16[4,32,4,32]{3,2,1,0:T(4,128)(2,1)S(1)}, bf16[4,32,4,32]{3,2,1,0:T(4,128)(2,1)}, u32[]{:S(2)}) copy-start(bf16[4,32,4,32]{3,2,1,0:T(4,128)(2,1)} %get-tuple-element.36) | copy-start | bytes 98308
  185.3 10.3 %copy-start.2 = (f32[4,32,4,32]{3,2,1,0:T(4,128)S(1)}, f32[4,32,4,32]{3,2,1,0:T(4,128)}, u32[]{:S(2)}) copy-start(f32[4,32,4,32]{3,2,1,0:T(4,128)} %get-tuple-element.34) | copy-start | bytes 196612
  185.3 52.0 %all-to-all-start.1 = ((bf16[32,2,64,128]{3,2,1,0:T(8,128)(2,1)}), bf16[32,2,64,128]{3,2,1,0:T(8,128)(2,1)}, u32[]{:S(2)}, u32[]{:S(2)}) async-start(bf16[32,2,64,128]{3,2,1,0:T(8,128)(2,1)} %copy.79), calls=%async_computation.1 | async-start | bytes 2097152 | tf_op jit(solution)/shard_map/all_to_all | solution.py:174
  196.1 12.0 %collective-permute-start.6 = (bf16[4,1,64,128]{3,2,1,0:T(8,128)(2,1)S(1)}, bf16[4,1,64,128]{3,2,1,0:T(8,128)(2,1)S(1)}, u32[]{:S(2)}, u32[]{:S(2)}) collective-permute-start(bf16[4,1,64,128]{3,2,1,0:T(8,128)(2,1)S(1)} %get-tuple-element.9), channel_id=1, source_target_pairs={{0,1},{1,2},{2,3},{3,4},{4,5},{5,6},{6,7},{7,8},{8,9},{9,10},{10,1... | collective-permute-start | bytes 196616 | tf_op jit(solution)/shard_map/ppermute | solution.py:67
  198.0 11.2 %collective-permute-start.7 = (bf16[4,1,64,128]{3,2,1,0:T(8,128)(2,1)S(1)}, bf16[4,1,64,128]{3,2,1,0:T(8,128)(2,1)S(1)}, u32[]{:S(2)}, u32[]{:S(2)}) collective-permute-start(bf16[4,1,64,128]{3,2,1,0:T(8,128)(2,1)S(1)} %get-tuple-element.10), channel_id=1, source_target_pairs={{1,0},{2,1},{3,2},{4,3},{5,4},{6,5},{7,6},{8,7},{9,8},{10,9},{11,1... | collective-permute-start | bytes 196616 | tf_op jit(solution)/shard_map/ppermute | solution.py:68
  201.7 37.6 %collective-permute-start.5 = (bf16[1,4,64,128]{3,2,1,0:T(8,128)(2,1)S(1)}, bf16[1,4,64,128]{3,2,1,0:T(8,128)(2,1)S(1)}, u32[]{:S(2)}, u32[]{:S(2)}) collective-permute-start(bf16[1,4,64,128]{3,2,1,0:T(8,128)(2,1)S(1)} %get-tuple-element.7), channel_id=1, source_target_pairs={{16,0},{32,16},{48,32},{64,48},{80,64},{96,80},{112,96},{128,112},... | collective-permute-start | bytes 196616 | tf_op jit(solution)/shard_map/ppermute | solution.py:66
  204.0 13.5 %collective-permute-start.4 = (bf16[1,4,64,128]{3,2,1,0:T(8,128)(2,1)S(1)}, bf16[1,4,64,128]{3,2,1,0:T(8,128)(2,1)S(1)}, u32[]{:S(2)}, u32[]{:S(2)}) collective-permute-start(bf16[1,4,64,128]{3,2,1,0:T(8,128)(2,1)S(1)} %get-tuple-element.8), channel_id=1, source_target_pairs={{0,16},{16,32},{32,48},{48,64},{64,80},{80,96},{96,112},{112,128},... | collective-permute-start | bytes 196616 | tf_op jit(solution)/shard_map/ppermute | solution.py:65
  209.2 28.1 %copy-start.7 = (s32[4,4]{1,0:T(4,128)S(1)}, s32[4,4]{1,0:T(4,128)}, u32[]{:S(2)}) copy-start(s32[4,4]{1,0:T(4,128)} %copy-done.6) | copy-start | bytes 196
  209.2 28.1 %copy-start.10 = (s32[64]{0:T(128)S(1)}, s32[64]{0:T(128)}, u32[]{:S(2)}) copy-start(s32[64]{0:T(128)} %sub.23) | copy-start | bytes 772
  240.7 1.0 copy-start.1

commit v3 on v2

--- a/solution.py
+++ b/solution.py
@@ -103,16 +103,15 @@
     return select.reshape(select.shape[0], -1).astype(jnp.bfloat16)
 
 
-def slot_targets(out_dev, out_target, cap):
+def slot_targets(select, out_target, n_rx):
     me = lax.axis_index("rx")
-    info = jnp.stack([out_dev.reshape(-1), out_target.reshape(-1)], axis=0)
-    every = lax.all_gather(info, "rx")
-    hits = (every[:, 0] == me).astype(jnp.int32)
-    ranks = jnp.cumsum(hits, axis=1) - 1
-    slot_ids = jnp.arange(cap, dtype=jnp.int32)
-    picks = hits[:, :, None] * (ranks[:, :, None] == slot_ids[None, None, :]).astype(jnp.int32)
-    found = jnp.sum(picks * (every[:, 1, :, None] + 1), axis=1) - 1
-    return found.reshape(-1)
+    mine = jnp.einsum(
+        "es,e->s", select.astype(jnp.float32), (out_target.reshape(-1) + 1).astype(jnp.float32)
+    ).reshape(n_rx, 1, CAP)
+    owner = (jnp.arange(n_rx, dtype=jnp.int32) == me).astype(jnp.float32)
+    table = mine * owner[None, :, None]
+    found = lax.psum_scatter(table, "rx", scatter_dimension=0, tiled=True)
+    return found.reshape(-1).astype(jnp.int32) - 1
 
 
 def send_products(signal, edge_tiles, sources, select):
@@ -160,7 +159,7 @@
     select = edge_select(out_dev, n_rx)
     sources = out_block.reshape(-1)
     edge_tiles = out_tiles.reshape(-1, block_size, block_size)
-    targets = slot_targets(out_dev, out_target, CAP)
+    targets = slot_targets(select, out_target, n_rx)
 
     send_one = send_products(gated, edge_tiles, sources, select)
     halo_one = fetch_halo(gated)

time: 244 us -> 351 us (1.44)
  the two profiles are of different devices: /device:TPU:56 before, /device:TPU:262 now
where the time goes in v3:
time: 351 us; the launch traced here: 349 us
  waiting for transfers between devices  193 us (55%)
  starting transfers between devices  96 us (27%)
  local copies, waits for them, and re-layouts  19.6 us (6%)
  matrix products  18.3 us (5%)
  between operations  14 us (4%)
  other arithmetic  8.55 us (2%)
    reduce_scatter x1, waiting for transfers between devices, slot_targets(): found = lax.psum_scatter(table, 'rx', scatter_dimension=0, tiled=True)  184 us
    all_to_all x1, starting transfers between devices, local(): lax.all_to_all(send_two, 'rx', split_axis=0, concat_axis=0, tiled=True)  29.4 us
    ppermute x2, starting transfers between devices, fetch_halo(): right = lax.ppermute(signal[:, :1], 'ry', shift_pairs(n_ry, -1))  28.9 us
    ppermute x2, starting transfers between devices, fetch_halo(): below = lax.ppermute(signal[:1], 'rx', shift_pairs(n_rx, -1))  20.2 us
    dot_general x8, matrix products, local_terms(): jnp.einsum('ijab,ijbf->ijaf', tiles[:, :, offset], neighbours[offset], pr...  9.97 us
    ppermute x2, waiting for transfers between devices, fetch_halo(): above = lax.ppermute(signal[-1:], 'rx', shift_pairs(n_rx, 1))  9.22 us
    all_to_all x1, starting transfers between devices, local(): lax.all_to_all(send_one, 'rx', split_axis=0, concat_axis=0, tiled=True)  8.35 us
  transfers between devices with their start and end apart: 11, of which 2 were waited for; matrix products, arithmetic and copies ran while one was open for 7% of the time, Pallas kernels for 0%

profile of v3, /device:TPU:262, one launch (start us, length us, event | category | flops | bytes accessed | tf_op | source)
XLA Modules:
  0.0 349.5 jit_solution(12098273690665486808)
XLA Ops:
  9.6 0.8 select_reduce_fusion
  12.6 1.8 reshape.364
  14.4 1.2 add_convert_fusion.1
  19.1 2.2 copy.36
  21.3 8.3 %all-to-all-start = ((bf16[32,2,64,128]{3,2,1,0:T(8,128)(2,1)}), bf16[32,2,64,128]{3,2,1,0:T(8,128)(2,1)}, u32[]{:S(2)}, u32[]{:S(2)}) async-start(bf16[32,2,64,128]{3,2,1,0:T(8,128)(2,1)} %copy.36), calls=%async_computation.1 | async-start | bytes 2097152 | tf_op jit(solution)/shard_map/all_to_all | solution.py:166
  30.0 1.0 broadcast_multiply_fusion
  31.7 3.4 collective-permute-start
  35.9 10.0 %collective-permute-start.1 = (bf16[1,4,64,128]{3,2,1,0:T(8,128)(2,1)}, bf16[1,4,64,128]{3,2,1,0:T(8,128)(2,1)}, u32[]{:S(2)}, u32[]{:S(2)}) collective-permute-start(bf16[1,4,64,128]{3,2,1,0:T(8,128)(2,1)} %bitcast.15), channel_id=1, source_target_pairs={{16,0},{32,16},{48,32},{64,48},{80,64},{96,80},{112,96},{128,112},... | collective-permute-start | bytes 196616 | tf_op jit(solution)/shard_map/ppermute | solution.py:66
  46.5 1.9 collective-permute-start.2
  48.4 14.5 %collective-permute-start.3 = (bf16[4,1,64,128]{3,2,1,0:T(8,128)(2,1)}, bf16[4,1,64,128]{3,2,1,0:T(8,128)(2,1)}, u32[]{:S(2)}, u32[]{:S(2)}) collective-permute-start(bf16[4,1,64,128]{3,2,1,0:T(8,128)(2,1)} %get-tuple-element.18), channel_id=1, source_target_pairs={{1,0},{2,1},{3,2},{4,3},{5,4},{6,5},{7,6},{8,7},{9,8},{10,9},{11,1... | collective-permute-start | bytes 196616 | tf_op jit(solution)/shard_map/ppermute | solution.py:68
  63.2 1.0 reshape.361
  65.0 0.8 fusion.102
  66.0 1.1 copy.31
  67.1 1.1 copy.30
  68.2 183.7 %reduce-scatter.2.cloned.1.call-done = f32[1,32,2]{2,1,0:T(8,128)} async-done(((f32[32,32,2]{2,1,0:T(8,128)}), f32[1,32,2]{2,1,0:T(8,128)}) %reduce-scatter.2.cloned.1.call-update) | async-done | bytes 272 | tf_op jit(solution)/shard_map/reduce_scatter | solution.py:113
  252.8 2.0 fusion.33
  254.7 1.8 fusion.37
  256.6 1.9 convolution_add_fusion.4
  258.5 2.0 fusion.14
  260.5 1.5 fusion.11
  261.9 0.8 gather_fusion.1
  263.9 2.2 copy.40
  266.1 29.4 %all-to-all-start.1 = ((bf16[32,2,64,128]{3,2,1,0:T(8,128)(2,1)}), bf16[32,2,64,128]{3,2,1,0:T(8,128)(2,1)}, u32[]{:S(2)}, u32[]{:S(2)}) async-start(bf16[32,2,64,128]{3,2,1,0:T(8,128)(2,1)} %copy.40), calls=%async_computation.2 | async-start | bytes 2097152 | tf_op jit(solution)/shard_map/all_to_all | solution.py:173
  296.3 1.9 collective-permute-start.6
  298.3 14.5 %collective-permute-start.7 = (bf16[4,1,64,128]{3,2,1,0:T(8,128)(2,1)S(1)}, bf16[4,1,64,128]{3,2,1,0:T(8,128)(2,1)S(1)}, u32[]{:S(2)}, u32[]{:S(2)}) collective-permute-start(bf16[4,1,64,128]{3,2,1,0:T(8,128)(2,1)S(1)} %get-tuple-element.10), channel_id=1, source_target_pairs={{1,0},{2,1},{3,2},{4,3},{5,4},{6,5},{7,6},{8,7},{9,8},{10,9},{11,1... | collective-permute-start | bytes 196616 | tf_op jit(solution)/shard_map/ppermute | solution.py:68
  313.4 10.2 %collective-permute-start.5 = (bf16[1,4,64,128]{3,2,1,0:T(8,128)(2,1)}, bf16[1,4,64,128]{3,2,1,0:T(8,128)(2,1)S(1)}, u32[]{:S(2)}, u32[]{:S(2)}) collective-permute-start(bf16[1,4,64,128]{3,2,1,0:T(8,128)(2,1)} %get-tuple-element.7), channel_id=1, source_target_pairs={{16,0},{32,16},{48,32},{64,48},{80,64},{96,80},{112,96},{128,112},... | collective-permute-start | bytes 196616 | tf_op jit(solution)/shard_map/ppermute | solution.py:66
  323.6 1.9 collective-permute-start.4
  327.0 1.0 fusion.51
  328.1 9.2 %collective-permute-done.4 = bf16[1,4,64,128]{3,2,1,0:T(8,128)(2,1)S(1)} collective-permute-done((bf16[1,4,64,128]{3,2,1,0:T(8,128)(2,1)S(1)}, bf16[1,4,64,128]{3,2,1,0:T(8,128)(2,1)S(1)}, u32[]{:S(2)}, u32[]{:S(2)}) %collective-permute-start.4) | collective-permute-done | bytes 65568 | tf_op jit(solution)/shard_map/ppermute | solution.py:65
  337.5 1.9 fusion.12
  339.5 1.4 fusion.5
  341.8 0.8 add_convert_fusion
  (101 shorter events, 18.4 us)
Async XLA Ops:
  8.7 8.6 %copy-start.9 = (s32[1024]{0:T(1024)}, s32[1024]{0:T(1024)S(1)}, u32[]{:S(2)}) copy-start(s32[1024]{0:T(1024)S(1)} %pad_clamp_fusion) | copy-start | bytes 12292
  14.4 2.0 copy-start.1
  21.3 8.5 %copy-start.13 = (s32[1,1,48]{2,1,0:T(1,128)S(1)}, s32[1,1,48]{2,1,0:T(1,128)}, u32[]{:S(2)}) copy-start(s32[1,1,48]{2,1,0:T(1,128)} %param.20) | copy-start | bytes 580
  21.3 237.1 %all-to-all-start = ((bf16[32,2,64,128]{3,2,1,0:T(8,128)(2,1)}), bf16[32,2,64,128]{3,2,1,0:T(8,128)(2,1)}, u32[]{:S(2)}, u32[]{:S(2)}) async-start(bf16[32,2,64,128]{3,2,1,0:T(8,128)(2,1)} %copy.36), calls=%async_computation.1 | async-start | bytes 2097152 | tf_op jit(solution)/shard_map/all_to_all | solution.py:166
  29.7 33.2 %copy-start.4 = (bf16[4,4,5,4096]{3,1,2,0:T(4,128)(2,1)S(1)}, bf16[4,4,5,4096]{3,1,2,0:T(4,128)(2,1)}, u32[]{:S(2)}) copy-start(bf16[4,4,5,4096]{3,1,2,0:T(4,128)(2,1)} %param.17) | copy-start | bytes 1966084
  29.7 222.2 %reduce-scatter.2.cloned.1.call-start = ((), (), s32[]{:S(2)}) async-start(), calls=%async_computation.3 | async-start | bytes 540672 | tf_op jit(solution)/shard_map/reduce_scatter | solution.py:113
  31.7 224.8 %collective-permute-start = (bf16[1,4,64,128]{3,2,1,0:T(8,128)(2,1)}, bf16[1,4,64,128]{3,2,1,0:T(8,128)(2,1)}, u32[]{:S(2)}, u32[]{:S(2)}) collective-permute-start(bf16[1,4,64,128]{3,2,1,0:T(8,128)(2,1)} %bitcast.11), channel_id=1, source_target_pairs={{0,16},{16,32},{32,48},{48,64},{64,80},{80,96},{96,112},{112,128},... | collective-permute-start | bytes 196616 | tf_op jit(solution)/shard_map/ppermute | solution.py:65
  35.9 224.6 %collective-permute-start.1 = (bf16[1,4,64,128]{3,2,1,0:T(8,128)(2,1)}, bf16[1,4,64,128]{3,2,1,0:T(8,128)(2,1)}, u32[]{:S(2)}, u32[]{:S(2)}) collective-permute-start(bf16[1,4,64,128]{3,2,1,0:T(8,128)(2,1)} %bitcast.15), channel_id=1, source_target_pairs={{16,0},{32,16},{48,32},{64,48},{80,64},{96,80},{112,96},{128,112},... | collective-permute-start | bytes 196616 | tf_op jit(solution)/shard_map/ppermute | solution.py:66
  46.5 206.3 %collective-permute-start.2 = (bf16[4,1,64,128]{3,2,1,0:T(8,128)(2,1)}, bf16[4,1,64,128]{3,2,1,0:T(8,128)(2,1)}, u32[]{:S(2)}, u32[]{:S(2)}) collective-permute-start(bf16[4,1,64,128]{3,2,1,0:T(8,128)(2,1)} %get-tuple-element.17), channel_id=1, source_target_pairs={{0,1},{1,2},{2,3},{3,4},{4,5},{5,6},{6,7},{7,8},{8,9},{9,10},{10,1... | collective-permute-start | bytes 196616 | tf_op jit(solution)/shard_map/ppermute | solution.py:67
  48.4 206.3 %collective-permute-start.3 = (bf16[4,1,64,128]{3,2,1,0:T(8,128)(2,1)}, bf16[4,1,64,128]{3,2,1,0:T(8,128)(2,1)}, u32[]{:S(2)}, u32[]{:S(2)}) collective-permute-start(bf16[4,1,64,128]{3,2,1,0:T(8,128)(2,1)} %get-tuple-element.18), channel_id=1, source_target_pairs={{1,0},{2,1},{3,2},{4,3},{5,4},{6,5},{7,6},{8,7},{9,8},{10,9},{11,1... | collective-permute-start | bytes 196616 | tf_op jit(solution)/shard_map/ppermute | solution.py:68
  66.0 192.5 %copy-start.7 = (s32[4,4]{1,0:T(4,128)}, s32[4,4]{1,0:T(4,128)S(1)}, u32[]{:S(2)}) copy-start(s32[4,4]{1,0:T(4,128)S(1)} %multiply_add_fusion) | copy-start | bytes 196
  252.8 5.7 %copy-start.10 = (s32[64]{0:T(128)}, s32[64]{0:T(128)S(1)}, u32[]{:S(2)}) copy-start(s32[64]{0:T(128)S(1)} %sub.19) | copy-start | bytes 772
  258.4 2.0 copy-start
  266.1 29.4 %copy-start.12 = (f32[32]{0:T(128)S(1)}, f32[32]{0:T(128)}, u32[]{:S(2)}) copy-start(f32[32]{0:T(128)} %param.23) | copy-start | bytes 388
  266.1 29.5 %copy-start.6 = (bf16[4,32,4,32]{3,2,1,0:T(4,128)(2,1)S(1)}, bf16[4,32,4,32]{3,2,1,0:T(4,128)(2,1)}, u32[]{:S(2)}) copy-start(bf16[4,32,4,32]{3,2,1,0:T(4,128)(2,1)} %get-tuple-element.35) | copy-start | bytes 98308
  266.1 29.7 %copy-start.5 = (bf16[4,32,4,32]{3,2,1,0:T(4,128)(2,1)S(1)}, bf16[4,32,4,32]{3,2,1,0:T(4,128)(2,1)}, u32[]{:S(2)}) copy-start(bf16[4,32,4,32]{3,2,1,0:T(4,128)(2,1)} %get-tuple-element.36) | copy-start | bytes 98308
  266.1 29.8 %copy-start.3 = (f32[4,32,4,32]{3,2,1,0:T(4,128)S(1)}, f32[4,32,4,32]{3,2,1,0:T(4,128)}, u32[]{:S(2)}) copy-start(f32[4,32,4,32]{3,2,1,0:T(4,128)} %get-tuple-element.34) | copy-start | bytes 196612
  266.1 71.4 %all-to-all-start.1 = ((bf16[32,2,64,128]{3,2,1,0:T(8,128)(2,1)}), bf16[32,2,64,128]{3,2,1,0:T(8,128)(2,1)}, u32[]{:S(2)}, u32[]{:S(2)}) async-start(bf16[32,2,64,128]{3,2,1,0:T(8,128)(2,1)} %copy.40), calls=%async_computation.2 | async-start | bytes 2097152 | tf_op jit(solution)/shard_map/all_to_all | solution.py:173
  296.3 30.5 %collective-permute-start.6 = (bf16[4,1,64,128]{3,2,1,0:T(8,128)(2,1)S(1)}, bf16[4,1,64,128]{3,2,1,0:T(8,128)(2,1)S(1)}, u32[]{:S(2)}, u32[]{:S(2)}) collective-permute-start(bf16[4,1,64,128]{3,2,1,0:T(8,128)(2,1)S(1)} %get-tuple-element.9), channel_id=1, source_target_pairs={{0,1},{1,2},{2,3},{3,4},{4,5},{5,6},{6,7},{7,8},{8,9},{9,10},{10,1... | collective-permute-start | bytes 196616 | tf_op jit(solution)/shard_map/ppermute | solution.py:67
  298.3 28.8 %collective-permute-start.7 = (bf16[4,1,64,128]{3,2,1,0:T(8,128)(2,1)S(1)}, bf16[4,1,64,128]{3,2,1,0:T(8,128)(2,1)S(1)}, u32[]{:S(2)}, u32[]{:S(2)}) collective-permute-start(bf16[4,1,64,128]{3,2,1,0:T(8,128)(2,1)S(1)} %get-tuple-element.10), channel_id=1, source_target_pairs={{1,0},{2,1},{3,2},{4,3},{5,4},{6,5},{7,6},{8,7},{9,8},{10,9},{11,1... | collective-permute-start | bytes 196616 | tf_op jit(solution)/shard_map/ppermute | solution.py:68
  313.4 26.1 %collective-permute-start.5 = (bf16[1,4,64,128]{3,2,1,0:T(8,128)(2,1)}, bf16[1,4,64,128]{3,2,1,0:T(8,128)(2,1)S(1)}, u32[]{:S(2)}, u32[]{:S(2)}) collective-permute-start(bf16[1,4,64,128]{3,2,1,0:T(8,128)(2,1)} %get-tuple-element.7), channel_id=1, source_target_pairs={{16,0},{32,16},{48,32},{64,48},{80,64},{96,80},{112,96},{128,112},... | collective-permute-start | bytes 196616 | tf_op jit(solution)/shard_map/ppermute | solution.py:66
  323.6 13.7 %collective-permute-start.4 = (bf16[1,4,64,128]{3,2,1,0:T(8,128)(2,1)S(1)}, bf16[1,4,64,128]{3,2,1,0:T(8,128)(2,1)S(1)}, u32[]{:S(2)}, u32[]{:S(2)}) collective-permute-start(bf16[1,4,64,128]{3,2,1,0:T(8,128)(2,1)S(1)} %get-tuple-element.8), channel_id=1, source_target_pairs={{0,16},{16,32},{32,48},{48,64},{64,80},{80,96},{96,112},{112,128},... | collective-permute-start | bytes 196616 | tf_op jit(solution)/shard_map/ppermute | solution.py:65
  327.0 10.5 %copy-start.8 = (s32[4,4]{1,0:T(4,128)S(1)}, s32[4,4]{1,0:T(4,128)}, u32[]{:S(2)}) copy-start(s32[4,4]{1,0:T(4,128)} %copy-done.7) | copy-start | bytes 196
  327.0 10.5 %copy-start.11 = (s32[64]{0:T(128)S(1)}, s32[64]{0:T(128)}, u32[]{:S(2)}) copy-start(s32[64]{0:T(128)} %copy-done.10) | copy-start | bytes 772
  340.9 1.0 copy-start.2
Sparse Core Ops, SparseCore 0:
  33.3 218.5 reduce-scatter.1

commit v4 on v3

--- a/solution.py
+++ b/solution.py
@@ -111,18 +111,17 @@
     owner = (jnp.arange(n_rx, dtype=jnp.int32) == me).astype(jnp.float32)
     table = mine * owner[None, :, None]
     found = lax.psum_scatter(table, "rx", scatter_dimension=0, tiled=True)
-    return found.reshape(-1).astype(jnp.int32) - 1
-
-
-def send_products(signal, edge_tiles, sources, select):
+    return found.reshape(-1).astype(jnp.int32) - 1, jnp.sum(found) * 0.0
+
+
+def send_products(signal, edge_tiles, sources, select, guard):
     block_rows, block_cols, block_size, features = signal.shape
     flat = signal.reshape(block_rows * block_cols, block_size, features)
     products = jnp.einsum(
         "eab,ebf->eaf", edge_tiles, flat[sources], preferred_element_type=jnp.float32
     ).astype(jnp.bfloat16)
-    slots = jnp.einsum(
-        "es,eaf->saf", select, products, preferred_element_type=jnp.float32
-    ).astype(jnp.bfloat16)
+    slots = jnp.einsum("es,eaf->saf", select, products, preferred_element_type=jnp.float32)
+    slots = (slots + guard).astype(jnp.bfloat16)
     return slots.reshape(lax.axis_size("rx"), CAP, block_size, features)
 
 
@@ -159,16 +158,16 @@
     select = edge_select(out_dev, n_rx)
     sources = out_block.reshape(-1)
     edge_tiles = out_tiles.reshape(-1, block_size, block_size)
-    targets = slot_targets(select, out_target, n_rx)
-
-    send_one = send_products(gated, edge_tiles, sources, select)
+    targets, guard = slot_targets(select, out_target, n_rx)
+
+    send_one = send_products(gated, edge_tiles, sources, select, guard)
     halo_one = fetch_halo(gated)
     recv_one = lax.all_to_all(send_one, "rx", split_axis=0, concat_axis=0, tiled=True)
     near_one = local_terms(gated, tiles, halo_one)
     far_one = far_terms(recv_one, targets, nblocks)
     first_hop = (near_one + far_one.reshape(gated.shape)).astype(jnp.bfloat16)
 
-    send_two = send_products(first_hop, edge_tiles, sources, select)
+    send_two = send_products(first_hop, edge_tiles, sources, select, 0.0)
     halo_two = fetch_halo(first_hop)
     recv_two = lax.all_to_all(send_two, "rx", split_axis=0, concat_axis=0, tiled=True)
     near_two = local_terms(first_hop, tiles, halo_two)

time: 351 us -> 383 us (1.091)
  the two profiles are of different devices: /device:TPU:262 before, /device:TPU:57 now
where the time goes in v4:
time: 383 us; the launch traced here: 382 us
  waiting for transfers between devices  240 us (63%)
  starting transfers between devices  84.3 us (22%)
  matrix products  19 us (5%)
  local copies, waits for them, and re-layouts  15.5 us (4%)
  between operations  14.6 us (4%)
  other arithmetic  8.39 us (2%)
    reduce_scatter x1, waiting for transfers between devices, slot_targets(): found = lax.psum_scatter(table, 'rx', scatter_dimension=0, tiled=True)  205 us
    ppermute x2, starting transfers between devices, fetch_halo(): left = lax.ppermute(signal[:, -1:], 'ry', shift_pairs(n_ry, 1))  43.5 us
    all_to_all x1, waiting for transfers between devices, local(): lax.all_to_all(send_two, 'rx', split_axis=0, concat_axis=0, tiled=True)  19.1 us
    ppermute x2, waiting for transfers between devices, fetch_halo(): right = lax.ppermute(signal[:, :1], 'ry', shift_pairs(n_ry, -1))  16.2 us
    all_to_all x1, starting transfers between devices, local(): lax.all_to_all(send_one, 'rx', split_axis=0, concat_axis=0, tiled=True)  13.7 us
    all_to_all x1, starting transfers between devices, local(): lax.all_to_all(send_two, 'rx', split_axis=0, concat_axis=0, tiled=True)  12 us
    dot_general x8, matrix products, local_terms(): jnp.einsum('ijab,ijbf->ijaf', tiles[:, :, offset], neighbours[offset], pr...  10.1 us
  transfers between devices with their start and end apart: 11, of which 4 were waited for; matrix products, arithmetic and copies ran while one was open for 7% of the time, Pallas kernels for 0%

profile of v4, /device:TPU:57, one launch (start us, length us, event | category | flops | bytes accessed | tf_op | source)
XLA Modules:
  0.0 381.7 jit_solution(12523011906747799252)
XLA Ops:
  7.6 0.8 select_reduce_fusion
  9.3 0.9 broadcast_multiply_fusion
  11.9 0.8 reshape.364
  12.8 1.2 add_convert_fusion.2
  16.8 204.6 %reduce-scatter.2.cloned.1.call-done = f32[1,32,2]{2,1,0:T(8,128)} async-done(((f32[32,32,2]{2,1,0:T(8,128)}), f32[1,32,2]{2,1,0:T(8,128)}) %reduce-scatter.2.cloned.1.call-update) | async-done | bytes 272 | tf_op jit(solution)/shard_map/reduce_scatter | solution.py:113
  221.4 1.4 reduce_sum.19
  224.1 2.2 copy.36
  226.3 13.7 %all-to-all-start = ((bf16[32,2,64,128]{3,2,1,0:T(8,128)(2,1)}), bf16[32,2,64,128]{3,2,1,0:T(8,128)(2,1)}, u32[]{:S(2)}, u32[]{:S(2)}) async-start(bf16[32,2,64,128]{3,2,1,0:T(8,128)(2,1)} %copy.36), calls=%async_computation.1 | async-start | bytes 2097152 | tf_op jit(solution)/shard_map/all_to_all | solution.py:165
  240.8 3.1 collective-permute-start
  244.6 2.8 collective-permute-start.1
  248.1 37.2 %collective-permute-start.2 = (bf16[4,1,64,128]{3,2,1,0:T(8,128)(2,1)}, bf16[4,1,64,128]{3,2,1,0:T(8,128)(2,1)}, u32[]{:S(2)}, u32[]{:S(2)}) collective-permute-start(bf16[4,1,64,128]{3,2,1,0:T(8,128)(2,1)} %get-tuple-element.17), channel_id=1, source_target_pairs={{0,1},{1,2},{2,3},{3,4},{4,5},{5,6},{6,7},{7,8},{8,9},{9,10},{10,1... | collective-permute-start | bytes 196616 | tf_op jit(solution)/shard_map/ppermute | solution.py:67
  285.3 1.9 collective-permute-start.3
  287.6 1.0 reshape.361
  289.5 0.8 fusion.105
  291.4 2.0 fusion.33
  293.4 8.6 %collective-permute-done.3 = bf16[4,1,64,128]{3,2,1,0:T(8,128)(2,1)} collective-permute-done((bf16[4,1,64,128]{3,2,1,0:T(8,128)(2,1)}, bf16[4,1,64,128]{3,2,1,0:T(8,128)(2,1)}, u32[]{:S(2)}, u32[]{:S(2)}) %collective-permute-start.3) | collective-permute-done | bytes 65568 | tf_op jit(solution)/shard_map/ppermute | solution.py:68
  302.0 2.0 fusion.37
  304.0 1.9 convolution_add_fusion.4
  305.9 2.0 fusion.14
  307.9 1.5 fusion.11
  309.3 0.8 gather_fusion.1
  311.3 2.2 copy.40
  313.5 12.0 %all-to-all-start.1 = ((bf16[32,2,64,128]{3,2,1,0:T(8,128)(2,1)}), bf16[32,2,64,128]{3,2,1,0:T(8,128)(2,1)}, u32[]{:S(2)}, u32[]{:S(2)}) async-start(bf16[32,2,64,128]{3,2,1,0:T(8,128)(2,1)} %copy.40), calls=%async_computation.2 | async-start | bytes 2097152 | tf_op jit(solution)/shard_map/all_to_all | solution.py:172
  326.3 6.3 %collective-permute-start.6 = (bf16[4,1,64,128]{3,2,1,0:T(8,128)(2,1)S(1)}, bf16[4,1,64,128]{3,2,1,0:T(8,128)(2,1)S(1)}, u32[]{:S(2)}, u32[]{:S(2)}) collective-permute-start(bf16[4,1,64,128]{3,2,1,0:T(8,128)(2,1)S(1)} %get-tuple-element.9), channel_id=1, source_target_pairs={{0,1},{1,2},{2,3},{3,4},{4,5},{5,6},{6,7},{7,8},{8,9},{9,10},{10,1... | collective-permute-start | bytes 196616 | tf_op jit(solution)/shard_map/ppermute | solution.py:67
  332.7 1.9 collective-permute-start.7
  335.2 1.9 collective-permute-start.5
  337.1 3.3 collective-permute-start.4
  341.9 7.5 %collective-permute-done.7 = bf16[4,1,64,128]{3,2,1,0:T(8,128)(2,1)S(1)} collective-permute-done((bf16[4,1,64,128]{3,2,1,0:T(8,128)(2,1)S(1)}, bf16[4,1,64,128]{3,2,1,0:T(8,128)(2,1)S(1)}, u32[]{:S(2)}, u32[]{:S(2)}) %collective-permute-start.7) | collective-permute-done | bytes 65568 | tf_op jit(solution)/shard_map/ppermute | solution.py:68
  349.5 1.0 fusion.51
  350.7 19.1 %all-to-all-done.1 = bf16[32,2,64,128]{3,2,1,0:T(8,128)(2,1)} async-done(((bf16[32,2,64,128]{3,2,1,0:T(8,128)(2,1)}), bf16[32,2,64,128]{3,2,1,0:T(8,128)(2,1)}, u32[]{:S(2)}, u32[]{:S(2)}) %all-to-all-start.1) | async-done | bytes 1048608 | tf_op jit(solution)/shard_map/all_to_all | solution.py:172
  369.8 1.9 fusion.12
  371.8 1.4 fusion.5
  (110 shorter events, 17.2 us)
Async XLA Ops:
  6.5 5.2 %copy-start.16 = (f32[32]{0:T(128)S(1)}, f32[32]{0:T(128)}, u32[]{:S(2)}) copy-start(f32[32]{0:T(128)} %param.16) | copy-start | bytes 388
  6.5 5.3 %copy-start.11 = (bf16[2,32,32]{2,1,0:T(8,128)(2,1)S(1)}, bf16[2,32,32]{2,1,0:T(8,128)(2,1)}, u32[]{:S(2)}) copy-start(bf16[2,32,32]{2,1,0:T(8,128)(2,1)} %param.13) | copy-start | bytes 12292
  6.5 5.3 %copy-start.12 = (bf16[2,32,32]{2,1,0:T(8,128)(2,1)S(1)}, bf16[2,32,32]{2,1,0:T(8,128)(2,1)}, u32[]{:S(2)}) copy-start(bf16[2,32,32]{2,1,0:T(8,128)(2,1)} %param.14) | copy-start | bytes 12292
  6.5 5.4 %copy-start.8 = (bf16[3,32,32]{2,1,0:T(8,128)(2,1)S(1)}, bf16[3,32,32]{2,1,0:T(8,128)(2,1)}, u32[]{:S(2)}) copy-start(bf16[3,32,32]{2,1,0:T(8,128)(2,1)} %param.22) | copy-start | bytes 18436
  6.5 5.4 %copy-start.7 = (bf16[1,1,48,4096]{3,2,1,0:T(8,128)(2,1)S(1)}, bf16[1,1,48,4096]{3,2,1,0:T(8,128)(2,1)}, u32[]{:S(2)}) copy-start(bf16[1,1,48,4096]{3,2,1,0:T(8,128)(2,1)} %param.21) | copy-start | bytes 1179652
  6.5 214.8 %reduce-scatter.2.cloned.1.call-start = ((), (), s32[]{:S(2)}) async-start(), calls=%async_computation.3 | async-start | bytes 540672 | tf_op jit(solution)/shard_map/reduce_scatter | solution.py:113
  11.8 3.8 %copy-start.13 = (s32[1024]{0:T(1024)}, s32[1024]{0:T(1024)S(1)}, u32[]{:S(2)}) copy-start(s32[1024]{0:T(1024)S(1)} %pad_clamp_fusion) | copy-start | bytes 12292
  12.8 2.0 copy-start.1
  226.3 60.9 %copy-start.4 = (bf16[4,4,5,4096]{3,1,2,0:T(4,128)(2,1)S(1)}, bf16[4,4,5,4096]{3,1,2,0:T(4,128)(2,1)}, u32[]{:S(2)}) copy-start(bf16[4,4,5,4096]{3,1,2,0:T(4,128)(2,1)} %param.17) | copy-start | bytes 1966084
  226.3 79.5 %all-to-all-start = ((bf16[32,2,64,128]{3,2,1,0:T(8,128)(2,1)}), bf16[32,2,64,128]{3,2,1,0:T(8,128)(2,1)}, u32[]{:S(2)}, u32[]{:S(2)}) async-start(bf16[32,2,64,128]{3,2,1,0:T(8,128)(2,1)} %copy.36), calls=%async_computation.1 | async-start | bytes 2097152 | tf_op jit(solution)/shard_map/all_to_all | solution.py:165
  240.8 63.2 %collective-permute-start = (bf16[1,4,64,128]{3,2,1,0:T(8,128)(2,1)}, bf16[1,4,64,128]{3,2,1,0:T(8,128)(2,1)}, u32[]{:S(2)}, u32[]{:S(2)}) collective-permute-start(bf16[1,4,64,128]{3,2,1,0:T(8,128)(2,1)} %bitcast.11), channel_id=1, source_target_pairs={{0,16},{16,32},{32,48},{48,64},{64,80},{80,96},{96,112},{112,128},... | collective-permute-start | bytes 196616 | tf_op jit(solution)/shard_map/ppermute | solution.py:65
  244.6 63.2 %collective-permute-start.1 = (bf16[1,4,64,128]{3,2,1,0:T(8,128)(2,1)}, bf16[1,4,64,128]{3,2,1,0:T(8,128)(2,1)}, u32[]{:S(2)}, u32[]{:S(2)}) collective-permute-start(bf16[1,4,64,128]{3,2,1,0:T(8,128)(2,1)} %bitcast.15), channel_id=1, source_target_pairs={{16,0},{32,16},{48,32},{64,48},{80,64},{96,80},{112,96},{128,112},... | collective-permute-start | bytes 196616 | tf_op jit(solution)/shard_map/ppermute | solution.py:66
  248.1 43.4 %collective-permute-start.2 = (bf16[4,1,64,128]{3,2,1,0:T(8,128)(2,1)}, bf16[4,1,64,128]{3,2,1,0:T(8,128)(2,1)}, u32[]{:S(2)}, u32[]{:S(2)}) collective-permute-start(bf16[4,1,64,128]{3,2,1,0:T(8,128)(2,1)} %get-tuple-element.17), channel_id=1, source_target_pairs={{0,1},{1,2},{2,3},{3,4},{4,5},{5,6},{6,7},{7,8},{8,9},{9,10},{10,1... | collective-permute-start | bytes 196616 | tf_op jit(solution)/shard_map/ppermute | solution.py:67
  285.3 16.7 %collective-permute-start.3 = (bf16[4,1,64,128]{3,2,1,0:T(8,128)(2,1)}, bf16[4,1,64,128]{3,2,1,0:T(8,128)(2,1)}, u32[]{:S(2)}, u32[]{:S(2)}) collective-permute-start(bf16[4,1,64,128]{3,2,1,0:T(8,128)(2,1)} %get-tuple-element.18), channel_id=1, source_target_pairs={{1,0},{2,1},{3,2},{4,3},{5,4},{6,5},{7,6},{8,7},{9,8},{10,9},{11,1... | collective-permute-start | bytes 196616 | tf_op jit(solution)/shard_map/ppermute | solution.py:68
  291.4 14.4 %copy-start.14 = (s32[64]{0:T(128)}, s32[64]{0:T(128)S(1)}, u32[]{:S(2)}) copy-start(s32[64]{0:T(128)S(1)} %sub.19) | copy-start | bytes 772
  302.0 3.8 %copy-start.9 = (s32[4,4]{1,0:T(4,128)S(1)}, s32[4,4]{1,0:T(4,128)}, u32[]{:S(2)}) copy-start(s32[4,4]{1,0:T(4,128)} %multiply_add_fusion) | copy-start | bytes 196
  305.8 2.0 copy-start
  313.5 12.0 %copy-start.17 = (f32[32]{0:T(128)S(1)}, f32[32]{0:T(128)}, u32[]{:S(2)}) copy-start(f32[32]{0:T(128)} %param.23) | copy-start | bytes 388
  313.5 12.1 %copy-start.6 = (bf16[4,32,4,32]{3,2,1,0:T(4,128)(2,1)S(1)}, bf16[4,32,4,32]{3,2,1,0:T(4,128)(2,1)}, u32[]{:S(2)}) copy-start(bf16[4,32,4,32]{3,2,1,0:T(4,128)(2,1)} %get-tuple-element.35) | copy-start | bytes 98308
  313.5 12.3 %copy-start.5 = (bf16[4,32,4,32]{3,2,1,0:T(4,128)(2,1)S(1)}, bf16[4,32,4,32]{3,2,1,0:T(4,128)(2,1)}, u32[]{:S(2)}) copy-start(bf16[4,32,4,32]{3,2,1,0:T(4,128)(2,1)} %get-tuple-element.36) | copy-start | bytes 98308
  313.5 12.4 %copy-start.3 = (f32[4,32,4,32]{3,2,1,0:T(4,128)S(1)}, f32[4,32,4,32]{3,2,1,0:T(4,128)}, u32[]{:S(2)}) copy-start(f32[4,32,4,32]{3,2,1,0:T(4,128)} %get-tuple-element.34) | copy-start | bytes 196612
  313.5 56.3 %all-to-all-start.1 = ((bf16[32,2,64,128]{3,2,1,0:T(8,128)(2,1)}), bf16[32,2,64,128]{3,2,1,0:T(8,128)(2,1)}, u32[]{:S(2)}, u32[]{:S(2)}) async-start(bf16[32,2,64,128]{3,2,1,0:T(8,128)(2,1)} %copy.40), calls=%async_computation.2 | async-start | bytes 2097152 | tf_op jit(solution)/shard_map/all_to_all | solution.py:172
  326.3 15.4 %collective-permute-start.6 = (bf16[4,1,64,128]{3,2,1,0:T(8,128)(2,1)S(1)}, bf16[4,1,64,128]{3,2,1,0:T(8,128)(2,1)S(1)}, u32[]{:S(2)}, u32[]{:S(2)}) collective-permute-start(bf16[4,1,64,128]{3,2,1,0:T(8,128)(2,1)S(1)} %get-tuple-element.9), channel_id=1, source_target_pairs={{0,1},{1,2},{2,3},{3,4},{4,5},{5,6},{6,7},{7,8},{8,9},{9,10},{10,1... | collective-permute-start | bytes 196616 | tf_op jit(solution)/shard_map/ppermute | solution.py:67
  332.7 16.8 %collective-permute-start.7 = (bf16[4,1,64,128]{3,2,1,0:T(8,128)(2,1)S(1)}, bf16[4,1,64,128]{3,2,1,0:T(8,128)(2,1)S(1)}, u32[]{:S(2)}, u32[]{:S(2)}) collective-permute-start(bf16[4,1,64,128]{3,2,1,0:T(8,128)(2,1)S(1)} %get-tuple-element.10), channel_id=1, source_target_pairs={{1,0},{2,1},{3,2},{4,3},{5,4},{6,5},{7,6},{8,7},{9,8},{10,9},{11,1... | collective-permute-start | bytes 196616 | tf_op jit(solution)/shard_map/ppermute | solution.py:68
  335.2 36.6 %collective-permute-start.5 = (bf16[1,4,64,128]{3,2,1,0:T(8,128)(2,1)}, bf16[1,4,64,128]{3,2,1,0:T(8,128)(2,1)S(1)}, u32[]{:S(2)}, u32[]{:S(2)}) collective-permute-start(bf16[1,4,64,128]{3,2,1,0:T(8,128)(2,1)} %get-tuple-element.7), channel_id=1, source_target_pairs={{16,0},{32,16},{48,32},{64,48},{80,64},{96,80},{112,96},{128,112},... | collective-permute-start | bytes 196616 | tf_op jit(solution)/shard_map/ppermute | solution.py:66
  337.1 13.4 %collective-permute-start.4 = (bf16[1,4,64,128]{3,2,1,0:T(8,128)(2,1)S(1)}, bf16[1,4,64,128]{3,2,1,0:T(8,128)(2,1)S(1)}, u32[]{:S(2)}, u32[]{:S(2)}) collective-permute-start(bf16[1,4,64,128]{3,2,1,0:T(8,128)(2,1)S(1)} %get-tuple-element.8), channel_id=1, source_target_pairs={{0,16},{16,32},{32,48},{48,64},{64,80},{80,96},{96,112},{112,128},... | collective-permute-start | bytes 196616 | tf_op jit(solution)/shard_map/ppermute | solution.py:65
  349.5 20.3 %copy-start.10 = (s32[4,4]{1,0:T(4,128)S(1)}, s32[4,4]{1,0:T(4,128)}, u32[]{:S(2)}) copy-start(s32[4,4]{1,0:T(4,128)} %multiply_add_fusion) | copy-start | bytes 196
  349.5 20.3 %copy-start.15 = (s32[64]{0:T(128)S(1)}, s32[64]{0:T(128)}, u32[]{:S(2)}) copy-start(s32[64]{0:T(128)} %copy-done.14) | copy-start | bytes 772
  373.2 1.0 copy-start.2
Sparse Core Ops, SparseCore 0:
  10.4 210.9 reduce-scatter.1

commit v5 on v3

--- a/solution.py
+++ b/solution.py
@@ -103,27 +103,19 @@
     return select.reshape(select.shape[0], -1).astype(jnp.bfloat16)
 
 
-def slot_targets(select, out_target, n_rx):
-    me = lax.axis_index("rx")
-    mine = jnp.einsum(
-        "es,e->s", select.astype(jnp.float32), (out_target.reshape(-1) + 1).astype(jnp.float32)
-    ).reshape(n_rx, 1, CAP)
-    owner = (jnp.arange(n_rx, dtype=jnp.int32) == me).astype(jnp.float32)
-    table = mine * owner[None, :, None]
-    found = lax.psum_scatter(table, "rx", scatter_dimension=0, tiled=True)
-    return found.reshape(-1).astype(jnp.int32) - 1
-
-
-def send_products(signal, edge_tiles, sources, select):
+def send_products(signal, edge_tiles, sources, select, target_col=None):
     block_rows, block_cols, block_size, features = signal.shape
     flat = signal.reshape(block_rows * block_cols, block_size, features)
     products = jnp.einsum(
         "eab,ebf->eaf", edge_tiles, flat[sources], preferred_element_type=jnp.float32
     ).astype(jnp.bfloat16)
+    products = products.reshape(products.shape[0], -1)
+    if target_col is not None:
+        products = jnp.concatenate([products, target_col], axis=1)
     slots = jnp.einsum(
-        "es,eaf->saf", select, products, preferred_element_type=jnp.float32
+        "es,ek->sk", select, products, preferred_element_type=jnp.float32
     ).astype(jnp.bfloat16)
-    return slots.reshape(lax.axis_size("rx"), CAP, block_size, features)
+    return slots.reshape(lax.axis_size("rx"), CAP, -1)
 
 
 def far_terms(received, targets, nblocks):
@@ -159,11 +151,18 @@
     select = edge_select(out_dev, n_rx)
     sources = out_block.reshape(-1)
     edge_tiles = out_tiles.reshape(-1, block_size, block_size)
-    targets = slot_targets(select, out_target, n_rx)
-
-    send_one = send_products(gated, edge_tiles, sources, select)
+    edge_count = sources.shape[0]
+    block_len = block_size * features
+    target_col = jnp.zeros((edge_count, 128), jnp.bfloat16).at[:, 0].set(
+        (out_target.reshape(-1) + 1).astype(jnp.bfloat16)
+    )
+
+    send_one = send_products(gated, edge_tiles, sources, select, target_col)
     halo_one = fetch_halo(gated)
     recv_one = lax.all_to_all(send_one, "rx", split_axis=0, concat_axis=0, tiled=True)
+    recv_one = recv_one.reshape(n_rx * CAP, -1)
+    targets = recv_one[:, block_len].astype(jnp.int32) - 1
+    recv_one = recv_one[:, :block_len]
     near_one = local_terms(gated, tiles, halo_one)
     far_one = far_terms(recv_one, targets, nblocks)
     first_hop = (near_one + far_one.reshape(gated.shape)).astype(jnp.bfloat16)

time: 351 us -> 162 us (0.46)
  the two profiles are of different devices: /device:TPU:262 before, /device:TPU:57 now
where the time goes in v5:
time: 162 us; the launch traced here: 161 us
  starting transfers between devices  62.5 us (39%)
  waiting for transfers between devices  54.7 us (34%)
  local copies, waits for them, and re-layouts  21.8 us (13%)
  matrix products  15.4 us (10%)
  other arithmetic  6.13 us (4%)
    ppermute x2, starting transfers between devices, fetch_halo(): left = lax.ppermute(signal[:, -1:], 'ry', shift_pairs(n_ry, 1))  19.8 us
    all_to_all x1, waiting for transfers between devices, local(): lax.all_to_all(send_two, 'rx', split_axis=0, concat_axis=0, tiled=True)  19.6 us
    all_to_all x1, waiting for transfers between devices, local(): lax.all_to_all(send_one, 'rx', split_axis=0, concat_axis=0, tiled=True)  15.6 us
    all_to_all x1, starting transfers between devices, local(): lax.all_to_all(send_one, 'rx', split_axis=0, concat_axis=0, tiled=True)  14.9 us
    ppermute x2, waiting for transfers between devices, fetch_halo(): right = lax.ppermute(signal[:, :1], 'ry', shift_pairs(n_ry, -1))  14.5 us
    all_to_all x1, starting transfers between devices, local(): lax.all_to_all(send_two, 'rx', split_axis=0, concat_axis=0, tiled=True)  12.8 us
    dot_general x8, matrix products, local_terms(): jnp.einsum('ijab,ijbf->ijaf', tiles[:, :, offset], neighbours[offset], pr...  9.08 us
    ppermute x2, starting transfers between devices, fetch_halo(): above = lax.ppermute(signal[-1:], 'rx', shift_pairs(n_rx, 1))  6.17 us
  transfers between devices with their start and end apart: 10, of which 6 were waited for; matrix products, arithmetic and copies ran while one was open for 13% of the time, Pallas kernels for 0%

profile of v5, /device:TPU:57, one launch (start us, length us, event | category | flops | bytes accessed | tf_op | source)
XLA Modules:
  0.0 161.0 jit_solution(4003770162902876284)
XLA Ops:
  2.9 1.2 add_convert_fusion.1
  6.5 0.8 reshape.399
  10.6 1.2 reshape.402
  11.8 14.9 %all-to-all-start = ((bf16[32,2,8320]{2,1,0:T(2,128)(2,1)}), bf16[32,2,8320]{2,1,0:T(2,128)(2,1)}, u32[]{:S(2)}, u32[]{:S(2)}) async-start(bf16[32,2,8320]{2,1,0:T(2,128)(2,1)} %reshape.402), calls=%async_computation | async-start | bytes 2129920 | tf_op jit(solution)/shard_map/all_to_all | solution.py:162
  27.4 3.1 %collective-permute-start = (bf16[1,4,64,128]{3,2,1,0:T(8,128)(2,1)}, bf16[1,4,64,128]{3,2,1,0:T(8,128)(2,1)}, u32[]{:S(2)}, u32[]{:S(2)}) collective-permute-start(bf16[1,4,64,128]{3,2,1,0:T(8,128)(2,1)} %bitcast.11), channel_id=1, source_target_pairs={{0,16},{16,32},{32,48},{48,64},{64,80},{80,96},{96,112},{112,128},... | collective-permute-start | bytes 196616 | tf_op jit(solution)/shard_map/ppermute | solution.py:65
  31.2 9.0 %collective-permute-start.2 = (bf16[4,1,64,128]{3,2,1,0:T(8,128)(2,1)}, bf16[4,1,64,128]{3,2,1,0:T(8,128)(2,1)}, u32[]{:S(2)}, u32[]{:S(2)}) collective-permute-start(bf16[4,1,64,128]{3,2,1,0:T(8,128)(2,1)} %get-tuple-element.29), channel_id=1, source_target_pairs={{0,1},{1,2},{2,3},{3,4},{4,5},{5,6},{6,7},{7,8},{8,9},{9,10},{10,1... | collective-permute-start | bytes 196616 | tf_op jit(solution)/shard_map/ppermute | solution.py:67
  40.2 1.9 %collective-permute-start.3 = (bf16[4,1,64,128]{3,2,1,0:T(8,128)(2,1)}, bf16[4,1,64,128]{3,2,1,0:T(8,128)(2,1)}, u32[]{:S(2)}, u32[]{:S(2)}) collective-permute-start(bf16[4,1,64,128]{3,2,1,0:T(8,128)(2,1)} %get-tuple-element.30), channel_id=1, source_target_pairs={{1,0},{2,1},{3,2},{4,3},{5,4},{6,5},{7,6},{8,7},{9,8},{10,9},{11,1... | collective-permute-start | bytes 196616 | tf_op jit(solution)/shard_map/ppermute | solution.py:68
  42.8 2.8 %collective-permute-start.1 = (bf16[1,4,64,128]{3,2,1,0:T(8,128)(2,1)}, bf16[1,4,64,128]{3,2,1,0:T(8,128)(2,1)}, u32[]{:S(2)}, u32[]{:S(2)}) collective-permute-start(bf16[1,4,64,128]{3,2,1,0:T(8,128)(2,1)} %bitcast.15), channel_id=1, source_target_pairs={{16,0},{32,16},{48,32},{64,48},{80,64},{96,80},{112,96},{128,112},... | collective-permute-start | bytes 196616 | tf_op jit(solution)/shard_map/ppermute | solution.py:66
  45.9 1.0 reshape.397
  48.0 1.1 copy.43
  49.1 1.7 %copy.44 = bf16[768,1,128]{2,0,1:T(8,128)(2,1)} copy(bf16[768,1,128]{0,2,1:T(8,128)(2,1)} %get-tuple-element.25) | data formatting | bytes 393216 | tf_op jit(solution)/shard_map/slice | solution.py:77
  50.9 1.9 %fusion.37 = f32[4,4,128,64]{2,3,1,0:T(8,128)} fusion(bf16[4,3,64,128]{3,2,1,0:T(8,128)(2,1)S(1)} %get-tuple-element.31, bf16[4,1,64,128]{3,2,1,0:T(8,128)(2,1)} %collective-permute-done.2, bf16[4,4,5,64,64]{4,3,1,0,2:T(8,128)(2,1)S(1)} %reshape.397), kind=kOutput, calls=%fused_computation.61 | convolution fusion | flops 17301504 | bytes 1048576 | tf_op jit(solution)/shard_map/ijab,ijbf->ijaf/dot_general | solution.py:85
  52.7 4.5 %collective-permute-done.3 = bf16[4,1,64,128]{3,2,1,0:T(8,128)(2,1)} collective-permute-done((bf16[4,1,64,128]{3,2,1,0:T(8,128)(2,1)}, bf16[4,1,64,128]{3,2,1,0:T(8,128)(2,1)}, u32[]{:S(2)}, u32[]{:S(2)}) %collective-permute-start.3) | collective-permute-done | bytes 65568 | tf_op jit(solution)/shard_map/ppermute | solution.py:68
  57.2 1.8 %fusion.41 = f32[4,4,128,64]{2,3,1,0:T(8,128)} fusion(bf16[4,1,64,128]{3,2,1,0:T(8,128)(2,1)} %collective-permute-done.3, bf16[4,3,64,128]{3,2,1,0:T(8,128)(2,1)S(1)} %get-tuple-element.32, bf16[4,4,5,64,64]{4,3,1,0,2:T(8,128)(2,1)S(1)} %reshape.397), kind=kOutput, calls=%fused_computation.65 | convolution fusion | flops 17301504 | bytes 1048576 | tf_op jit(solution)/shard_map/ijab,ijbf->ijaf/dot_general | solution.py:85
  59.0 4.5 %collective-permute-done = bf16[1,4,64,128]{3,2,1,0:T(8,128)(2,1)} collective-permute-done((bf16[1,4,64,128]{3,2,1,0:T(8,128)(2,1)}, bf16[1,4,64,128]{3,2,1,0:T(8,128)(2,1)}, u32[]{:S(2)}, u32[]{:S(2)}) %collective-permute-start) | collective-permute-done | bytes 65568 | tf_op jit(solution)/shard_map/ppermute | solution.py:65
  63.6 1.8 %convolution_add_fusion.4 = f32[4,4,128,64]{2,3,1,0:T(8,128)} fusion(f32[4,4,128,64]{2,3,1,0:T(8,128)S(1)} %fusion.61, bf16[3,4,64,128]{3,2,1,0:T(8,128)(2,1)S(1)} %bitcast.135, bf16[1,4,64,128]{3,2,1,0:T(8,128)(2,1)} %collective-permute-done, bf16[4,4,5,64,64]{4,3,1,0,2:T(8,128)(2,1)S(1)} %reshape.397), kind=kOutput, calls=%fused_computation.24 | convolution fusion | flops 17432576 | bytes 1572864 | tf_op jit(solution)/shard_map/ijab,ijbf->ijaf/dot_general | solution.py:85
  65.4 15.6 %all-to-all-done = bf16[32,2,8320]{2,1,0:T(2,128)(2,1)} async-done(((bf16[32,2,8320]{2,1,0:T(2,128)(2,1)}), bf16[32,2,8320]{2,1,0:T(2,128)(2,1)}, u32[]{:S(2)}, u32[]{:S(2)}) %all-to-all-start) | async-done | bytes 1064992 | tf_op jit(solution)/shard_map/all_to_all | solution.py:162
  81.0 1.5 reshape.403
  84.0 1.1 fusion.12
  86.3 1.7 %convolution_convert_fusion.1 = bf16[64,8192]{1,0:T(8,128)(2,1)} fusion(bf16[48,64]{0,1:T(8,128)(2,1)S(1)} %bitcast.138, bf16[6,8,64,128]{3,2,1,0:T(8,128)(2,1)S(1)} %bitcast.128), kind=kOutput, calls=%fused_computation.3 | convolution fusion | flops 50855936 | bytes 1841152 | tf_op jit(solution)/shard_map/es,ek->sk/dot_general | solution.py:115
  88.0 2.5 %reshape.408 = bf16[32,2,8192]{2,1,0:T(2,128)(2,1)} reshape(bf16[64,8192]{1,0:T(8,128)(2,1)} %convolution_convert_fusion.1) | data formatting | bytes 2097152 | tf_op jit(solution)/shard_map/reshape | solution.py:118
  90.5 12.8 %all-to-all-start.1 = ((bf16[32,2,8192]{2,1,0:T(2,128)(2,1)}), bf16[32,2,8192]{2,1,0:T(2,128)(2,1)}, u32[]{:S(2)}, u32[]{:S(2)}) async-start(bf16[32,2,8192]{2,1,0:T(2,128)(2,1)} %reshape.408), calls=%async_computation.1 | async-start | bytes 2097152 | tf_op jit(solution)/shard_map/all_to_all | solution.py:172
  104.2 3.1 %collective-permute-start.4 = (bf16[1,4,64,128]{3,2,1,0:T(8,128)(2,1)S(1)}, bf16[1,4,64,128]{3,2,1,0:T(8,128)(2,1)S(1)}, u32[]{:S(2)}, u32[]{:S(2)}) collective-permute-start(bf16[1,4,64,128]{3,2,1,0:T(8,128)(2,1)S(1)} %get-tuple-element.20), channel_id=1, source_target_pairs={{0,16},{16,32},{32,48},{48,64},{64,80},{80,96},{96,112},{112,128},... | collective-permute-start | bytes 196616 | tf_op jit(solution)/shard_map/ppermute | solution.py:65
  107.3 10.8 %collective-permute-start.6 = (bf16[4,1,64,128]{3,2,1,0:T(8,128)(2,1)S(1)}, bf16[4,1,64,128]{3,2,1,0:T(8,128)(2,1)S(1)}, u32[]{:S(2)}, u32[]{:S(2)}) collective-permute-start(bf16[4,1,64,128]{3,2,1,0:T(8,128)(2,1)S(1)} %get-tuple-element.21), channel_id=1, source_target_pairs={{0,1},{1,2},{2,3},{3,4},{4,5},{5,6},{6,7},{7,8},{8,9},{9,10},{10,1... | collective-permute-start | bytes 196616 | tf_op jit(solution)/shard_map/ppermute | solution.py:67
  118.1 1.9 %collective-permute-start.7 = (bf16[4,1,64,128]{3,2,1,0:T(8,128)(2,1)S(1)}, bf16[4,1,64,128]{3,2,1,0:T(8,128)(2,1)S(1)}, u32[]{:S(2)}, u32[]{:S(2)}) collective-permute-start(bf16[4,1,64,128]{3,2,1,0:T(8,128)(2,1)S(1)} %get-tuple-element.22), channel_id=1, source_target_pairs={{1,0},{2,1},{3,2},{4,3},{5,4},{6,5},{7,6},{8,7},{9,8},{10,9},{11,1... | collective-permute-start | bytes 196616 | tf_op jit(solution)/shard_map/ppermute | solution.py:68
  120.1 2.2 %collective-permute-start.5 = (bf16[1,4,64,128]{3,2,1,0:T(8,128)(2,1)S(1)}, bf16[1,4,64,128]{3,2,1,0:T(8,128)(2,1)S(1)}, u32[]{:S(2)}, u32[]{:S(2)}) collective-permute-start(bf16[1,4,64,128]{3,2,1,0:T(8,128)(2,1)S(1)} %get-tuple-element.19), channel_id=1, source_target_pairs={{16,0},{32,16},{48,32},{64,48},{80,64},{96,80},{112,96},{128,112},... | collective-permute-start | bytes 196616 | tf_op jit(solution)/shard_map/ppermute | solution.py:66
  122.5 1.0 convolution_add_fusion
  123.6 1.0 fusion.51
  124.7 10.1 %collective-permute-done.7 = bf16[4,1,64,128]{3,2,1,0:T(8,128)(2,1)S(1)} collective-permute-done((bf16[4,1,64,128]{3,2,1,0:T(8,128)(2,1)S(1)}, bf16[4,1,64,128]{3,2,1,0:T(8,128)(2,1)S(1)}, u32[]{:S(2)}, u32[]{:S(2)}) %collective-permute-start.7) | collective-permute-done | bytes 65568 | tf_op jit(solution)/shard_map/ppermute | solution.py:68
  134.7 1.0 fusion.55
  136.3 19.6 %all-to-all-done.1 = bf16[32,2,8192]{2,1,0:T(2,128)(2,1)} async-done(((bf16[32,2,8192]{2,1,0:T(2,128)(2,1)}), bf16[32,2,8192]{2,1,0:T(2,128)(2,1)}, u32[]{:S(2)}, u32[]{:S(2)}) %all-to-all-start.1) | async-done | bytes 1048608 | tf_op jit(solution)/shard_map/all_to_all | solution.py:172
  156.0 1.5 reshape.409
  (113 shorter events, 19.7 us)
Async XLA Ops:
  0.0 4.6 %copy-start.16 = (f32[32]{0:T(128)S(1)}, f32[32]{0:T(128)}, u32[]{:S(2)}) copy-start(f32[32]{0:T(128)} %param.17) | copy-start | bytes 388
  0.0 4.7 %copy-start.17 = (f32[32]{0:T(128)S(1)}, f32[32]{0:T(128)}, u32[]{:S(2)}) copy-start(f32[32]{0:T(128)} %param.18) | copy-start | bytes 388
  2.9 2.2 %copy-start.6 = (bf16[4,4,64,128]{3,2,1,0:T(8,128)(2,1)S(1)}, bf16[4,4,64,128]{3,2,1,0:T(8,128)(2,1)}, u32[]{:S(2)}) copy-start(bf16[4,4,64,128]{3,2,1,0:T(8,128)(2,1)} %param.14) | copy-start | bytes 786436
  5.4 0.7 copy-start.19
  5.4 1.0 copy-start.13
  6.4 1.6 copy-start.14
  8.4 0.7 copy-start.15
  8.4 1.1 copy-start.20
  11.8 33.8 %copy-start.10 = (bf16[4,4,5,4096]{3,1,2,0:T(4,128)(2,1)S(1)}, bf16[4,4,5,4096]{3,1,2,0:T(4,128)(2,1)}, u32[]{:S(2)}) copy-start(bf16[4,4,5,4096]{3,1,2,0:T(4,128)(2,1)} %param.19) | copy-start | bytes 1966084
  11.8 69.2 %all-to-all-start = ((bf16[32,2,8320]{2,1,0:T(2,128)(2,1)}), bf16[32,2,8320]{2,1,0:T(2,128)(2,1)}, u32[]{:S(2)}, u32[]{:S(2)}) async-start(bf16[32,2,8320]{2,1,0:T(2,128)(2,1)} %reshape.402), calls=%async_computation | async-start | bytes 2129920 | tf_op jit(solution)/shard_map/all_to_all | solution.py:162
  27.4 36.2 %collective-permute-start = (bf16[1,4,64,128]{3,2,1,0:T(8,128)(2,1)}, bf16[1,4,64,128]{3,2,1,0:T(8,128)(2,1)}, u32[]{:S(2)}, u32[]{:S(2)}) collective-permute-start(bf16[1,4,64,128]{3,2,1,0:T(8,128)(2,1)} %bitcast.11), channel_id=1, source_target_pairs={{0,16},{16,32},{32,48},{48,64},{64,80},{80,96},{96,112},{112,128},... | collective-permute-start | bytes 196616 | tf_op jit(solution)/shard_map/ppermute | solution.py:65
  31.2 19.7 %collective-permute-start.2 = (bf16[4,1,64,128]{3,2,1,0:T(8,128)(2,1)}, bf16[4,1,64,128]{3,2,1,0:T(8,128)(2,1)}, u32[]{:S(2)}, u32[]{:S(2)}) collective-permute-start(bf16[4,1,64,128]{3,2,1,0:T(8,128)(2,1)} %get-tuple-element.29), channel_id=1, source_target_pairs={{0,1},{1,2},{2,3},{3,4},{4,5},{5,6},{6,7},{7,8},{8,9},{9,10},{10,1... | collective-permute-start | bytes 196616 | tf_op jit(solution)/shard_map/ppermute | solution.py:67
  40.2 17.0 %collective-permute-start.3 = (bf16[4,1,64,128]{3,2,1,0:T(8,128)(2,1)}, bf16[4,1,64,128]{3,2,1,0:T(8,128)(2,1)}, u32[]{:S(2)}, u32[]{:S(2)}) collective-permute-start(bf16[4,1,64,128]{3,2,1,0:T(8,128)(2,1)} %get-tuple-element.30), channel_id=1, source_target_pairs={{1,0},{2,1},{3,2},{4,3},{5,4},{6,5},{7,6},{8,7},{9,8},{10,9},{11,1... | collective-permute-start | bytes 196616 | tf_op jit(solution)/shard_map/ppermute | solution.py:68
  42.8 40.2 %collective-permute-start.1 = (bf16[1,4,64,128]{3,2,1,0:T(8,128)(2,1)}, bf16[1,4,64,128]{3,2,1,0:T(8,128)(2,1)}, u32[]{:S(2)}, u32[]{:S(2)}) collective-permute-start(bf16[1,4,64,128]{3,2,1,0:T(8,128)(2,1)} %bitcast.15), channel_id=1, source_target_pairs={{16,0},{32,16},{48,32},{64,48},{80,64},{96,80},{112,96},{128,112},... | collective-permute-start | bytes 196616 | tf_op jit(solution)/shard_map/ppermute | solution.py:66
  82.6 1.1 copy-start
  82.6 1.2 copy-start.3
  82.6 1.3 copy-start.5
  82.6 1.4 copy-start.9
  90.5 12.9 %copy-start.12 = (bf16[4,32,4,32]{3,2,1,0:T(4,128)(2,1)S(1)}, bf16[4,32,4,32]{3,2,1,0:T(4,128)(2,1)}, u32[]{:S(2)}) copy-start(bf16[4,32,4,32]{3,2,1,0:T(4,128)(2,1)} %get-tuple-element.48) | copy-start | bytes 98308
  90.5 13.0 %copy-start.11 = (bf16[4,32,4,32]{3,2,1,0:T(4,128)(2,1)S(1)}, bf16[4,32,4,32]{3,2,1,0:T(4,128)(2,1)}, u32[]{:S(2)}) copy-start(bf16[4,32,4,32]{3,2,1,0:T(4,128)(2,1)} %get-tuple-element.47) | copy-start | bytes 98308
  90.5 13.1 %copy-start.8 = (f32[4,32,4,32]{3,2,1,0:T(4,128)S(1)}, f32[4,32,4,32]{3,2,1,0:T(4,128)}, u32[]{:S(2)}) copy-start(f32[4,32,4,32]{3,2,1,0:T(4,128)} %get-tuple-element.46) | copy-start | bytes 196612
  90.5 13.3 %copy-start.18 = (f32[32]{0:T(128)S(1)}, f32[32]{0:T(128)}, u32[]{:S(2)}) copy-start(f32[32]{0:T(128)} %param.25) | copy-start | bytes 388
  90.5 65.4 %all-to-all-start.1 = ((bf16[32,2,8192]{2,1,0:T(2,128)(2,1)}), bf16[32,2,8192]{2,1,0:T(2,128)(2,1)}, u32[]{:S(2)}, u32[]{:S(2)}) async-start(bf16[32,2,8192]{2,1,0:T(2,128)(2,1)} %reshape.408), calls=%async_computation.1 | async-start | bytes 2097152 | tf_op jit(solution)/shard_map/all_to_all | solution.py:172
  104.2 31.9 %collective-permute-start.4 = (bf16[1,4,64,128]{3,2,1,0:T(8,128)(2,1)S(1)}, bf16[1,4,64,128]{3,2,1,0:T(8,128)(2,1)S(1)}, u32[]{:S(2)}, u32[]{:S(2)}) collective-permute-start(bf16[1,4,64,128]{3,2,1,0:T(8,128)(2,1)S(1)} %get-tuple-element.20), channel_id=1, source_target_pairs={{0,16},{16,32},{32,48},{48,64},{64,80},{80,96},{96,112},{112,128},... | collective-permute-start | bytes 196616 | tf_op jit(solution)/shard_map/ppermute | solution.py:65
  107.3 16.3 %collective-permute-start.6 = (bf16[4,1,64,128]{3,2,1,0:T(8,128)(2,1)S(1)}, bf16[4,1,64,128]{3,2,1,0:T(8,128)(2,1)S(1)}, u32[]{:S(2)}, u32[]{:S(2)}) collective-permute-start(bf16[4,1,64,128]{3,2,1,0:T(8,128)(2,1)S(1)} %get-tuple-element.21), channel_id=1, source_target_pairs={{0,1},{1,2},{2,3},{3,4},{4,5},{5,6},{6,7},{7,8},{8,9},{9,10},{10,1... | collective-permute-start | bytes 196616 | tf_op jit(solution)/shard_map/ppermute | solution.py:67
  118.1 16.6 %collective-permute-start.7 = (bf16[4,1,64,128]{3,2,1,0:T(8,128)(2,1)S(1)}, bf16[4,1,64,128]{3,2,1,0:T(8,128)(2,1)S(1)}, u32[]{:S(2)}, u32[]{:S(2)}) collective-permute-start(bf16[4,1,64,128]{3,2,1,0:T(8,128)(2,1)S(1)} %get-tuple-element.22), channel_id=1, source_target_pairs={{1,0},{2,1},{3,2},{4,3},{5,4},{6,5},{7,6},{8,7},{9,8},{10,9},{11,1... | collective-permute-start | bytes 196616 | tf_op jit(solution)/shard_map/ppermute | solution.py:68
  120.1 37.7 %collective-permute-start.5 = (bf16[1,4,64,128]{3,2,1,0:T(8,128)(2,1)S(1)}, bf16[1,4,64,128]{3,2,1,0:T(8,128)(2,1)S(1)}, u32[]{:S(2)}, u32[]{:S(2)}) collective-permute-start(bf16[1,4,64,128]{3,2,1,0:T(8,128)(2,1)S(1)} %get-tuple-element.19), channel_id=1, source_target_pairs={{16,0},{32,16},{48,32},{64,48},{80,64},{96,80},{112,96},{128,112},... | collective-permute-start | bytes 196616 | tf_op jit(solution)/shard_map/ppermute | solution.py:66
  157.4 1.0 copy-start.2
  157.4 1.2 copy-start.4
  158.6 1.0 copy-start.1
  158.9 1.4 copy-start.7

commit v6 on v5

--- a/solution.py
+++ b/solution.py
@@ -1,6 +1,8 @@
 import jax
 import jax.numpy as jnp
 from jax import lax
+from jax.experimental import pallas as pl
+from jax.experimental.pallas import tpu as pltpu
 from jax.sharding import PartitionSpec as P
 
 DILATION_STEP = 2
@@ -103,19 +105,58 @@
     return select.reshape(select.shape[0], -1).astype(jnp.bfloat16)
 
 
-def send_products(signal, edge_tiles, sources, select, target_col=None):
+def edge_slots(out_dev, senders):
+    destinations = out_dev.reshape(-1)
+    owners = jnp.arange(senders, dtype=jnp.int32)
+    dest_hits = (destinations[:, None] == owners[None, :]).astype(jnp.int32)
+    edge_ranks = jnp.sum((jnp.cumsum(dest_hits, axis=0) - 1) * dest_hits, axis=1)
+    return destinations * CAP + edge_ranks
+
+
+def product_kernel(src_ref, slot_ref, sig_ref, tile_ref, out_ref):
+    out_ref[...] = jnp.zeros(out_ref.shape, out_ref.dtype)
+
+    def body(edge, carry):
+        block = sig_ref[src_ref[edge]]
+        product = jnp.dot(tile_ref[edge], block, preferred_element_type=jnp.float32)
+        out_ref[slot_ref[edge]] = product.astype(out_ref.dtype)
+        return carry
+
+    lax.fori_loop(0, tile_ref.shape[0], body, 0)
+
+
+def send_products(signal, edge_tiles, sources, slots, select, target_col=None):
     block_rows, block_cols, block_size, features = signal.shape
-    flat = signal.reshape(block_rows * block_cols, block_size, features)
-    products = jnp.einsum(
-        "eab,ebf->eaf", edge_tiles, flat[sources], preferred_element_type=jnp.float32
+    nblocks = block_rows * block_cols
+    edge_count = edge_tiles.shape[0]
+    nslots = lax.axis_size("rx") * CAP
+    whole = lambda i, s, t: (0, 0, 0)
+    products = pl.pallas_call(
+        product_kernel,
+        out_shape=jax.ShapeDtypeStruct((nslots, block_size, features), jnp.bfloat16),
+        grid_spec=pltpu.PrefetchScalarGridSpec(
+            num_scalar_prefetch=2,
+            grid=(1,),
+            in_specs=[
+                pl.BlockSpec((nblocks, block_size, features), whole),
+                pl.BlockSpec((edge_count, block_size, block_size), whole),
+            ],
+            out_specs=pl.BlockSpec((nslots, block_size, features), whole),
+        ),
+        cost_estimate=pl.CostEstimate(
+            flops=2 * edge_count * block_size * block_size * features,
+            bytes_accessed=2 * (nblocks + nslots) * block_size * features
+            + 2 * edge_count * block_size * block_size,
+            transcendentals=0,
+        ),
+    )(sources, slots, signal.reshape(nblocks, block_size, features), edge_tiles)
+    if target_col is None:
+        return products.reshape(lax.axis_size("rx"), CAP, block_size, features)
+    slot_targets = jnp.einsum(
+        "es,ek->sk", select, target_col, preferred_element_type=jnp.float32
     ).astype(jnp.bfloat16)
-    products = products.reshape(products.shape[0], -1)
-    if target_col is not None:
-        products = jnp.concatenate([products, target_col], axis=1)
-    slots = jnp.einsum(
-        "es,ek->sk", select, products, preferred_element_type=jnp.float32
-    ).astype(jnp.bfloat16)
-    return slots.reshape(lax.axis_size("rx"), CAP, -1)
+    payload = jnp.concatenate([products.reshape(nslots, -1), slot_targets], axis=1)
+    return payload.reshape(lax.axis_size("rx"), CAP, -1)
 
 
 def far_terms(received, targets, nblocks):
@@ -151,13 +192,14 @@
     select = edge_select(out_dev, n_rx)
     sources = out_block.reshape(-1)
     edge_tiles = out_tiles.reshape(-1, block_size, block_size)
+    slots = edge_slots(out_dev, n_rx)
     edge_count = sources.shape[0]
     block_len = block_size * features
     target_col = jnp.zeros((edge_count, 128), jnp.bfloat16).at[:, 0].set(
         (out_target.reshape(-1) + 1).astype(jnp.bfloat16)
     )
 
-    send_one = send_products(gated, edge_tiles, sources, select, target_col)
+    send_one = send_products(gated, edge_tiles, sources, slots, select, target_col)
     halo_one = fetch_halo(gated)
     recv_one = lax.all_to_all(send_one, "rx", split_axis=0, concat_axis=0, tiled=True)
     recv_one = recv_one.reshape(n_rx * CAP, -1)
@@ -167,7 +209,7 @@
     far_one = far_terms(recv_one, targets, nblocks)
     first_hop = (near_one + far_one.reshape(gated.shape)).astype(jnp.bfloat16)
 
-    send_two = send_products(first_hop, edge_tiles, sources, select)
+    send_two = send_products(first_hop, edge_tiles, sources, slots, select)
     halo_two = fetch_halo(first_hop)
     recv_two = lax.all_to_all(send_two, "rx", split_axis=0, concat_axis=0, tiled=True)
     near_two = local_terms(first_hop, tiles, halo_two)

time: 162 us -> 179 us (1.10)
  Pallas kernels: 0 us -> 18.2 us
  waiting for transfers between devices: 54.7 us -> 43.2 us
  starting transfers between devices: 62.5 us -> 73.8 us
  local copies, waits for them, and re-layouts: 21.8 us -> 13.9 us
  other arithmetic: 6.13 us -> 11.4 us
    pallas_call x0 -> x2, Pallas kernels: none -> 18.2 us  [send_products(): pl.pallas_call(product_kernel, out_shape=jax.ShapeDtypeStruct((nslots, bl...]
    ppermute x2, waiting for transfers between devices: 14.5 us -> 0.01 us  [fetch_halo(): right = lax.ppermute(signal[:, :1], 'ry', shift_pairs(n_ry, -1))]
    ppermute x2, starting transfers between devices: 19.8 us -> 27.7 us  [fetch_halo(): left = lax.ppermute(signal[:, -1:], 'ry', shift_pairs(n_ry, 1))]
    reshape x3 -> x0, local copies, waits for them, and re-layouts: 5.23 us -> none  [the longest x2 3.77 us: send_products(): return slots.reshape(lax.axis_size('rx'), CAP, -1)]
    unnamed x46 -> x38, local copies, waits for them, and re-layouts: 4.37 us -> 0.81 us
    ppermute x2, waiting for transfers between devices: 4.93 us -> 8.23 us  [fetch_halo(): above = lax.ppermute(signal[-1:], 'rx', shift_pairs(n_rx, 1))]
    dot_general x4 -> x1, matrix products: 2.83 us -> 0.12 us  [send_products(): jnp.einsum('es,ek->sk', select, target_col, preferred_element_type=jnp.fl...]
    dot_general x8, matrix products: 9.08 us -> 11.4 us  [local_terms(): jnp.einsum('ijab,ijbf->ijaf', tiles[:, :, offset], neighbours[offset], pr...]
  transfers between devices with their start and end apart: 10 -> 10, of which waited for: 6 -> 4; matrix products, arithmetic and copies ran while one was open for 13% -> 12% of each run, Pallas kernels for 0% -> 0%
where the time goes in v6:
time: 179 us; the launch traced here: 178 us
  starting transfers between devices  73.8 us (41%)
  waiting for transfers between devices  43.2 us (24%)
  Pallas kernels  18.2 us (10%)
  matrix products  16.7 us (9%)
  local copies, waits for them, and re-layouts  13.9 us (8%)
  other arithmetic  11.4 us (6%)
    ppermute x2, starting transfers between devices, fetch_halo(): left = lax.ppermute(signal[:, -1:], 'ry', shift_pairs(n_ry, 1))  27.7 us
    all_to_all x1, waiting for transfers between devices, local(): lax.all_to_all(send_two, 'rx', split_axis=0, concat_axis=0, tiled=True)  19.5 us
    pallas_call x2, Pallas kernels, send_products(): pl.pallas_call(product_kernel, out_shape=jax.ShapeDtypeStruct((nslots, bl...  18.2 us
    all_to_all x1, waiting for transfers between devices, local(): lax.all_to_all(send_one, 'rx', split_axis=0, concat_axis=0, tiled=True)  15.4 us
    all_to_all x1, starting transfers between devices, local(): lax.all_to_all(send_two, 'rx', split_axis=0, concat_axis=0, tiled=True)  15 us
    all_to_all x1, starting transfers between devices, local(): lax.all_to_all(send_one, 'rx', split_axis=0, concat_axis=0, tiled=True)  14.8 us
    dot_general x8, matrix products, local_terms(): jnp.einsum('ijab,ijbf->ijaf', tiles[:, :, offset], neighbours[offset], pr...  11.4 us
    ppermute x2, waiting for transfers between devices, fetch_halo(): above = lax.ppermute(signal[-1:], 'rx', shift_pairs(n_rx, 1))  8.23 us
  transfers between devices with their start and end apart: 10, of which 4 were waited for; matrix products, arithmetic and copies ran while one was open for 12% of the time, Pallas kernels for 0%

profile of v6, /device:TPU:57, one launch (start us, length us, event | category | flops | bytes accessed | tf_op | source)
XLA Modules:
  0.0 177.7 jit_solution(12191103089322956051)
XLA Ops:
  2.4 1.2 multiply_add_fusion.1.slot_ref
  5.8 1.2 add_convert_fusion.1
  9.5 1.7 reshape.361.tile_ref
  11.2 9.1 %shard_map.118 = bf16[64,64,128]{2,1,0:T(8,128)(2,1)} custom-call(s32[48]{0:T(128)} %bitcast.131, s32[48]{0:T(128)} %multiply_add_fusion.1.slot_ref, bf16[16,64,128]{2,1,0:T(8,128)(2,1)} %bitcast.115, bf16[48,64,64]{2,1,0:T(8,128)(2,1)} %reshape.361.tile_ref), custom_call_target="tpu_custom_call" | custom-call | flops 50331648 | bytes 1703936 | tf_op jit(solution)/shard_map/pallas_call | solution.py:134
  20.3 1.3 concatenate.48
  22.4 2.0 %pad_maximum_fusion = bf16[32,2,8320]{2,1,0:T(2,128)(2,1)} fusion(bf16[32,2,128]{2,1,0:T(2,128)(2,1)S(1)} %bitcast.127, bf16[32,2,8192]{2,1,0:T(2,128)(2,1)S(1)} %concatenate.48), kind=kLoop, calls=%fused_computation.21 | loop fusion | flops 2129920 | bytes 2129920 | tf_op jit(solution)/shard_map/concatenate | solution.py:158
  24.4 14.8 %all-to-all-start = ((bf16[32,2,8320]{2,1,0:T(2,128)(2,1)}), bf16[32,2,8320]{2,1,0:T(2,128)(2,1)S(1)}, u32[]{:S(2)}, u32[]{:S(2)}) async-start(bf16[32,2,8320]{2,1,0:T(2,128)(2,1)} %pad_maximum_fusion), calls=%async_computation | async-start | bytes 2129920 | tf_op jit(solution)/shard_map/all_to_all | solution.py:204
  39.9 3.1 %collective-permute-start.3 = (bf16[4,1,64,128]{3,2,1,0:T(8,128)(2,1)}, bf16[4,1,64,128]{3,2,1,0:T(8,128)(2,1)}, u32[]{:S(2)}, u32[]{:S(2)}) collective-permute-start(bf16[4,1,64,128]{3,2,1,0:T(8,128)(2,1)} %get-tuple-element.30), channel_id=1, source_target_pairs={{1,0},{2,1},{3,2},{4,3},{5,4},{6,5},{7,6},{8,7},{9,8},{10,9},{11,1... | collective-permute-start | bytes 196616 | tf_op jit(solution)/shard_map/ppermute | solution.py:70
  43.1 13.2 %collective-permute-start.2 = (bf16[4,1,64,128]{3,2,1,0:T(8,128)(2,1)}, bf16[4,1,64,128]{3,2,1,0:T(8,128)(2,1)}, u32[]{:S(2)}, u32[]{:S(2)}) collective-permute-start(bf16[4,1,64,128]{3,2,1,0:T(8,128)(2,1)} %get-tuple-element.29), channel_id=1, source_target_pairs={{0,1},{1,2},{2,3},{3,4},{4,5},{5,6},{6,7},{7,8},{8,9},{9,10},{10,1... | collective-permute-start | bytes 196616 | tf_op jit(solution)/shard_map/ppermute | solution.py:69
  57.1 3.1 %collective-permute-start = (bf16[1,4,64,128]{3,2,1,0:T(8,128)(2,1)}, bf16[1,4,64,128]{3,2,1,0:T(8,128)(2,1)}, u32[]{:S(2)}, u32[]{:S(2)}) collective-permute-start(bf16[1,4,64,128]{3,2,1,0:T(8,128)(2,1)} %bitcast.11), channel_id=1, source_target_pairs={{0,16},{16,32},{32,48},{48,64},{64,80},{80,96},{96,112},{112,128},... | collective-permute-start | bytes 196616 | tf_op jit(solution)/shard_map/ppermute | solution.py:67
  60.9 2.8 %collective-permute-start.1 = (bf16[1,4,64,128]{3,2,1,0:T(8,128)(2,1)}, bf16[1,4,64,128]{3,2,1,0:T(8,128)(2,1)}, u32[]{:S(2)}, u32[]{:S(2)}) collective-permute-start(bf16[1,4,64,128]{3,2,1,0:T(8,128)(2,1)} %bitcast.15), channel_id=1, source_target_pairs={{16,0},{32,16},{48,32},{64,48},{80,64},{96,80},{112,96},{128,112},... | collective-permute-start | bytes 196616 | tf_op jit(solution)/shard_map/ppermute | solution.py:68
  67.6 1.1 copy.43
  68.7 2.0 %fusion.32 = f32[4,4,128,64]{2,3,1,0:T(8,128)} fusion(bf16[4,1,64,128]{3,2,1,0:T(8,128)(2,1)} %collective-permute-done.3, bf16[4,3,64,128]{3,2,1,0:T(8,128)(2,1)} %get-tuple-element.32, bf16[4,4,5,64,64]{4,3,1,0,2:T(8,128)(2,1)S(1)} %reshape.358), kind=kOutput, calls=%fused_computation.52 | convolution fusion | flops 17301504 | bytes 1048576 | tf_op jit(solution)/shard_map/ijab,ijbf->ijaf/dot_general | solution.py:87
  70.7 2.0 %fusion.28 = f32[4,4,128,64]{2,3,1,0:T(8,128)} fusion(bf16[4,3,64,128]{3,2,1,0:T(8,128)(2,1)} %get-tuple-element.31, bf16[4,1,64,128]{3,2,1,0:T(8,128)(2,1)} %collective-permute-done.2, bf16[4,4,5,64,64]{4,3,1,0,2:T(8,128)(2,1)S(1)} %reshape.358), kind=kOutput, calls=%fused_computation.48 | convolution fusion | flops 17301504 | bytes 1048576 | tf_op jit(solution)/shard_map/ijab,ijbf->ijaf/dot_general | solution.py:87
  72.6 3.6 %collective-permute-done = bf16[1,4,64,128]{3,2,1,0:T(8,128)(2,1)} collective-permute-done((bf16[1,4,64,128]{3,2,1,0:T(8,128)(2,1)}, bf16[1,4,64,128]{3,2,1,0:T(8,128)(2,1)}, u32[]{:S(2)}, u32[]{:S(2)}) %collective-permute-start) | collective-permute-done | bytes 65568 | tf_op jit(solution)/shard_map/ppermute | solution.py:67
  76.2 1.9 %convolution_add_fusion.4 = f32[4,4,128,64]{2,3,1,0:T(8,128)} fusion(f32[4,4,128,64]{2,3,1,0:T(8,128)S(1)} %fusion.52, bf16[3,4,64,128]{3,2,1,0:T(8,128)(2,1)S(1)} %bitcast.126, bf16[1,4,64,128]{3,2,1,0:T(8,128)(2,1)} %collective-permute-done, bf16[4,4,5,64,64]{4,3,1,0,2:T(8,128)(2,1)S(1)} %reshape.358), kind=kOutput, calls=%fused_computation.16 | convolution fusion | flops 17432576 | bytes 1572864 | tf_op jit(solution)/shard_map/ijab,ijbf->ijaf/dot_general | solution.py:87
  78.1 15.4 %all-to-all-done = bf16[32,2,8320]{2,1,0:T(2,128)(2,1)S(1)} async-done(((bf16[32,2,8320]{2,1,0:T(2,128)(2,1)}), bf16[32,2,8320]{2,1,0:T(2,128)(2,1)S(1)}, u32[]{:S(2)}, u32[]{:S(2)}) %all-to-all-start) | async-done | bytes 1064992 | tf_op jit(solution)/shard_map/all_to_all | solution.py:204
  93.5 1.2 reshape.363
  95.6 1.6 convolution_bitcast_fusion.1
  97.4 1.8 %fusion.11 = bf16[4,4,64,128]{3,2,1,0:T(8,128)(2,1)} fusion(f32[4,4,64,128]{3,2,1,0:T(8,128)S(1)} %bitcast.122, f32[4,4,128,64]{2,3,1,0:T(8,128)S(1)} %copy-done.4, f32[4,4,128,64]{2,3,1,0:T(8,128)S(1)} %copy-done.5, f32[4,4,128,64]{2,3,1,0:T(8,128)S(1)} %copy-done.2, bf16[1,4,64,128]{3,2,1,0:T(8,128)(2,1)} %collective-permute-done.1, ...), kind=kOutput, calls=%fused_computation.19 | convolution fusion | flops 17956864 | bytes 2883584 | tf_op jit(solution)/shard_map/ijab,ijbf->ijaf/dot_general | solution.py:87
  99.1 9.1 %shard_map.119 = bf16[64,64,128]{2,1,0:T(8,128)(2,1)} custom-call(s32[48]{0:T(128)} %bitcast.132, s32[48]{0:T(128)} %multiply_add_fusion.1.slot_ref, bf16[16,64,128]{2,1,0:T(8,128)(2,1)} %bitcast.113, bf16[48,64,64]{2,1,0:T(8,128)(2,1)} %reshape.361.tile_ref), custom_call_target="tpu_custom_call" | custom-call | flops 50331648 | bytes 1703936 | tf_op jit(solution)/shard_map/pallas_call | solution.py:134
  108.3 15.0 %all-to-all-start.1 = ((bf16[32,2,64,128]{3,2,1,0:T(8,128)(2,1)}), bf16[32,2,64,128]{3,2,1,0:T(8,128)(2,1)S(1)}, u32[]{:S(2)}, u32[]{:S(2)}) async-start(bf16[32,2,64,128]{3,2,1,0:T(8,128)(2,1)} %bitcast.120), calls=%async_computation.1 | async-start | bytes 2097152 | tf_op jit(solution)/shard_map/all_to_all | solution.py:214
  124.2 1.9 %collective-permute-start.7 = (bf16[4,1,64,128]{3,2,1,0:T(8,128)(2,1)S(1)}, bf16[4,1,64,128]{3,2,1,0:T(8,128)(2,1)S(1)}, u32[]{:S(2)}, u32[]{:S(2)}) collective-permute-start(bf16[4,1,64,128]{3,2,1,0:T(8,128)(2,1)S(1)} %get-tuple-element.22), channel_id=1, source_target_pairs={{1,0},{2,1},{3,2},{4,3},{5,4},{6,5},{7,6},{8,7},{9,8},{10,9},{11,1... | collective-permute-start | bytes 196616 | tf_op jit(solution)/shard_map/ppermute | solution.py:70
  126.1 14.5 %collective-permute-start.6 = (bf16[4,1,64,128]{3,2,1,0:T(8,128)(2,1)S(1)}, bf16[4,1,64,128]{3,2,1,0:T(8,128)(2,1)S(1)}, u32[]{:S(2)}, u32[]{:S(2)}) collective-permute-start(bf16[4,1,64,128]{3,2,1,0:T(8,128)(2,1)S(1)} %get-tuple-element.21), channel_id=1, source_target_pairs={{0,1},{1,2},{2,3},{3,4},{4,5},{5,6},{6,7},{7,8},{8,9},{9,10},{10,1... | collective-permute-start | bytes 196616 | tf_op jit(solution)/shard_map/ppermute | solution.py:69
  140.6 3.1 %collective-permute-start.4 = (bf16[1,4,64,128]{3,2,1,0:T(8,128)(2,1)S(1)}, bf16[1,4,64,128]{3,2,1,0:T(8,128)(2,1)S(1)}, u32[]{:S(2)}, u32[]{:S(2)}) collective-permute-start(bf16[1,4,64,128]{3,2,1,0:T(8,128)(2,1)S(1)} %get-tuple-element.20), channel_id=1, source_target_pairs={{0,16},{16,32},{32,48},{48,64},{64,80},{80,96},{96,112},{112,128},... | collective-permute-start | bytes 196616 | tf_op jit(solution)/shard_map/ppermute | solution.py:67
  143.7 2.2 %collective-permute-start.5 = (bf16[1,4,64,128]{3,2,1,0:T(8,128)(2,1)S(1)}, bf16[1,4,64,128]{3,2,1,0:T(8,128)(2,1)S(1)}, u32[]{:S(2)}, u32[]{:S(2)}) collective-permute-start(bf16[1,4,64,128]{3,2,1,0:T(8,128)(2,1)S(1)} %get-tuple-element.19), channel_id=1, source_target_pairs={{16,0},{32,16},{48,32},{64,48},{80,64},{96,80},{112,96},{128,112},... | collective-permute-start | bytes 196616 | tf_op jit(solution)/shard_map/ppermute | solution.py:68
  146.2 1.0 convolution_add_fusion
  147.3 1.0 fusion.46
  148.3 1.0 fusion.42
  149.3 4.7 %collective-permute-done.4 = bf16[1,4,64,128]{3,2,1,0:T(8,128)(2,1)S(1)} collective-permute-done((bf16[1,4,64,128]{3,2,1,0:T(8,128)(2,1)S(1)}, bf16[1,4,64,128]{3,2,1,0:T(8,128)(2,1)S(1)}, u32[]{:S(2)}, u32[]{:S(2)}) %collective-permute-start.4) | collective-permute-done | bytes 65568 | tf_op jit(solution)/shard_map/ppermute | solution.py:67
  154.2 19.5 %all-to-all-done.1 = bf16[32,2,64,128]{3,2,1,0:T(8,128)(2,1)S(1)} async-done(((bf16[32,2,64,128]{3,2,1,0:T(8,128)(2,1)}), bf16[32,2,64,128]{3,2,1,0:T(8,128)(2,1)S(1)}, u32[]{:S(2)}, u32[]{:S(2)}) %all-to-all-start.1) | async-done | bytes 1048608 | tf_op jit(solution)/shard_map/all_to_all | solution.py:214
  174.4 1.5 fusion.5
  (100 shorter events, 18.4 us)
Async XLA Ops:
  0.0 7.5 %copy-start.14 = (f32[32]{0:T(128)S(1)}, f32[32]{0:T(128)}, u32[]{:S(2)}) copy-start(f32[32]{0:T(128)} %param.18) | copy-start | bytes 388
  0.0 7.6 %copy-start.15 = (f32[32]{0:T(128)S(1)}, f32[32]{0:T(128)}, u32[]{:S(2)}) copy-start(f32[32]{0:T(128)} %param.17) | copy-start | bytes 388
  5.8 2.2 %copy-start.6 = (bf16[4,4,64,128]{3,2,1,0:T(8,128)(2,1)S(1)}, bf16[4,4,64,128]{3,2,1,0:T(8,128)(2,1)}, u32[]{:S(2)}) copy-start(bf16[4,4,64,128]{3,2,1,0:T(8,128)(2,1)} %param.14) | copy-start | bytes 786436
  8.4 1.2 copy-start.13
  20.3 1.4 copy-start.17
  24.4 14.8 %copy-start.1 = (bf16[1024,1,128]{2,0,1:T(8,128)(2,1)S(1)}, bf16[1024,1,128]{2,0,1:T(8,128)(2,1)}, u32[]{:S(2)}) copy-start(bf16[1024,1,128]{2,0,1:T(8,128)(2,1)} %copy.39) | copy-start | bytes 786436
  24.4 39.2 %copy-start.10 = (bf16[4,4,5,4096]{3,1,2,0:T(4,128)(2,1)S(1)}, bf16[4,4,5,4096]{3,1,2,0:T(4,128)(2,1)}, u32[]{:S(2)}) copy-start(bf16[4,4,5,4096]{3,1,2,0:T(4,128)(2,1)} %param.19) | copy-start | bytes 1966084
  24.4 69.1 %all-to-all-start = ((bf16[32,2,8320]{2,1,0:T(2,128)(2,1)}), bf16[32,2,8320]{2,1,0:T(2,128)(2,1)S(1)}, u32[]{:S(2)}, u32[]{:S(2)}) async-start(bf16[32,2,8320]{2,1,0:T(2,128)(2,1)} %pad_maximum_fusion), calls=%async_computation | async-start | bytes 2129920 | tf_op jit(solution)/shard_map/all_to_all | solution.py:204
  39.9 28.7 %collective-permute-start.3 = (bf16[4,1,64,128]{3,2,1,0:T(8,128)(2,1)}, bf16[4,1,64,128]{3,2,1,0:T(8,128)(2,1)}, u32[]{:S(2)}, u32[]{:S(2)}) collective-permute-start(bf16[4,1,64,128]{3,2,1,0:T(8,128)(2,1)} %get-tuple-element.30), channel_id=1, source_target_pairs={{1,0},{2,1},{3,2},{4,3},{5,4},{6,5},{7,6},{8,7},{9,8},{10,9},{11,1... | collective-permute-start | bytes 196616 | tf_op jit(solution)/shard_map/ppermute | solution.py:70
  43.1 27.6 %collective-permute-start.2 = (bf16[4,1,64,128]{3,2,1,0:T(8,128)(2,1)}, bf16[4,1,64,128]{3,2,1,0:T(8,128)(2,1)}, u32[]{:S(2)}, u32[]{:S(2)}) collective-permute-start(bf16[4,1,64,128]{3,2,1,0:T(8,128)(2,1)} %get-tuple-element.29), channel_id=1, source_target_pairs={{0,1},{1,2},{2,3},{3,4},{4,5},{5,6},{6,7},{7,8},{8,9},{9,10},{10,1... | collective-permute-start | bytes 196616 | tf_op jit(solution)/shard_map/ppermute | solution.py:69
  57.1 19.1 %collective-permute-start = (bf16[1,4,64,128]{3,2,1,0:T(8,128)(2,1)}, bf16[1,4,64,128]{3,2,1,0:T(8,128)(2,1)}, u32[]{:S(2)}, u32[]{:S(2)}) collective-permute-start(bf16[1,4,64,128]{3,2,1,0:T(8,128)(2,1)} %bitcast.11), channel_id=1, source_target_pairs={{0,16},{16,32},{32,48},{48,64},{64,80},{80,96},{96,112},{112,128},... | collective-permute-start | bytes 196616 | tf_op jit(solution)/shard_map/ppermute | solution.py:67
  60.9 36.4 %collective-permute-start.1 = (bf16[1,4,64,128]{3,2,1,0:T(8,128)(2,1)}, bf16[1,4,64,128]{3,2,1,0:T(8,128)(2,1)}, u32[]{:S(2)}, u32[]{:S(2)}) collective-permute-start(bf16[1,4,64,128]{3,2,1,0:T(8,128)(2,1)} %bitcast.15), channel_id=1, source_target_pairs={{16,0},{32,16},{48,32},{64,48},{80,64},{96,80},{112,96},{128,112},... | collective-permute-start | bytes 196616 | tf_op jit(solution)/shard_map/ppermute | solution.py:68
  68.6 7.6 %copy-start.9 = (bf16[768,1,128]{2,0,1:T(8,128)(2,1)S(1)}, bf16[768,1,128]{2,0,1:T(8,128)(2,1)}, u32[]{:S(2)}) copy-start(bf16[768,1,128]{2,0,1:T(8,128)(2,1)} %copy.42) | copy-start | bytes 589828
  95.6 1.8 copy-start.2
  95.6 1.8 copy-start.4
  95.6 1.8 copy-start.5
  108.2 15.1 %copy-start.12 = (bf16[4,32,4,32]{3,2,1,0:T(4,128)(2,1)S(1)}, bf16[4,32,4,32]{3,2,1,0:T(4,128)(2,1)}, u32[]{:S(2)}) copy-start(bf16[4,32,4,32]{3,2,1,0:T(4,128)(2,1)} %get-tuple-element.48) | copy-start | bytes 98308
  108.2 15.2 %copy-start.11 = (bf16[4,32,4,32]{3,2,1,0:T(4,128)(2,1)S(1)}, bf16[4,32,4,32]{3,2,1,0:T(4,128)(2,1)}, u32[]{:S(2)}) copy-start(bf16[4,32,4,32]{3,2,1,0:T(4,128)(2,1)} %get-tuple-element.47) | copy-start | bytes 98308
  108.2 15.3 %copy-start.8 = (f32[4,32,4,32]{3,2,1,0:T(4,128)S(1)}, f32[4,32,4,32]{3,2,1,0:T(4,128)}, u32[]{:S(2)}) copy-start(f32[4,32,4,32]{3,2,1,0:T(4,128)} %get-tuple-element.46) | copy-start | bytes 196612
  108.2 15.5 %copy-start.16 = (f32[32]{0:T(128)S(1)}, f32[32]{0:T(128)}, u32[]{:S(2)}) copy-start(f32[32]{0:T(128)} %param.25) | copy-start | bytes 388
  108.3 15.9 %copy-start = (bf16[4,4,64,128]{3,2,1,0:T(8,128)(2,1)S(1)}, bf16[4,4,64,128]{3,2,1,0:T(8,128)(2,1)}, u32[]{:S(2)}) copy-start(bf16[4,4,64,128]{3,2,1,0:T(8,128)(2,1)} %fusion.11) | copy-start | bytes 786436
  108.3 65.5 %all-to-all-start.1 = ((bf16[32,2,64,128]{3,2,1,0:T(8,128)(2,1)}), bf16[32,2,64,128]{3,2,1,0:T(8,128)(2,1)S(1)}, u32[]{:S(2)}, u32[]{:S(2)}) async-start(bf16[32,2,64,128]{3,2,1,0:T(8,128)(2,1)} %bitcast.120), calls=%async_computation.1 | async-start | bytes 2097152 | tf_op jit(solution)/shard_map/all_to_all | solution.py:214
  124.2 23.1 %collective-permute-start.7 = (bf16[4,1,64,128]{3,2,1,0:T(8,128)(2,1)S(1)}, bf16[4,1,64,128]{3,2,1,0:T(8,128)(2,1)S(1)}, u32[]{:S(2)}, u32[]{:S(2)}) collective-permute-start(bf16[4,1,64,128]{3,2,1,0:T(8,128)(2,1)S(1)} %get-tuple-element.22), channel_id=1, source_target_pairs={{1,0},{2,1},{3,2},{4,3},{5,4},{6,5},{7,6},{8,7},{9,8},{10,9},{11,1... | collective-permute-start | bytes 196616 | tf_op jit(solution)/shard_map/ppermute | solution.py:70
  126.1 22.2 %collective-permute-start.6 = (bf16[4,1,64,128]{3,2,1,0:T(8,128)(2,1)S(1)}, bf16[4,1,64,128]{3,2,1,0:T(8,128)(2,1)S(1)}, u32[]{:S(2)}, u32[]{:S(2)}) collective-permute-start(bf16[4,1,64,128]{3,2,1,0:T(8,128)(2,1)S(1)} %get-tuple-element.21), channel_id=1, source_target_pairs={{0,1},{1,2},{2,3},{3,4},{4,5},{5,6},{6,7},{7,8},{8,9},{9,10},{10,1... | collective-permute-start | bytes 196616 | tf_op jit(solution)/shard_map/ppermute | solution.py:69
  140.6 13.4 %collective-permute-start.4 = (bf16[1,4,64,128]{3,2,1,0:T(8,128)(2,1)S(1)}, bf16[1,4,64,128]{3,2,1,0:T(8,128)(2,1)S(1)}, u32[]{:S(2)}, u32[]{:S(2)}) collective-permute-start(bf16[1,4,64,128]{3,2,1,0:T(8,128)(2,1)S(1)} %get-tuple-element.20), channel_id=1, source_target_pairs={{0,16},{16,32},{32,48},{48,64},{64,80},{80,96},{96,112},{112,128},... | collective-permute-start | bytes 196616 | tf_op jit(solution)/shard_map/ppermute | solution.py:67
  143.7 30.8 %collective-permute-start.5 = (bf16[1,4,64,128]{3,2,1,0:T(8,128)(2,1)S(1)}, bf16[1,4,64,128]{3,2,1,0:T(8,128)(2,1)S(1)}, u32[]{:S(2)}, u32[]{:S(2)}) collective-permute-start(bf16[1,4,64,128]{3,2,1,0:T(8,128)(2,1)S(1)} %get-tuple-element.19), channel_id=1, source_target_pairs={{16,0},{32,16},{48,32},{64,48},{80,64},{96,80},{112,96},{128,112},... | collective-permute-start | bytes 196616 | tf_op jit(solution)/shard_map/ppermute | solution.py:68
  174.4 1.5 copy-start.3
  175.9 1.0 copy-start.7

commit v7 on v6

--- a/solution.py
+++ b/solution.py
@@ -122,7 +122,7 @@
         out_ref[slot_ref[edge]] = product.astype(out_ref.dtype)
         return carry
 
-    lax.fori_loop(0, tile_ref.shape[0], body, 0)
+    lax.fori_loop(0, tile_ref.shape[0], body, 0, unroll=True)
 
 
 def send_products(signal, edge_tiles, sources, slots, select, target_col=None):

time: 179 us -> 167 us (0.933)
  Pallas kernels: 18.2 us -> 6.64 us
    pallas_call x2, Pallas kernels: 18.2 us -> 6.64 us  [send_products(): pl.pallas_call(product_kernel, out_shape=jax.ShapeDtypeStruct((nslots, bl...]
  transfers between devices with their start and end apart: 10 -> 10, of which waited for: 4 -> 4; matrix products, arithmetic and copies ran while one was open for 12% -> 13% of each run, Pallas kernels for 0% -> 0%
where the time goes in v7:
time: 167 us; the launch traced here: 166 us
  starting transfers between devices  73.8 us (44%)
  waiting for transfers between devices  43.2 us (26%)
  matrix products  16.7 us (10%)
  local copies, waits for them, and re-layouts  13.9 us (8%)
  other arithmetic  11.4 us (7%)
  Pallas kernels  6.64 us (4%)
    ppermute x2, starting transfers between devices, fetch_halo(): left = lax.ppermute(signal[:, -1:], 'ry', shift_pairs(n_ry, 1))  27.7 us
    all_to_all x1, waiting for transfers between devices, local(): lax.all_to_all(send_two, 'rx', split_axis=0, concat_axis=0, tiled=True)  19.5 us
    all_to_all x1, waiting for transfers between devices, local(): lax.all_to_all(send_one, 'rx', split_axis=0, concat_axis=0, tiled=True)  15.4 us
    all_to_all x1, starting transfers between devices, local(): lax.all_to_all(send_two, 'rx', split_axis=0, concat_axis=0, tiled=True)  15 us
    all_to_all x1, starting transfers between devices, local(): lax.all_to_all(send_one, 'rx', split_axis=0, concat_axis=0, tiled=True)  14.8 us
    dot_general x8, matrix products, local_terms(): jnp.einsum('ijab,ijbf->ijaf', tiles[:, :, offset], neighbours[offset], pr...  11.4 us
    ppermute x2, waiting for transfers between devices, fetch_halo(): above = lax.ppermute(signal[-1:], 'rx', shift_pairs(n_rx, 1))  8.23 us
    pallas_call x2, Pallas kernels, send_products(): pl.pallas_call(product_kernel, out_shape=jax.ShapeDtypeStruct((nslots, bl...  6.64 us
  transfers between devices with their start and end apart: 10, of which 4 were waited for; matrix products, arithmetic and copies ran while one was open for 13% of the time, Pallas kernels for 0%

profile of v7, /device:TPU:57, one launch (start us, length us, event | category | flops | bytes accessed | tf_op | source)
XLA Modules:
  0.0 166.1 jit_solution(308359185584356024)
XLA Ops:
  2.4 1.2 multiply_add_fusion.1.slot_ref
  5.8 1.2 add_convert_fusion.1
  9.5 1.7 %reshape.361.tile_ref = bf16[48,64,64]{2,1,0:T(8,128)(2,1)} reshape(bf16[1,1,48,4096]{3,2,1,0:T(8,128)(2,1)S(1)} %copy-done.13) | data formatting | bytes 786432 | tf_op jit(solution)/shard_map/reshape | solution.py:194
  11.2 3.3 %shard_map.118 = bf16[64,64,128]{2,1,0:T(8,128)(2,1)} custom-call(s32[48]{0:T(128)} %bitcast.131, s32[48]{0:T(128)} %multiply_add_fusion.1.slot_ref, bf16[16,64,128]{2,1,0:T(8,128)(2,1)} %bitcast.115, bf16[48,64,64]{2,1,0:T(8,128)(2,1)} %reshape.361.tile_ref), custom_call_target="tpu_custom_call" | custom-call | flops 50331648 | bytes 1703936 | tf_op jit(solution)/shard_map/pallas_call | solution.py:134
  14.6 1.3 concatenate.48
  16.6 2.0 %pad_maximum_fusion = bf16[32,2,8320]{2,1,0:T(2,128)(2,1)} fusion(bf16[32,2,128]{2,1,0:T(2,128)(2,1)S(1)} %bitcast.127, bf16[32,2,8192]{2,1,0:T(2,128)(2,1)S(1)} %concatenate.48), kind=kLoop, calls=%fused_computation.21 | loop fusion | flops 2129920 | bytes 2129920 | tf_op jit(solution)/shard_map/concatenate | solution.py:158
  18.7 14.8 %all-to-all-start = ((bf16[32,2,8320]{2,1,0:T(2,128)(2,1)}), bf16[32,2,8320]{2,1,0:T(2,128)(2,1)S(1)}, u32[]{:S(2)}, u32[]{:S(2)}) async-start(bf16[32,2,8320]{2,1,0:T(2,128)(2,1)} %pad_maximum_fusion), calls=%async_computation | async-start | bytes 2129920 | tf_op jit(solution)/shard_map/all_to_all | solution.py:204
  34.2 3.1 %collective-permute-start.3 = (bf16[4,1,64,128]{3,2,1,0:T(8,128)(2,1)}, bf16[4,1,64,128]{3,2,1,0:T(8,128)(2,1)}, u32[]{:S(2)}, u32[]{:S(2)}) collective-permute-start(bf16[4,1,64,128]{3,2,1,0:T(8,128)(2,1)} %get-tuple-element.30), channel_id=1, source_target_pairs={{1,0},{2,1},{3,2},{4,3},{5,4},{6,5},{7,6},{8,7},{9,8},{10,9},{11,1... | collective-permute-start | bytes 196616 | tf_op jit(solution)/shard_map/ppermute | solution.py:70
  37.3 13.2 %collective-permute-start.2 = (bf16[4,1,64,128]{3,2,1,0:T(8,128)(2,1)}, bf16[4,1,64,128]{3,2,1,0:T(8,128)(2,1)}, u32[]{:S(2)}, u32[]{:S(2)}) collective-permute-start(bf16[4,1,64,128]{3,2,1,0:T(8,128)(2,1)} %get-tuple-element.29), channel_id=1, source_target_pairs={{0,1},{1,2},{2,3},{3,4},{4,5},{5,6},{6,7},{7,8},{8,9},{9,10},{10,1... | collective-permute-start | bytes 196616 | tf_op jit(solution)/shard_map/ppermute | solution.py:69
  51.3 3.1 %collective-permute-start = (bf16[1,4,64,128]{3,2,1,0:T(8,128)(2,1)}, bf16[1,4,64,128]{3,2,1,0:T(8,128)(2,1)}, u32[]{:S(2)}, u32[]{:S(2)}) collective-permute-start(bf16[1,4,64,128]{3,2,1,0:T(8,128)(2,1)} %bitcast.11), channel_id=1, source_target_pairs={{0,16},{16,32},{32,48},{48,64},{64,80},{80,96},{96,112},{112,128},... | collective-permute-start | bytes 196616 | tf_op jit(solution)/shard_map/ppermute | solution.py:67
  55.1 2.8 %collective-permute-start.1 = (bf16[1,4,64,128]{3,2,1,0:T(8,128)(2,1)}, bf16[1,4,64,128]{3,2,1,0:T(8,128)(2,1)}, u32[]{:S(2)}, u32[]{:S(2)}) collective-permute-start(bf16[1,4,64,128]{3,2,1,0:T(8,128)(2,1)} %bitcast.15), channel_id=1, source_target_pairs={{16,0},{32,16},{48,32},{64,48},{80,64},{96,80},{112,96},{128,112},... | collective-permute-start | bytes 196616 | tf_op jit(solution)/shard_map/ppermute | solution.py:68
  61.8 1.1 copy.43
  62.9 2.0 %fusion.32 = f32[4,4,128,64]{2,3,1,0:T(8,128)} fusion(bf16[4,1,64,128]{3,2,1,0:T(8,128)(2,1)} %collective-permute-done.3, bf16[4,3,64,128]{3,2,1,0:T(8,128)(2,1)} %get-tuple-element.32, bf16[4,4,5,64,64]{4,3,1,0,2:T(8,128)(2,1)S(1)} %reshape.358), kind=kOutput, calls=%fused_computation.52 | convolution fusion | flops 17301504 | bytes 1048576 | tf_op jit(solution)/shard_map/ijab,ijbf->ijaf/dot_general | solution.py:87
  64.9 2.0 %fusion.28 = f32[4,4,128,64]{2,3,1,0:T(8,128)} fusion(bf16[4,3,64,128]{3,2,1,0:T(8,128)(2,1)} %get-tuple-element.31, bf16[4,1,64,128]{3,2,1,0:T(8,128)(2,1)} %collective-permute-done.2, bf16[4,4,5,64,64]{4,3,1,0,2:T(8,128)(2,1)S(1)} %reshape.358), kind=kOutput, calls=%fused_computation.48 | convolution fusion | flops 17301504 | bytes 1048576 | tf_op jit(solution)/shard_map/ijab,ijbf->ijaf/dot_general | solution.py:87
  66.9 3.6 %collective-permute-done = bf16[1,4,64,128]{3,2,1,0:T(8,128)(2,1)} collective-permute-done((bf16[1,4,64,128]{3,2,1,0:T(8,128)(2,1)}, bf16[1,4,64,128]{3,2,1,0:T(8,128)(2,1)}, u32[]{:S(2)}, u32[]{:S(2)}) %collective-permute-start) | collective-permute-done | bytes 65568 | tf_op jit(solution)/shard_map/ppermute | solution.py:67
  70.4 1.9 %convolution_add_fusion.4 = f32[4,4,128,64]{2,3,1,0:T(8,128)} fusion(f32[4,4,128,64]{2,3,1,0:T(8,128)S(1)} %fusion.52, bf16[3,4,64,128]{3,2,1,0:T(8,128)(2,1)S(1)} %bitcast.126, bf16[1,4,64,128]{3,2,1,0:T(8,128)(2,1)} %collective-permute-done, bf16[4,4,5,64,64]{4,3,1,0,2:T(8,128)(2,1)S(1)} %reshape.358), kind=kOutput, calls=%fused_computation.16 | convolution fusion | flops 17432576 | bytes 1572864 | tf_op jit(solution)/shard_map/ijab,ijbf->ijaf/dot_general | solution.py:87
  72.3 15.4 %all-to-all-done = bf16[32,2,8320]{2,1,0:T(2,128)(2,1)S(1)} async-done(((bf16[32,2,8320]{2,1,0:T(2,128)(2,1)}), bf16[32,2,8320]{2,1,0:T(2,128)(2,1)S(1)}, u32[]{:S(2)}, u32[]{:S(2)}) %all-to-all-start) | async-done | bytes 1064992 | tf_op jit(solution)/shard_map/all_to_all | solution.py:204
  87.7 1.2 reshape.363
  89.8 1.6 convolution_bitcast_fusion.1
  91.6 1.8 %fusion.11 = bf16[4,4,64,128]{3,2,1,0:T(8,128)(2,1)} fusion(f32[4,4,64,128]{3,2,1,0:T(8,128)S(1)} %bitcast.122, f32[4,4,128,64]{2,3,1,0:T(8,128)S(1)} %copy-done.4, f32[4,4,128,64]{2,3,1,0:T(8,128)S(1)} %copy-done.5, f32[4,4,128,64]{2,3,1,0:T(8,128)S(1)} %copy-done.2, bf16[1,4,64,128]{3,2,1,0:T(8,128)(2,1)} %collective-permute-done.1, ...), kind=kOutput, calls=%fused_computation.19 | convolution fusion | flops 17956864 | bytes 2883584 | tf_op jit(solution)/shard_map/ijab,ijbf->ijaf/dot_general | solution.py:87
  93.4 3.3 %shard_map.119 = bf16[64,64,128]{2,1,0:T(8,128)(2,1)} custom-call(s32[48]{0:T(128)} %bitcast.132, s32[48]{0:T(128)} %multiply_add_fusion.1.slot_ref, bf16[16,64,128]{2,1,0:T(8,128)(2,1)} %bitcast.113, bf16[48,64,64]{2,1,0:T(8,128)(2,1)} %reshape.361.tile_ref), custom_call_target="tpu_custom_call" | custom-call | flops 50331648 | bytes 1703936 | tf_op jit(solution)/shard_map/pallas_call | solution.py:134
  96.7 15.0 %all-to-all-start.1 = ((bf16[32,2,64,128]{3,2,1,0:T(8,128)(2,1)}), bf16[32,2,64,128]{3,2,1,0:T(8,128)(2,1)S(1)}, u32[]{:S(2)}, u32[]{:S(2)}) async-start(bf16[32,2,64,128]{3,2,1,0:T(8,128)(2,1)} %bitcast.120), calls=%async_computation.1 | async-start | bytes 2097152 | tf_op jit(solution)/shard_map/all_to_all | solution.py:214
  112.6 1.9 %collective-permute-start.7 = (bf16[4,1,64,128]{3,2,1,0:T(8,128)(2,1)S(1)}, bf16[4,1,64,128]{3,2,1,0:T(8,128)(2,1)S(1)}, u32[]{:S(2)}, u32[]{:S(2)}) collective-permute-start(bf16[4,1,64,128]{3,2,1,0:T(8,128)(2,1)S(1)} %get-tuple-element.22), channel_id=1, source_target_pairs={{1,0},{2,1},{3,2},{4,3},{5,4},{6,5},{7,6},{8,7},{9,8},{10,9},{11,1... | collective-permute-start | bytes 196616 | tf_op jit(solution)/shard_map/ppermute | solution.py:70
  114.5 14.5 %collective-permute-start.6 = (bf16[4,1,64,128]{3,2,1,0:T(8,128)(2,1)S(1)}, bf16[4,1,64,128]{3,2,1,0:T(8,128)(2,1)S(1)}, u32[]{:S(2)}, u32[]{:S(2)}) collective-permute-start(bf16[4,1,64,128]{3,2,1,0:T(8,128)(2,1)S(1)} %get-tuple-element.21), channel_id=1, source_target_pairs={{0,1},{1,2},{2,3},{3,4},{4,5},{5,6},{6,7},{7,8},{8,9},{9,10},{10,1... | collective-permute-start | bytes 196616 | tf_op jit(solution)/shard_map/ppermute | solution.py:69
  129.0 3.1 %collective-permute-start.4 = (bf16[1,4,64,128]{3,2,1,0:T(8,128)(2,1)S(1)}, bf16[1,4,64,128]{3,2,1,0:T(8,128)(2,1)S(1)}, u32[]{:S(2)}, u32[]{:S(2)}) collective-permute-start(bf16[1,4,64,128]{3,2,1,0:T(8,128)(2,1)S(1)} %get-tuple-element.20), channel_id=1, source_target_pairs={{0,16},{16,32},{32,48},{48,64},{64,80},{80,96},{96,112},{112,128},... | collective-permute-start | bytes 196616 | tf_op jit(solution)/shard_map/ppermute | solution.py:67
  132.1 2.2 %collective-permute-start.5 = (bf16[1,4,64,128]{3,2,1,0:T(8,128)(2,1)S(1)}, bf16[1,4,64,128]{3,2,1,0:T(8,128)(2,1)S(1)}, u32[]{:S(2)}, u32[]{:S(2)}) collective-permute-start(bf16[1,4,64,128]{3,2,1,0:T(8,128)(2,1)S(1)} %get-tuple-element.19), channel_id=1, source_target_pairs={{16,0},{32,16},{48,32},{64,48},{80,64},{96,80},{112,96},{128,112},... | collective-permute-start | bytes 196616 | tf_op jit(solution)/shard_map/ppermute | solution.py:68
  134.6 1.0 convolution_add_fusion
  135.7 1.0 fusion.46
  136.7 1.0 fusion.42
  137.7 4.7 %collective-permute-done.4 = bf16[1,4,64,128]{3,2,1,0:T(8,128)(2,1)S(1)} collective-permute-done((bf16[1,4,64,128]{3,2,1,0:T(8,128)(2,1)S(1)}, bf16[1,4,64,128]{3,2,1,0:T(8,128)(2,1)S(1)}, u32[]{:S(2)}, u32[]{:S(2)}) %collective-permute-start.4) | collective-permute-done | bytes 65568 | tf_op jit(solution)/shard_map/ppermute | solution.py:67
  142.6 19.5 %all-to-all-done.1 = bf16[32,2,64,128]{3,2,1,0:T(8,128)(2,1)S(1)} async-done(((bf16[32,2,64,128]{3,2,1,0:T(8,128)(2,1)}), bf16[32,2,64,128]{3,2,1,0:T(8,128)(2,1)S(1)}, u32[]{:S(2)}, u32[]{:S(2)}) %all-to-all-start.1) | async-done | bytes 1048608 | tf_op jit(solution)/shard_map/all_to_all | solution.py:214
  162.9 1.5 fusion.5
  (100 shorter events, 18.4 us)
Async XLA Ops:
  0.0 7.5 %copy-start.14 = (f32[32]{0:T(128)S(1)}, f32[32]{0:T(128)}, u32[]{:S(2)}) copy-start(f32[32]{0:T(128)} %param.18) | copy-start | bytes 388
  0.0 7.6 %copy-start.15 = (f32[32]{0:T(128)S(1)}, f32[32]{0:T(128)}, u32[]{:S(2)}) copy-start(f32[32]{0:T(128)} %param.17) | copy-start | bytes 388
  5.8 2.2 %copy-start.6 = (bf16[4,4,64,128]{3,2,1,0:T(8,128)(2,1)S(1)}, bf16[4,4,64,128]{3,2,1,0:T(8,128)(2,1)}, u32[]{:S(2)}) copy-start(bf16[4,4,64,128]{3,2,1,0:T(8,128)(2,1)} %param.14) | copy-start | bytes 786436
  8.4 1.2 copy-start.13
  14.6 1.4 copy-start.17
  18.7 14.8 %copy-start.1 = (bf16[1024,1,128]{2,0,1:T(8,128)(2,1)S(1)}, bf16[1024,1,128]{2,0,1:T(8,128)(2,1)}, u32[]{:S(2)}) copy-start(bf16[1024,1,128]{2,0,1:T(8,128)(2,1)} %copy.39) | copy-start | bytes 786436
  18.7 39.2 %copy-start.10 = (bf16[4,4,5,4096]{3,1,2,0:T(4,128)(2,1)S(1)}, bf16[4,4,5,4096]{3,1,2,0:T(4,128)(2,1)}, u32[]{:S(2)}) copy-start(bf16[4,4,5,4096]{3,1,2,0:T(4,128)(2,1)} %param.19) | copy-start | bytes 1966084
  18.7 69.1 %all-to-all-start = ((bf16[32,2,8320]{2,1,0:T(2,128)(2,1)}), bf16[32,2,8320]{2,1,0:T(2,128)(2,1)S(1)}, u32[]{:S(2)}, u32[]{:S(2)}) async-start(bf16[32,2,8320]{2,1,0:T(2,128)(2,1)} %pad_maximum_fusion), calls=%async_computation | async-start | bytes 2129920 | tf_op jit(solution)/shard_map/all_to_all | solution.py:204
  34.2 28.7 %collective-permute-start.3 = (bf16[4,1,64,128]{3,2,1,0:T(8,128)(2,1)}, bf16[4,1,64,128]{3,2,1,0:T(8,128)(2,1)}, u32[]{:S(2)}, u32[]{:S(2)}) collective-permute-start(bf16[4,1,64,128]{3,2,1,0:T(8,128)(2,1)} %get-tuple-element.30), channel_id=1, source_target_pairs={{1,0},{2,1},{3,2},{4,3},{5,4},{6,5},{7,6},{8,7},{9,8},{10,9},{11,1... | collective-permute-start | bytes 196616 | tf_op jit(solution)/shard_map/ppermute | solution.py:70
  37.3 27.6 %collective-permute-start.2 = (bf16[4,1,64,128]{3,2,1,0:T(8,128)(2,1)}, bf16[4,1,64,128]{3,2,1,0:T(8,128)(2,1)}, u32[]{:S(2)}, u32[]{:S(2)}) collective-permute-start(bf16[4,1,64,128]{3,2,1,0:T(8,128)(2,1)} %get-tuple-element.29), channel_id=1, source_target_pairs={{0,1},{1,2},{2,3},{3,4},{4,5},{5,6},{6,7},{7,8},{8,9},{9,10},{10,1... | collective-permute-start | bytes 196616 | tf_op jit(solution)/shard_map/ppermute | solution.py:69
  51.3 19.1 %collective-permute-start = (bf16[1,4,64,128]{3,2,1,0:T(8,128)(2,1)}, bf16[1,4,64,128]{3,2,1,0:T(8,128)(2,1)}, u32[]{:S(2)}, u32[]{:S(2)}) collective-permute-start(bf16[1,4,64,128]{3,2,1,0:T(8,128)(2,1)} %bitcast.11), channel_id=1, source_target_pairs={{0,16},{16,32},{32,48},{48,64},{64,80},{80,96},{96,112},{112,128},... | collective-permute-start | bytes 196616 | tf_op jit(solution)/shard_map/ppermute | solution.py:67
  55.1 36.4 %collective-permute-start.1 = (bf16[1,4,64,128]{3,2,1,0:T(8,128)(2,1)}, bf16[1,4,64,128]{3,2,1,0:T(8,128)(2,1)}, u32[]{:S(2)}, u32[]{:S(2)}) collective-permute-start(bf16[1,4,64,128]{3,2,1,0:T(8,128)(2,1)} %bitcast.15), channel_id=1, source_target_pairs={{16,0},{32,16},{48,32},{64,48},{80,64},{96,80},{112,96},{128,112},... | collective-permute-start | bytes 196616 | tf_op jit(solution)/shard_map/ppermute | solution.py:68
  62.9 7.6 %copy-start.9 = (bf16[768,1,128]{2,0,1:T(8,128)(2,1)S(1)}, bf16[768,1,128]{2,0,1:T(8,128)(2,1)}, u32[]{:S(2)}) copy-start(bf16[768,1,128]{2,0,1:T(8,128)(2,1)} %copy.42) | copy-start | bytes 589828
  89.8 1.8 %copy-start.2 = (f32[4,4,128,64]{2,3,1,0:T(8,128)S(1)}, f32[4,4,128,64]{2,3,1,0:T(8,128)}, u32[]{:S(2)}) copy-start(f32[4,4,128,64]{2,3,1,0:T(8,128)} %convolution_add_fusion.4) | copy-start | bytes 1572868
  89.8 1.8 %copy-start.4 = (f32[4,4,128,64]{2,3,1,0:T(8,128)S(1)}, f32[4,4,128,64]{2,3,1,0:T(8,128)}, u32[]{:S(2)}) copy-start(f32[4,4,128,64]{2,3,1,0:T(8,128)} %fusion.32) | copy-start | bytes 1572868
  89.8 1.8 %copy-start.5 = (f32[4,4,128,64]{2,3,1,0:T(8,128)S(1)}, f32[4,4,128,64]{2,3,1,0:T(8,128)}, u32[]{:S(2)}) copy-start(f32[4,4,128,64]{2,3,1,0:T(8,128)} %fusion.28) | copy-start | bytes 1572868
  96.7 15.1 %copy-start.12 = (bf16[4,32,4,32]{3,2,1,0:T(4,128)(2,1)S(1)}, bf16[4,32,4,32]{3,2,1,0:T(4,128)(2,1)}, u32[]{:S(2)}) copy-start(bf16[4,32,4,32]{3,2,1,0:T(4,128)(2,1)} %get-tuple-element.48) | copy-start | bytes 98308
  96.7 15.2 %copy-start.11 = (bf16[4,32,4,32]{3,2,1,0:T(4,128)(2,1)S(1)}, bf16[4,32,4,32]{3,2,1,0:T(4,128)(2,1)}, u32[]{:S(2)}) copy-start(bf16[4,32,4,32]{3,2,1,0:T(4,128)(2,1)} %get-tuple-element.47) | copy-start | bytes 98308
  96.7 15.3 %copy-start.8 = (f32[4,32,4,32]{3,2,1,0:T(4,128)S(1)}, f32[4,32,4,32]{3,2,1,0:T(4,128)}, u32[]{:S(2)}) copy-start(f32[4,32,4,32]{3,2,1,0:T(4,128)} %get-tuple-element.46) | copy-start | bytes 196612
  96.7 15.5 %copy-start.16 = (f32[32]{0:T(128)S(1)}, f32[32]{0:T(128)}, u32[]{:S(2)}) copy-start(f32[32]{0:T(128)} %param.25) | copy-start | bytes 388
  96.7 15.9 %copy-start = (bf16[4,4,64,128]{3,2,1,0:T(8,128)(2,1)S(1)}, bf16[4,4,64,128]{3,2,1,0:T(8,128)(2,1)}, u32[]{:S(2)}) copy-start(bf16[4,4,64,128]{3,2,1,0:T(8,128)(2,1)} %fusion.11) | copy-start | bytes 786436
  96.7 65.5 %all-to-all-start.1 = ((bf16[32,2,64,128]{3,2,1,0:T(8,128)(2,1)}), bf16[32,2,64,128]{3,2,1,0:T(8,128)(2,1)S(1)}, u32[]{:S(2)}, u32[]{:S(2)}) async-start(bf16[32,2,64,128]{3,2,1,0:T(8,128)(2,1)} %bitcast.120), calls=%async_computation.1 | async-start | bytes 2097152 | tf_op jit(solution)/shard_map/all_to_all | solution.py:214
  112.6 23.1 %collective-permute-start.7 = (bf16[4,1,64,128]{3,2,1,0:T(8,128)(2,1)S(1)}, bf16[4,1,64,128]{3,2,1,0:T(8,128)(2,1)S(1)}, u32[]{:S(2)}, u32[]{:S(2)}) collective-permute-start(bf16[4,1,64,128]{3,2,1,0:T(8,128)(2,1)S(1)} %get-tuple-element.22), channel_id=1, source_target_pairs={{1,0},{2,1},{3,2},{4,3},{5,4},{6,5},{7,6},{8,7},{9,8},{10,9},{11,1... | collective-permute-start | bytes 196616 | tf_op jit(solution)/shard_map/ppermute | solution.py:70
  114.5 22.2 %collective-permute-start.6 = (bf16[4,1,64,128]{3,2,1,0:T(8,128)(2,1)S(1)}, bf16[4,1,64,128]{3,2,1,0:T(8,128)(2,1)S(1)}, u32[]{:S(2)}, u32[]{:S(2)}) collective-permute-start(bf16[4,1,64,128]{3,2,1,0:T(8,128)(2,1)S(1)} %get-tuple-element.21), channel_id=1, source_target_pairs={{0,1},{1,2},{2,3},{3,4},{4,5},{5,6},{6,7},{7,8},{8,9},{9,10},{10,1... | collective-permute-start | bytes 196616 | tf_op jit(solution)/shard_map/ppermute | solution.py:69
  129.0 13.4 %collective-permute-start.4 = (bf16[1,4,64,128]{3,2,1,0:T(8,128)(2,1)S(1)}, bf16[1,4,64,128]{3,2,1,0:T(8,128)(2,1)S(1)}, u32[]{:S(2)}, u32[]{:S(2)}) collective-permute-start(bf16[1,4,64,128]{3,2,1,0:T(8,128)(2,1)S(1)} %get-tuple-element.20), channel_id=1, source_target_pairs={{0,16},{16,32},{32,48},{48,64},{64,80},{80,96},{96,112},{112,128},... | collective-permute-start | bytes 196616 | tf_op jit(solution)/shard_map/ppermute | solution.py:67
  132.1 30.8 %collective-permute-start.5 = (bf16[1,4,64,128]{3,2,1,0:T(8,128)(2,1)S(1)}, bf16[1,4,64,128]{3,2,1,0:T(8,128)(2,1)S(1)}, u32[]{:S(2)}, u32[]{:S(2)}) collective-permute-start(bf16[1,4,64,128]{3,2,1,0:T(8,128)(2,1)S(1)} %get-tuple-element.19), channel_id=1, source_target_pairs={{16,0},{32,16},{48,32},{64,48},{80,64},{96,80},{112,96},{128,112},... | collective-permute-start | bytes 196616 | tf_op jit(solution)/shard_map/ppermute | solution.py:68
  162.9 1.5 copy-start.3
  164.4 1.0 copy-start.7

commit v8 on v7

--- a/solution.py
+++ b/solution.py
@@ -159,6 +159,19 @@
     return payload.reshape(lax.axis_size("rx"), CAP, -1)
 
 
+def send_products_xla(signal, edge_tiles, sources, select, target_col):
+    block_rows, block_cols, block_size, features = signal.shape
+    flat = signal.reshape(block_rows * block_cols, block_size, features)
+    products = jnp.einsum(
+        "eab,ebf->eaf", edge_tiles, flat[sources], preferred_element_type=jnp.float32
+    ).astype(jnp.bfloat16)
+    products = jnp.concatenate([products.reshape(products.shape[0], -1), target_col], axis=1)
+    slots = jnp.einsum(
+        "es,ek->sk", select, products, preferred_element_type=jnp.float32
+    ).astype(jnp.bfloat16)
+    return slots.reshape(lax.axis_size("rx"), CAP, -1)
+
+
 def far_terms(received, targets, nblocks):
     received = received.reshape(targets.shape[0], -1)
     onehot = (targets[None, :] == jnp.arange(nblocks, dtype=jnp.int32)[:, None]).astype(
@@ -199,7 +212,7 @@
         (out_target.reshape(-1) + 1).astype(jnp.bfloat16)
     )
 
-    send_one = send_products(gated, edge_tiles, sources, slots, select, target_col)
+    send_one = send_products_xla(gated, edge_tiles, sources, select, target_col)
     halo_one = fetch_halo(gated)
     recv_one = lax.all_to_all(send_one, "rx", split_axis=0, concat_axis=0, tiled=True)
     recv_one = recv_one.reshape(n_rx * CAP, -1)

time: 167 us -> 158 us (0.946)
  other arithmetic: 11.4 us -> 7.01 us
  Pallas kernels: 6.64 us -> 3.31 us
    pallas_call x2 -> x1, Pallas kernels: 6.64 us -> 3.31 us  [send_products(): pl.pallas_call(product_kernel, out_shape=jax.ShapeDtypeStruct((nslots, bl...]
    concatenate x1 -> x0, other arithmetic: 2.01 us -> none  [send_products(): jnp.concatenate([products.reshape(nslots, -1), slot_targets], axis=1)]
where the time goes in v8:
time: 158 us; the launch traced here: 157 us
  starting transfers between devices  72.6 us (46%)
  waiting for transfers between devices  43.5 us (28%)
  matrix products  15.6 us (10%)
  local copies, waits for them, and re-layouts  14.2 us (9%)
  other arithmetic  7.01 us (4%)
  Pallas kernels  3.31 us (2%)
    ppermute x2, starting transfers between devices, fetch_halo(): left = lax.ppermute(signal[:, -1:], 'ry', shift_pairs(n_ry, 1))  27.7 us
    all_to_all x1, waiting for transfers between devices, local(): lax.all_to_all(send_two, 'rx', split_axis=0, concat_axis=0, tiled=True)  19.5 us
    all_to_all x1, waiting for transfers between devices, local(): lax.all_to_all(send_one, 'rx', split_axis=0, concat_axis=0, tiled=True)  16.4 us
    all_to_all x1, starting transfers between devices, local(): lax.all_to_all(send_one, 'rx', split_axis=0, concat_axis=0, tiled=True)  14.9 us
    all_to_all x1, starting transfers between devices, local(): lax.all_to_all(send_two, 'rx', split_axis=0, concat_axis=0, tiled=True)  13.9 us
    dot_general x8, matrix products, local_terms(): jnp.einsum('ijab,ijbf->ijaf', tiles[:, :, offset], neighbours[offset], pr...  10.3 us
    ppermute x2, waiting for transfers between devices, fetch_halo(): above = lax.ppermute(signal[-1:], 'rx', shift_pairs(n_rx, 1))  7.64 us
    ppermute x2, starting transfers between devices, fetch_halo(): above = lax.ppermute(signal[-1:], 'rx', shift_pairs(n_rx, 1))  6.17 us
  transfers between devices with their start and end apart: 10, of which 4 were waited for; matrix products, arithmetic and copies ran while one was open for 13% of the time, Pallas kernels for 0%

profile of v8, /device:TPU:57, one launch (start us, length us, event | category | flops | bytes accessed | tf_op | source)
XLA Modules:
  0.0 156.9 jit_solution(3689066231548025922)
XLA Ops:
  3.0 1.3 add_convert_fusion.1
  6.2 0.8 reshape.389.tile_ref
  10.4 1.2 reshape.392
  11.7 14.9 %all-to-all-start = ((bf16[32,2,8320]{2,1,0:T(2,128)(2,1)}), bf16[32,2,8320]{2,1,0:T(2,128)(2,1)}, u32[]{:S(2)}, u32[]{:S(2)}) async-start(bf16[32,2,8320]{2,1,0:T(2,128)(2,1)} %reshape.392), calls=%async_computation | async-start | bytes 2129920 | tf_op jit(solution)/shard_map/all_to_all | solution.py:217
  27.2 3.1 %collective-permute-start.3 = (bf16[4,1,64,128]{3,2,1,0:T(8,128)(2,1)}, bf16[4,1,64,128]{3,2,1,0:T(8,128)(2,1)}, u32[]{:S(2)}, u32[]{:S(2)}) collective-permute-start(bf16[4,1,64,128]{3,2,1,0:T(8,128)(2,1)} %get-tuple-element.30), channel_id=1, source_target_pairs={{1,0},{2,1},{3,2},{4,3},{5,4},{6,5},{7,6},{8,7},{9,8},{10,9},{11,1... | collective-permute-start | bytes 196616 | tf_op jit(solution)/shard_map/ppermute | solution.py:70
  30.3 13.2 %collective-permute-start.2 = (bf16[4,1,64,128]{3,2,1,0:T(8,128)(2,1)}, bf16[4,1,64,128]{3,2,1,0:T(8,128)(2,1)}, u32[]{:S(2)}, u32[]{:S(2)}) collective-permute-start(bf16[4,1,64,128]{3,2,1,0:T(8,128)(2,1)} %get-tuple-element.29), channel_id=1, source_target_pairs={{0,1},{1,2},{2,3},{3,4},{4,5},{5,6},{6,7},{7,8},{8,9},{9,10},{10,1... | collective-permute-start | bytes 196616 | tf_op jit(solution)/shard_map/ppermute | solution.py:69
  44.3 3.1 %collective-permute-start = (bf16[1,4,64,128]{3,2,1,0:T(8,128)(2,1)}, bf16[1,4,64,128]{3,2,1,0:T(8,128)(2,1)}, u32[]{:S(2)}, u32[]{:S(2)}) collective-permute-start(bf16[1,4,64,128]{3,2,1,0:T(8,128)(2,1)} %bitcast.11), channel_id=1, source_target_pairs={{0,16},{16,32},{32,48},{48,64},{64,80},{80,96},{96,112},{112,128},... | collective-permute-start | bytes 196616 | tf_op jit(solution)/shard_map/ppermute | solution.py:67
  48.1 2.8 %collective-permute-start.1 = (bf16[1,4,64,128]{3,2,1,0:T(8,128)(2,1)}, bf16[1,4,64,128]{3,2,1,0:T(8,128)(2,1)}, u32[]{:S(2)}, u32[]{:S(2)}) collective-permute-start(bf16[1,4,64,128]{3,2,1,0:T(8,128)(2,1)} %bitcast.15), channel_id=1, source_target_pairs={{16,0},{32,16},{48,32},{64,48},{80,64},{96,80},{112,96},{128,112},... | collective-permute-start | bytes 196616 | tf_op jit(solution)/shard_map/ppermute | solution.py:68
  51.3 1.0 reshape.387
  53.4 0.8 copy.44
  54.2 1.8 %fusion.39 = f32[4,4,128,64]{2,3,1,0:T(8,128)} fusion(bf16[4,1,64,128]{3,2,1,0:T(8,128)(2,1)} %collective-permute-done.3, bf16[4,3,64,128]{3,2,1,0:T(8,128)(2,1)S(1)} %get-tuple-element.32, bf16[4,4,5,64,64]{4,3,1,0,2:T(8,128)(2,1)S(1)} %reshape.387), kind=kOutput, calls=%fused_computation.61 | convolution fusion | flops 17301504 | bytes 1048576 | tf_op jit(solution)/shard_map/ijab,ijbf->ijaf/dot_general | solution.py:87
  56.0 1.9 %fusion.35 = f32[4,4,128,64]{2,3,1,0:T(8,128)} fusion(bf16[4,3,64,128]{3,2,1,0:T(8,128)(2,1)S(1)} %get-tuple-element.31, bf16[4,1,64,128]{3,2,1,0:T(8,128)(2,1)} %collective-permute-done.2, bf16[4,4,5,64,64]{4,3,1,0,2:T(8,128)(2,1)S(1)} %reshape.387), kind=kOutput, calls=%fused_computation.57 | convolution fusion | flops 17301504 | bytes 1048576 | tf_op jit(solution)/shard_map/ijab,ijbf->ijaf/dot_general | solution.py:87
  57.9 5.6 %collective-permute-done = bf16[1,4,64,128]{3,2,1,0:T(8,128)(2,1)} collective-permute-done((bf16[1,4,64,128]{3,2,1,0:T(8,128)(2,1)}, bf16[1,4,64,128]{3,2,1,0:T(8,128)(2,1)}, u32[]{:S(2)}, u32[]{:S(2)}) %collective-permute-start) | collective-permute-done | bytes 65568 | tf_op jit(solution)/shard_map/ppermute | solution.py:67
  63.4 1.0 convolution_add_fusion.4
  64.5 16.4 %all-to-all-done = bf16[32,2,8320]{2,1,0:T(2,128)(2,1)} async-done(((bf16[32,2,8320]{2,1,0:T(2,128)(2,1)}), bf16[32,2,8320]{2,1,0:T(2,128)(2,1)}, u32[]{:S(2)}, u32[]{:S(2)}) %all-to-all-start) | async-done | bytes 1064992 | tf_op jit(solution)/shard_map/all_to_all | solution.py:217
  80.8 1.5 reshape.393
  83.7 1.8 %fusion.12 = bf16[4,4,64,128]{3,2,1,0:T(8,128)(2,1)} fusion(f32[4,4,64,128]{3,2,1,0:T(8,128)S(1)} %bitcast.133, f32[4,4,128,64]{2,3,1,0:T(8,128)S(1)} %copy-done.3, f32[4,4,128,64]{2,3,1,0:T(8,128)S(1)} %copy-done.4, f32[4,4,128,64]{2,3,1,0:T(8,128)S(1)} %convolution_add_fusion.4, bf16[1,4,64,128]{3,2,1,0:T(8,128)(2,1)} %collective-permute-done.1, ...), kind=kOutput, calls=%fused_computation.24 | convolution fusion | flops 17956864 | bytes 2883584 | tf_op jit(solution)/shard_map/ijab,ijbf->ijaf/dot_general | solution.py:87
  85.5 3.3 %shard_map.118 = bf16[64,64,128]{2,1,0:T(8,128)(2,1)} custom-call(s32[48]{0:T(128)} %bitcast.142, s32[48]{0:T(128)} %multiply_add_fusion.1.slot_ref, bf16[16,64,128]{2,1,0:T(8,128)(2,1)} %bitcast.123, bf16[48,64,64]{2,1,0:T(8,128)(2,1)} %copy-done.1), custom_call_target="tpu_custom_call" | custom-call | flops 50331648 | bytes 1703936 | tf_op jit(solution)/shard_map/pallas_call | solution.py:134
  88.8 13.9 %all-to-all-start.1 = ((bf16[32,2,64,128]{3,2,1,0:T(8,128)(2,1)}), bf16[32,2,64,128]{3,2,1,0:T(8,128)(2,1)S(1)}, u32[]{:S(2)}, u32[]{:S(2)}) async-start(bf16[32,2,64,128]{3,2,1,0:T(8,128)(2,1)} %bitcast.130), calls=%async_computation.1 | async-start | bytes 2097152 | tf_op jit(solution)/shard_map/all_to_all | solution.py:227
  102.7 1.6 %convert_element_type.140 = bf16[128,128]{1,0:T(8,128)(2,1)} reshape(bf16[4,32,4,32]{3,2,1,0:T(4,128)(2,1)} %get-tuple-element.48) | data formatting | bytes 65536 | tf_op jit(solution)/shard_map/convert_element_type | solution.py:235
  105.3 1.0 fusion.57
  106.4 1.9 %collective-permute-start.7 = (bf16[4,1,64,128]{3,2,1,0:T(8,128)(2,1)S(1)}, bf16[4,1,64,128]{3,2,1,0:T(8,128)(2,1)S(1)}, u32[]{:S(2)}, u32[]{:S(2)}) collective-permute-start(bf16[4,1,64,128]{3,2,1,0:T(8,128)(2,1)S(1)} %get-tuple-element.22), channel_id=1, source_target_pairs={{1,0},{2,1},{3,2},{4,3},{5,4},{6,5},{7,6},{8,7},{9,8},{10,9},{11,1... | collective-permute-start | bytes 196616 | tf_op jit(solution)/shard_map/ppermute | solution.py:70
  108.3 14.5 %collective-permute-start.6 = (bf16[4,1,64,128]{3,2,1,0:T(8,128)(2,1)S(1)}, bf16[4,1,64,128]{3,2,1,0:T(8,128)(2,1)S(1)}, u32[]{:S(2)}, u32[]{:S(2)}) collective-permute-start(bf16[4,1,64,128]{3,2,1,0:T(8,128)(2,1)S(1)} %get-tuple-element.21), channel_id=1, source_target_pairs={{0,1},{1,2},{2,3},{3,4},{4,5},{5,6},{6,7},{7,8},{8,9},{9,10},{10,1... | collective-permute-start | bytes 196616 | tf_op jit(solution)/shard_map/ppermute | solution.py:69
  122.8 3.1 %collective-permute-start.4 = (bf16[1,4,64,128]{3,2,1,0:T(8,128)(2,1)S(1)}, bf16[1,4,64,128]{3,2,1,0:T(8,128)(2,1)S(1)}, u32[]{:S(2)}, u32[]{:S(2)}) collective-permute-start(bf16[1,4,64,128]{3,2,1,0:T(8,128)(2,1)S(1)} %get-tuple-element.20), channel_id=1, source_target_pairs={{0,16},{16,32},{32,48},{48,64},{64,80},{80,96},{96,112},{112,128},... | collective-permute-start | bytes 196616 | tf_op jit(solution)/shard_map/ppermute | solution.py:67
  125.9 2.2 %collective-permute-start.5 = (bf16[1,4,64,128]{3,2,1,0:T(8,128)(2,1)S(1)}, bf16[1,4,64,128]{3,2,1,0:T(8,128)(2,1)S(1)}, u32[]{:S(2)}, u32[]{:S(2)}) collective-permute-start(bf16[1,4,64,128]{3,2,1,0:T(8,128)(2,1)S(1)} %get-tuple-element.19), channel_id=1, source_target_pairs={{16,0},{32,16},{48,32},{64,48},{80,64},{96,80},{112,96},{128,112},... | collective-permute-start | bytes 196616 | tf_op jit(solution)/shard_map/ppermute | solution.py:68
  128.4 1.0 convolution_add_fusion
  129.4 1.0 fusion.53
  130.5 1.0 fusion.49
  131.5 2.1 %collective-permute-done.4 = bf16[1,4,64,128]{3,2,1,0:T(8,128)(2,1)S(1)} collective-permute-done((bf16[1,4,64,128]{3,2,1,0:T(8,128)(2,1)S(1)}, bf16[1,4,64,128]{3,2,1,0:T(8,128)(2,1)S(1)}, u32[]{:S(2)}, u32[]{:S(2)}) %collective-permute-start.4) | collective-permute-done | bytes 65568 | tf_op jit(solution)/shard_map/ppermute | solution.py:67
  133.8 19.5 %all-to-all-done.1 = bf16[32,2,64,128]{3,2,1,0:T(8,128)(2,1)S(1)} async-done(((bf16[32,2,64,128]{3,2,1,0:T(8,128)(2,1)}), bf16[32,2,64,128]{3,2,1,0:T(8,128)(2,1)S(1)}, u32[]{:S(2)}, u32[]{:S(2)}) %all-to-all-start.1) | async-done | bytes 1048608 | tf_op jit(solution)/shard_map/all_to_all | solution.py:227
  154.1 1.5 fusion.6
  156.1 0.8 add_convert_fusion
  (106 shorter events, 15.7 us)
Async XLA Ops:
  0.0 4.8 %copy-start.14 = (f32[32]{0:T(128)S(1)}, f32[32]{0:T(128)}, u32[]{:S(2)}) copy-start(f32[32]{0:T(128)} %param.18) | copy-start | bytes 388
  0.0 4.9 %copy-start.15 = (f32[32]{0:T(128)S(1)}, f32[32]{0:T(128)}, u32[]{:S(2)}) copy-start(f32[32]{0:T(128)} %param.17) | copy-start | bytes 388
  0.0 5.0 %copy-start.13 = (s32[1,1,48,1]{2,3,1,0:T(1,128)S(1)}, s32[1,1,48,1]{2,3,1,0:T(1,128)}, u32[]{:S(2)}) copy-start(s32[1,1,48,1]{2,3,1,0:T(1,128)} %param.21) | copy-start | bytes 580
  0.0 5.4 %copy-start.18 = (s32[1,1,48]{2,1,0:T(1,128)S(1)}, s32[1,1,48]{2,1,0:T(1,128)}, u32[]{:S(2)}) copy-start(s32[1,1,48]{2,1,0:T(1,128)} %param.22) | copy-start | bytes 580
  0.0 6.2 %copy-start.9 = (bf16[1,1,48,4096]{3,2,1,0:T(8,128)(2,1)S(1)}, bf16[1,1,48,4096]{3,2,1,0:T(8,128)(2,1)}, u32[]{:S(2)}) copy-start(bf16[1,1,48,4096]{3,2,1,0:T(8,128)(2,1)} %param.23) | copy-start | bytes 1179652
  4.6 2.7 %copy-start.5 = (bf16[4,4,64,128]{3,2,1,0:T(8,128)(2,1)S(1)}, bf16[4,4,64,128]{3,2,1,0:T(8,128)(2,1)}, u32[]{:S(2)}) copy-start(bf16[4,4,64,128]{3,2,1,0:T(8,128)(2,1)} %param.14) | copy-start | bytes 786436
  7.1 2.0 %copy-start.1 = (bf16[48,64,64]{2,1,0:T(8,128)(2,1)}, bf16[48,64,64]{2,1,0:T(8,128)(2,1)S(1)}, u32[]{:S(2)}) copy-start(bf16[48,64,64]{2,1,0:T(8,128)(2,1)S(1)} %reshape.389.tile_ref) | copy-start | bytes 1179652
  7.7 0.7 copy-start.17
  11.7 39.3 %copy-start.8 = (bf16[4,4,5,4096]{3,1,2,0:T(4,128)(2,1)S(1)}, bf16[4,4,5,4096]{3,1,2,0:T(4,128)(2,1)}, u32[]{:S(2)}) copy-start(bf16[4,4,5,4096]{3,1,2,0:T(4,128)(2,1)} %param.19) | copy-start | bytes 1966084
  11.7 69.2 %all-to-all-start = ((bf16[32,2,8320]{2,1,0:T(2,128)(2,1)}), bf16[32,2,8320]{2,1,0:T(2,128)(2,1)}, u32[]{:S(2)}, u32[]{:S(2)}) async-start(bf16[32,2,8320]{2,1,0:T(2,128)(2,1)} %reshape.392), calls=%async_computation | async-start | bytes 2129920 | tf_op jit(solution)/shard_map/all_to_all | solution.py:217
  27.2 27.0 %collective-permute-start.3 = (bf16[4,1,64,128]{3,2,1,0:T(8,128)(2,1)}, bf16[4,1,64,128]{3,2,1,0:T(8,128)(2,1)}, u32[]{:S(2)}, u32[]{:S(2)}) collective-permute-start(bf16[4,1,64,128]{3,2,1,0:T(8,128)(2,1)} %get-tuple-element.30), channel_id=1, source_target_pairs={{1,0},{2,1},{3,2},{4,3},{5,4},{6,5},{7,6},{8,7},{9,8},{10,9},{11,1... | collective-permute-start | bytes 196616 | tf_op jit(solution)/shard_map/ppermute | solution.py:70
  30.3 25.7 %collective-permute-start.2 = (bf16[4,1,64,128]{3,2,1,0:T(8,128)(2,1)}, bf16[4,1,64,128]{3,2,1,0:T(8,128)(2,1)}, u32[]{:S(2)}, u32[]{:S(2)}) collective-permute-start(bf16[4,1,64,128]{3,2,1,0:T(8,128)(2,1)} %get-tuple-element.29), channel_id=1, source_target_pairs={{0,1},{1,2},{2,3},{3,4},{4,5},{5,6},{6,7},{7,8},{8,9},{9,10},{10,1... | collective-permute-start | bytes 196616 | tf_op jit(solution)/shard_map/ppermute | solution.py:69
  44.3 19.1 %collective-permute-start = (bf16[1,4,64,128]{3,2,1,0:T(8,128)(2,1)}, bf16[1,4,64,128]{3,2,1,0:T(8,128)(2,1)}, u32[]{:S(2)}, u32[]{:S(2)}) collective-permute-start(bf16[1,4,64,128]{3,2,1,0:T(8,128)(2,1)} %bitcast.11), channel_id=1, source_target_pairs={{0,16},{16,32},{32,48},{48,64},{64,80},{80,96},{96,112},{112,128},... | collective-permute-start | bytes 196616 | tf_op jit(solution)/shard_map/ppermute | solution.py:67
  48.1 34.8 %collective-permute-start.1 = (bf16[1,4,64,128]{3,2,1,0:T(8,128)(2,1)}, bf16[1,4,64,128]{3,2,1,0:T(8,128)(2,1)}, u32[]{:S(2)}, u32[]{:S(2)}) collective-permute-start(bf16[1,4,64,128]{3,2,1,0:T(8,128)(2,1)} %bitcast.15), channel_id=1, source_target_pairs={{16,0},{32,16},{48,32},{64,48},{80,64},{96,80},{112,96},{128,112},... | collective-permute-start | bytes 196616 | tf_op jit(solution)/shard_map/ppermute | solution.py:68
  82.4 0.5 copy-start.11
  82.4 1.0 copy-start.3
  82.5 1.2 copy-start.4
  82.5 1.2 copy-start.7
  88.8 16.3 %copy-start.6 = (f32[4,32,4,32]{3,2,1,0:T(4,128)S(1)}, f32[4,32,4,32]{3,2,1,0:T(4,128)}, u32[]{:S(2)}) copy-start(f32[4,32,4,32]{3,2,1,0:T(4,128)} %get-tuple-element.46) | copy-start | bytes 196612
  88.8 16.4 %copy-start.16 = (f32[32]{0:T(128)S(1)}, f32[32]{0:T(128)}, u32[]{:S(2)}) copy-start(f32[32]{0:T(128)} %param.25) | copy-start | bytes 388
  88.8 17.5 %copy-start = (bf16[4,4,64,128]{3,2,1,0:T(8,128)(2,1)S(1)}, bf16[4,4,64,128]{3,2,1,0:T(8,128)(2,1)}, u32[]{:S(2)}) copy-start(bf16[4,4,64,128]{3,2,1,0:T(8,128)(2,1)} %fusion.12) | copy-start | bytes 786436
  88.8 64.5 %all-to-all-start.1 = ((bf16[32,2,64,128]{3,2,1,0:T(8,128)(2,1)}), bf16[32,2,64,128]{3,2,1,0:T(8,128)(2,1)S(1)}, u32[]{:S(2)}, u32[]{:S(2)}) async-start(bf16[32,2,64,128]{3,2,1,0:T(8,128)(2,1)} %bitcast.130), calls=%async_computation.1 | async-start | bytes 2097152 | tf_op jit(solution)/shard_map/all_to_all | solution.py:227
  106.3 22.0 %copy-start.10 = (bf16[128,128]{1,0:T(8,128)(2,1)S(1)}, bf16[128,128]{1,0:T(8,128)(2,1)}, u32[]{:S(2)}) copy-start(bf16[128,128]{1,0:T(8,128)(2,1)} %convert_element_type.152) | copy-start | bytes 98308
  106.4 23.1 %collective-permute-start.7 = (bf16[4,1,64,128]{3,2,1,0:T(8,128)(2,1)S(1)}, bf16[4,1,64,128]{3,2,1,0:T(8,128)(2,1)S(1)}, u32[]{:S(2)}, u32[]{:S(2)}) collective-permute-start(bf16[4,1,64,128]{3,2,1,0:T(8,128)(2,1)S(1)} %get-tuple-element.22), channel_id=1, source_target_pairs={{1,0},{2,1},{3,2},{4,3},{5,4},{6,5},{7,6},{8,7},{9,8},{10,9},{11,1... | collective-permute-start | bytes 196616 | tf_op jit(solution)/shard_map/ppermute | solution.py:70
  108.3 22.2 %collective-permute-start.6 = (bf16[4,1,64,128]{3,2,1,0:T(8,128)(2,1)S(1)}, bf16[4,1,64,128]{3,2,1,0:T(8,128)(2,1)S(1)}, u32[]{:S(2)}, u32[]{:S(2)}) collective-permute-start(bf16[4,1,64,128]{3,2,1,0:T(8,128)(2,1)S(1)} %get-tuple-element.21), channel_id=1, source_target_pairs={{0,1},{1,2},{2,3},{3,4},{4,5},{5,6},{6,7},{7,8},{8,9},{9,10},{10,1... | collective-permute-start | bytes 196616 | tf_op jit(solution)/shard_map/ppermute | solution.py:69
  122.8 10.8 %collective-permute-start.4 = (bf16[1,4,64,128]{3,2,1,0:T(8,128)(2,1)S(1)}, bf16[1,4,64,128]{3,2,1,0:T(8,128)(2,1)S(1)}, u32[]{:S(2)}, u32[]{:S(2)}) collective-permute-start(bf16[1,4,64,128]{3,2,1,0:T(8,128)(2,1)S(1)} %get-tuple-element.20), channel_id=1, source_target_pairs={{0,16},{16,32},{32,48},{48,64},{64,80},{80,96},{96,112},{112,128},... | collective-permute-start | bytes 196616 | tf_op jit(solution)/shard_map/ppermute | solution.py:67
  125.9 28.2 %collective-permute-start.5 = (bf16[1,4,64,128]{3,2,1,0:T(8,128)(2,1)S(1)}, bf16[1,4,64,128]{3,2,1,0:T(8,128)(2,1)S(1)}, u32[]{:S(2)}, u32[]{:S(2)}) collective-permute-start(bf16[1,4,64,128]{3,2,1,0:T(8,128)(2,1)S(1)} %get-tuple-element.19), channel_id=1, source_target_pairs={{16,0},{32,16},{48,32},{64,48},{80,64},{96,80},{112,96},{128,112},... | collective-permute-start | bytes 196616 | tf_op jit(solution)/shard_map/ppermute | solution.py:68
  130.5 22.9 %copy-start.12 = (s32[64]{0:T(128)S(1)}, s32[64]{0:T(128)}, u32[]{:S(2)}) copy-start(s32[64]{0:T(128)} %copy-done.11) | copy-start | bytes 772
  154.1 1.5 copy-start.2

commit v9 on v8

--- a/solution.py
+++ b/solution.py
@@ -19,24 +19,22 @@
 def time_tables(w_filter, w_gate, channels):
     group_members = 128 // channels
     input_signals, output_signals = group_eye(channels)
-    diagonal = (input_signals == output_signals).astype(jnp.float32)
-    within_group = (input_signals == output_signals - DILATION_STEP).astype(jnp.float32)
+    diagonal = (input_signals == output_signals).astype(jnp.bfloat16)
+    within_group = (input_signals == output_signals - DILATION_STEP).astype(jnp.bfloat16)
     across_groups = (input_signals == output_signals - DILATION_STEP + group_members).astype(
-        jnp.float32
-    )
-    filter_taps = w_filter.astype(jnp.float32)
-    gate_taps = w_gate.astype(jnp.float32)
+        jnp.bfloat16
+    )
     current_tab = jnp.concatenate(
         [
-            jnp.kron(diagonal, filter_taps[1]) + jnp.kron(within_group, filter_taps[0]),
-            jnp.kron(diagonal, gate_taps[1]) + jnp.kron(within_group, gate_taps[0]),
+            jnp.kron(diagonal, w_filter[1]) + jnp.kron(within_group, w_filter[0]),
+            jnp.kron(diagonal, w_gate[1]) + jnp.kron(within_group, w_gate[0]),
         ],
         axis=1,
     )
     earlier_tab = jnp.concatenate(
-        [jnp.kron(across_groups, filter_taps[0]), jnp.kron(across_groups, gate_taps[0])], axis=1
-    )
-    return (current_tab.astype(jnp.bfloat16), earlier_tab.astype(jnp.bfloat16))
+        [jnp.kron(across_groups, w_filter[0]), jnp.kron(across_groups, w_gate[0])], axis=1
+    )
+    return (current_tab, earlier_tab)
 
 
 def gated_units(cell_input, current_tab, earlier_tab, bias_filter, bias_gate):
@@ -173,11 +171,12 @@
 
 
 def far_terms(received, targets, nblocks):
-    received = received.reshape(targets.shape[0], -1)
-    onehot = (targets[None, :] == jnp.arange(nblocks, dtype=jnp.int32)[:, None]).astype(
+    senders, cap = received.shape[0], received.shape[1]
+    received = received.reshape(senders, cap, -1)
+    onehot = (targets[None] == jnp.arange(nblocks, dtype=jnp.int32)[:, None, None]).astype(
         jnp.bfloat16
     )
-    return jnp.einsum("ns,sk->nk", onehot, received, preferred_element_type=jnp.float32)
+    return jnp.einsum("nrc,rck->nk", onehot, received, preferred_element_type=jnp.float32)
 
 
 def local(
@@ -215,9 +214,8 @@
     send_one = send_products_xla(gated, edge_tiles, sources, select, target_col)
     halo_one = fetch_halo(gated)
     recv_one = lax.all_to_all(send_one, "rx", split_axis=0, concat_axis=0, tiled=True)
-    recv_one = recv_one.reshape(n_rx * CAP, -1)
-    targets = recv_one[:, block_len].astype(jnp.int32) - 1
-    recv_one = recv_one[:, :block_len]
+    targets = recv_one[:, :, block_len].astype(jnp.int32) - 1
+    recv_one = recv_one[:, :, :block_len]
     near_one = local_terms(gated, tiles, halo_one)
     far_one = far_terms(recv_one, targets, nblocks)
     first_hop = (near_one + far_one.reshape(gated.shape)).astype(jnp.bfloat16)
@@ -232,8 +230,8 @@
     input_signals, output_signals = group_eye(channels)
     diagonal = (input_signals == output_signals).astype(jnp.float32)
     mix_weights = w_mix.astype(jnp.float32)
-    table_zero = jnp.kron(diagonal, mix_weights[0]).astype(jnp.bfloat16)
-    table_one = jnp.kron(diagonal, mix_weights[1]).astype(jnp.bfloat16)
+    table_zero = jnp.kron(diagonal.astype(jnp.bfloat16), w_mix[0])
+    table_one = jnp.kron(diagonal.astype(jnp.bfloat16), w_mix[1])
     table_two = jnp.kron(diagonal, mix_weights[2])
     grouped_shape = (nblocks * block_size, features // 128, 128)
     mixture = jnp.einsum(

time: 158 us -> 157 us (level)
  waiting for transfers between devices: 43.5 us -> 60.7 us
  starting transfers between devices: 72.6 us -> 59.6 us
  matrix products: 15.6 us -> 11.6 us
  other arithmetic: 7.01 us -> 3.95 us
  local copies, waits for them, and re-layouts: 14.2 us -> 16.6 us
    ppermute x2, waiting for transfers between devices: 0.01 us -> 18.1 us  [fetch_halo(): right = lax.ppermute(signal[:, :1], 'ry', shift_pairs(n_ry, -1))]
    ppermute x2, starting transfers between devices: 27.7 us -> 19 us  [fetch_halo(): left = lax.ppermute(signal[:, -1:], 'ry', shift_pairs(n_ry, 1))]
    dot_general x8, matrix products: 10.3 us -> 6.48 us  [local_terms(): jnp.einsum('ijab,ijbf->ijaf', tiles[:, :, offset], neighbours[offset], pr...]
    slice x0 -> x2, local copies, waits for them, and re-layouts: none -> 2.8 us  [the longest x1 2.07 us: local(): recv_one = recv_one[:, :, :block_len]]
    all_to_all x1, starting transfers between devices: 13.9 us -> 11.2 us  [local(): lax.all_to_all(send_two, 'rx', split_axis=0, concat_axis=0, tiled=True)]
    convert_element_type x2 -> x0, local copies, waits for them, and re-layouts: 2.37 us -> none  [the longest x1 1.65 us: local(): table_zero = jnp.kron(diagonal, mix_weights[0]).astype(jnp.bfloat16)]
    convert_element_type x4 -> x3, other arithmetic: 2.19 us -> 0.02 us  [the longest x1 0.01 us: local(): table_zero = jnp.kron(diagonal.astype(jnp.bfloat16), w_mix[0])]
    ppermute x2, waiting for transfers between devices: 7.64 us -> 5.82 us  [fetch_halo(): above = lax.ppermute(signal[-1:], 'rx', shift_pairs(n_rx, 1))]
  transfers between devices with their start and end apart: 10 -> 10, of which waited for: 4 -> 6; matrix products, arithmetic and copies ran while one was open for 13% -> 12% of each run, Pallas kernels for 0% -> 0%
where the time goes in v9:
time: 157 us; the launch traced here: 156 us
  waiting for transfers between devices  60.7 us (39%)
  starting transfers between devices  59.6 us (38%)
  local copies, waits for them, and re-layouts  16.6 us (11%)
  matrix products  11.6 us (7%)
  other arithmetic  3.95 us (3%)
  Pallas kernels  3.31 us (2%)
    all_to_all x1, waiting for transfers between devices, local(): lax.all_to_all(send_two, 'rx', split_axis=0, concat_axis=0, tiled=True)  19.6 us
    ppermute x2, starting transfers between devices, fetch_halo(): left = lax.ppermute(signal[:, -1:], 'ry', shift_pairs(n_ry, 1))  19 us
    ppermute x2, waiting for transfers between devices, fetch_halo(): right = lax.ppermute(signal[:, :1], 'ry', shift_pairs(n_ry, -1))  18.1 us
    all_to_all x1, waiting for transfers between devices, local(): lax.all_to_all(send_one, 'rx', split_axis=0, concat_axis=0, tiled=True)  17.2 us
    all_to_all x1, starting transfers between devices, local(): lax.all_to_all(send_one, 'rx', split_axis=0, concat_axis=0, tiled=True)  14.9 us
    all_to_all x1, starting transfers between devices, local(): lax.all_to_all(send_two, 'rx', split_axis=0, concat_axis=0, tiled=True)  11.2 us
    dot_general x8, matrix products, local_terms(): jnp.einsum('ijab,ijbf->ijaf', tiles[:, :, offset], neighbours[offset], pr...  6.48 us
    ppermute x2, starting transfers between devices, fetch_halo(): above = lax.ppermute(signal[-1:], 'rx', shift_pairs(n_rx, 1))  6.17 us
  transfers between devices with their start and end apart: 10, of which 6 were waited for; matrix products, arithmetic and copies ran while one was open for 12% of the time, Pallas kernels for 0%

profile of v9, /device:TPU:57, one launch (start us, length us, event | category | flops | bytes accessed | tf_op | source)
XLA Modules:
  0.0 156.4 jit_solution(1482522930225778900)
XLA Ops:
  4.1 0.8 reshape.388.tile_ref
  8.3 1.2 reshape.391
  9.6 14.9 %all-to-all-start = ((bf16[32,2,8320]{2,1,0:T(2,128)(2,1)}), bf16[32,2,8320]{2,1,0:T(2,128)(2,1)}, u32[]{:S(2)}, u32[]{:S(2)}) async-start(bf16[32,2,8320]{2,1,0:T(2,128)(2,1)} %reshape.391), calls=%async_computation | async-start | bytes 2129920 | tf_op jit(solution)/shard_map/all_to_all | solution.py:216
  25.2 3.1 %collective-permute-start = (bf16[1,4,64,128]{3,2,1,0:T(8,128)(2,1)}, bf16[1,4,64,128]{3,2,1,0:T(8,128)(2,1)S(1)}, u32[]{:S(2)}, u32[]{:S(2)}) collective-permute-start(bf16[1,4,64,128]{3,2,1,0:T(8,128)(2,1)} %bitcast.11), channel_id=1, source_target_pairs={{0,16},{16,32},{32,48},{48,64},{64,80},{80,96},{96,112},{112,128},... | collective-permute-start | bytes 196616 | tf_op jit(solution)/shard_map/ppermute | solution.py:65
  28.9 9.0 %collective-permute-start.2 = (bf16[4,1,64,128]{3,2,1,0:T(8,128)(2,1)S(1)}, bf16[4,1,64,128]{3,2,1,0:T(8,128)(2,1)}, u32[]{:S(2)}, u32[]{:S(2)}) collective-permute-start(bf16[4,1,64,128]{3,2,1,0:T(8,128)(2,1)S(1)} %get-tuple-element.29), channel_id=1, source_target_pairs={{0,1},{1,2},{2,3},{3,4},{4,5},{5,6},{6,7},{7,8},{8,9},{9,10},{10,1... | collective-permute-start | bytes 196616 | tf_op jit(solution)/shard_map/ppermute | solution.py:67
  37.9 1.9 %collective-permute-start.3 = (bf16[4,1,64,128]{3,2,1,0:T(8,128)(2,1)}, bf16[4,1,64,128]{3,2,1,0:T(8,128)(2,1)}, u32[]{:S(2)}, u32[]{:S(2)}) collective-permute-start(bf16[4,1,64,128]{3,2,1,0:T(8,128)(2,1)} %get-tuple-element.30), channel_id=1, source_target_pairs={{1,0},{2,1},{3,2},{4,3},{5,4},{6,5},{7,6},{8,7},{9,8},{10,9},{11,1... | collective-permute-start | bytes 196616 | tf_op jit(solution)/shard_map/ppermute | solution.py:68
  40.6 2.2 %collective-permute-start.1 = (bf16[1,4,64,128]{3,2,1,0:T(8,128)(2,1)}, bf16[1,4,64,128]{3,2,1,0:T(8,128)(2,1)S(1)}, u32[]{:S(2)}, u32[]{:S(2)}) collective-permute-start(bf16[1,4,64,128]{3,2,1,0:T(8,128)(2,1)} %bitcast.15), channel_id=1, source_target_pairs={{16,0},{32,16},{48,32},{64,48},{80,64},{96,80},{112,96},{128,112},... | collective-permute-start | bytes 196616 | tf_op jit(solution)/shard_map/ppermute | solution.py:66
  43.1 1.0 reshape.386
  45.2 0.8 copy.61
  46.0 1.0 fusion.34
  47.1 7.9 %collective-permute-done.3 = bf16[4,1,64,128]{3,2,1,0:T(8,128)(2,1)} collective-permute-done((bf16[4,1,64,128]{3,2,1,0:T(8,128)(2,1)}, bf16[4,1,64,128]{3,2,1,0:T(8,128)(2,1)}, u32[]{:S(2)}, u32[]{:S(2)}) %collective-permute-start.3) | collective-permute-done | bytes 65568 | tf_op jit(solution)/shard_map/ppermute | solution.py:68
  54.9 1.8 %fusion.38 = f32[4,4,128,64]{2,3,1,0:T(8,128)} fusion(bf16[4,1,64,128]{3,2,1,0:T(8,128)(2,1)} %collective-permute-done.3, bf16[4,3,64,128]{3,2,1,0:T(8,128)(2,1)S(1)} %get-tuple-element.32, bf16[4,4,5,64,64]{4,3,1,0,2:T(8,128)(2,1)S(1)} %reshape.386), kind=kOutput, calls=%fused_computation.61 | convolution fusion | flops 17301504 | bytes 1048576 | tf_op jit(solution)/shard_map/ijab,ijbf->ijaf/dot_general | solution.py:85
  56.8 4.6 %collective-permute-done = bf16[1,4,64,128]{3,2,1,0:T(8,128)(2,1)S(1)} collective-permute-done((bf16[1,4,64,128]{3,2,1,0:T(8,128)(2,1)}, bf16[1,4,64,128]{3,2,1,0:T(8,128)(2,1)S(1)}, u32[]{:S(2)}, u32[]{:S(2)}) %collective-permute-start) | collective-permute-done | bytes 65568 | tf_op jit(solution)/shard_map/ppermute | solution.py:65
  61.6 17.2 %all-to-all-done = bf16[32,2,8320]{2,1,0:T(2,128)(2,1)} async-done(((bf16[32,2,8320]{2,1,0:T(2,128)(2,1)}), bf16[32,2,8320]{2,1,0:T(2,128)(2,1)}, u32[]{:S(2)}, u32[]{:S(2)}) %all-to-all-start) | async-done | bytes 1064992 | tf_op jit(solution)/shard_map/all_to_all | solution.py:216
  79.6 2.1 %slice.184 = bf16[32,2,8192]{2,1,0:T(2,128)(2,1)S(1)} slice(bf16[32,2,8320]{2,1,0:T(2,128)(2,1)} %all-to-all-done), slice={[0:32], [0:2], [0:8192]} | slice | bytes 2097152 | tf_op jit(solution)/shard_map/slice | solution.py:218
  82.8 0.9 fusion.12
  83.7 3.3 %shard_map.118 = bf16[64,64,128]{2,1,0:T(8,128)(2,1)} custom-call(s32[48]{0:T(128)} %bitcast.147, s32[48]{0:T(128)} %multiply_add_fusion.3.slot_ref, bf16[16,64,128]{2,1,0:T(8,128)(2,1)} %bitcast.129, bf16[48,64,64]{2,1,0:T(8,128)(2,1)} %copy-done.1), custom_call_target="tpu_custom_call" | custom-call | flops 50331648 | bytes 1703936 | tf_op jit(solution)/shard_map/pallas_call | solution.py:132
  87.0 11.2 %all-to-all-start.1 = ((bf16[32,2,64,128]{3,2,1,0:T(8,128)(2,1)}), bf16[32,2,64,128]{3,2,1,0:T(8,128)(2,1)}, u32[]{:S(2)}, u32[]{:S(2)}) async-start(bf16[32,2,64,128]{3,2,1,0:T(8,128)(2,1)} %bitcast.135), calls=%async_computation.1 | async-start | bytes 2097152 | tf_op jit(solution)/shard_map/all_to_all | solution.py:225
  99.4 3.1 %collective-permute-start.4 = (bf16[1,4,64,128]{3,2,1,0:T(8,128)(2,1)S(1)}, bf16[1,4,64,128]{3,2,1,0:T(8,128)(2,1)S(1)}, u32[]{:S(2)}, u32[]{:S(2)}) collective-permute-start(bf16[1,4,64,128]{3,2,1,0:T(8,128)(2,1)S(1)} %get-tuple-element.20), channel_id=1, source_target_pairs={{0,16},{16,32},{32,48},{48,64},{64,80},{80,96},{96,112},{112,128},... | collective-permute-start | bytes 196616 | tf_op jit(solution)/shard_map/ppermute | solution.py:65
  102.5 10.0 %collective-permute-start.6 = (bf16[4,1,64,128]{3,2,1,0:T(8,128)(2,1)S(1)}, bf16[4,1,64,128]{3,2,1,0:T(8,128)(2,1)S(1)}, u32[]{:S(2)}, u32[]{:S(2)}) collective-permute-start(bf16[4,1,64,128]{3,2,1,0:T(8,128)(2,1)S(1)} %get-tuple-element.21), channel_id=1, source_target_pairs={{0,1},{1,2},{2,3},{3,4},{4,5},{5,6},{6,7},{7,8},{8,9},{9,10},{10,1... | collective-permute-start | bytes 196616 | tf_op jit(solution)/shard_map/ppermute | solution.py:67
  112.5 1.9 %collective-permute-start.7 = (bf16[4,1,64,128]{3,2,1,0:T(8,128)(2,1)S(1)}, bf16[4,1,64,128]{3,2,1,0:T(8,128)(2,1)S(1)}, u32[]{:S(2)}, u32[]{:S(2)}) collective-permute-start(bf16[4,1,64,128]{3,2,1,0:T(8,128)(2,1)S(1)} %get-tuple-element.22), channel_id=1, source_target_pairs={{1,0},{2,1},{3,2},{4,3},{5,4},{6,5},{7,6},{8,7},{9,8},{10,9},{11,1... | collective-permute-start | bytes 196616 | tf_op jit(solution)/shard_map/ppermute | solution.py:68
  114.4 2.4 %collective-permute-start.5 = (bf16[1,4,64,128]{3,2,1,0:T(8,128)(2,1)S(1)}, bf16[1,4,64,128]{3,2,1,0:T(8,128)(2,1)S(1)}, u32[]{:S(2)}, u32[]{:S(2)}) collective-permute-start(bf16[1,4,64,128]{3,2,1,0:T(8,128)(2,1)S(1)} %get-tuple-element.19), channel_id=1, source_target_pairs={{16,0},{32,16},{48,32},{64,48},{80,64},{96,80},{112,96},{128,112},... | collective-permute-start | bytes 196616 | tf_op jit(solution)/shard_map/ppermute | solution.py:66
  117.1 1.0 convolution_add_fusion
  118.2 1.0 fusion.48
  119.2 10.2 %collective-permute-done.7 = bf16[4,1,64,128]{3,2,1,0:T(8,128)(2,1)S(1)} collective-permute-done((bf16[4,1,64,128]{3,2,1,0:T(8,128)(2,1)S(1)}, bf16[4,1,64,128]{3,2,1,0:T(8,128)(2,1)S(1)}, u32[]{:S(2)}, u32[]{:S(2)}) %collective-permute-start.7) | collective-permute-done | bytes 65568 | tf_op jit(solution)/shard_map/ppermute | solution.py:68
  129.4 1.0 fusion.52
  130.4 1.2 collective-permute-done.4
  131.8 19.6 %all-to-all-done.1 = bf16[32,2,64,128]{3,2,1,0:T(8,128)(2,1)} async-done(((bf16[32,2,64,128]{3,2,1,0:T(8,128)(2,1)}), bf16[32,2,64,128]{3,2,1,0:T(8,128)(2,1)}, u32[]{:S(2)}, u32[]{:S(2)}) %all-to-all-start.1) | async-done | bytes 1048608 | tf_op jit(solution)/shard_map/all_to_all | solution.py:225
  151.4 1.3 reshape.413
  152.8 0.8 convolution_bitcast_fusion.1
  154.2 0.8 copy-done.2
  155.6 0.8 add_convert_fusion
  (108 shorter events, 15.7 us)
Async XLA Ops:
  0.0 2.3 %copy-start.13 = (f32[32]{0:T(128)S(1)}, f32[32]{0:T(128)}, u32[]{:S(2)}) copy-start(f32[32]{0:T(128)} %param.17) | copy-start | bytes 388
  0.0 2.4 %copy-start.14 = (f32[32]{0:T(128)S(1)}, f32[32]{0:T(128)}, u32[]{:S(2)}) copy-start(f32[32]{0:T(128)} %param.18) | copy-start | bytes 388
  0.0 2.8 %copy-start.6 = (bf16[4,4,64,128]{3,2,1,0:T(8,128)(2,1)S(1)}, bf16[4,4,64,128]{3,2,1,0:T(8,128)(2,1)}, u32[]{:S(2)}) copy-start(bf16[4,4,64,128]{3,2,1,0:T(8,128)(2,1)} %param.14) | copy-start | bytes 786436
  3.1 0.7 copy-start.16
  3.1 1.0 copy-start.10
  5.0 1.1 copy-start.1
  6.0 0.7 copy-start.12
  6.1 1.1 copy-start.17
  9.6 33.2 %copy-start.9 = (bf16[4,4,5,4096]{3,1,2,0:T(4,128)(2,1)S(1)}, bf16[4,4,5,4096]{3,1,2,0:T(4,128)(2,1)}, u32[]{:S(2)}) copy-start(bf16[4,4,5,4096]{3,1,2,0:T(4,128)(2,1)} %param.19) | copy-start | bytes 1966084
  9.6 69.2 %all-to-all-start = ((bf16[32,2,8320]{2,1,0:T(2,128)(2,1)}), bf16[32,2,8320]{2,1,0:T(2,128)(2,1)}, u32[]{:S(2)}, u32[]{:S(2)}) async-start(bf16[32,2,8320]{2,1,0:T(2,128)(2,1)} %reshape.391), calls=%async_computation | async-start | bytes 2129920 | tf_op jit(solution)/shard_map/all_to_all | solution.py:216
  25.2 36.2 %collective-permute-start = (bf16[1,4,64,128]{3,2,1,0:T(8,128)(2,1)}, bf16[1,4,64,128]{3,2,1,0:T(8,128)(2,1)S(1)}, u32[]{:S(2)}, u32[]{:S(2)}) collective-permute-start(bf16[1,4,64,128]{3,2,1,0:T(8,128)(2,1)} %bitcast.11), channel_id=1, source_target_pairs={{0,16},{16,32},{32,48},{48,64},{64,80},{80,96},{96,112},{112,128},... | collective-permute-start | bytes 196616 | tf_op jit(solution)/shard_map/ppermute | solution.py:65
  28.9 17.1 %collective-permute-start.2 = (bf16[4,1,64,128]{3,2,1,0:T(8,128)(2,1)S(1)}, bf16[4,1,64,128]{3,2,1,0:T(8,128)(2,1)}, u32[]{:S(2)}, u32[]{:S(2)}) collective-permute-start(bf16[4,1,64,128]{3,2,1,0:T(8,128)(2,1)S(1)} %get-tuple-element.29), channel_id=1, source_target_pairs={{0,1},{1,2},{2,3},{3,4},{4,5},{5,6},{6,7},{7,8},{8,9},{9,10},{10,1... | collective-permute-start | bytes 196616 | tf_op jit(solution)/shard_map/ppermute | solution.py:67
  37.9 17.0 %collective-permute-start.3 = (bf16[4,1,64,128]{3,2,1,0:T(8,128)(2,1)}, bf16[4,1,64,128]{3,2,1,0:T(8,128)(2,1)}, u32[]{:S(2)}, u32[]{:S(2)}) collective-permute-start(bf16[4,1,64,128]{3,2,1,0:T(8,128)(2,1)} %get-tuple-element.30), channel_id=1, source_target_pairs={{1,0},{2,1},{3,2},{4,3},{5,4},{6,5},{7,6},{8,7},{9,8},{10,9},{11,1... | collective-permute-start | bytes 196616 | tf_op jit(solution)/shard_map/ppermute | solution.py:68
  40.6 41.9 %collective-permute-start.1 = (bf16[1,4,64,128]{3,2,1,0:T(8,128)(2,1)}, bf16[1,4,64,128]{3,2,1,0:T(8,128)(2,1)S(1)}, u32[]{:S(2)}, u32[]{:S(2)}) collective-permute-start(bf16[1,4,64,128]{3,2,1,0:T(8,128)(2,1)} %bitcast.15), channel_id=1, source_target_pairs={{16,0},{32,16},{48,32},{64,48},{80,64},{96,80},{112,96},{128,112},... | collective-permute-start | bytes 196616 | tf_op jit(solution)/shard_map/ppermute | solution.py:66
  81.7 1.0 copy-start.4
  81.7 1.1 copy-start.8
  87.0 11.3 %copy-start.11 = (bf16[3,32,32]{2,1,0:T(8,128)(2,1)S(1)}, bf16[3,32,32]{2,1,0:T(8,128)(2,1)}, u32[]{:S(2)}) copy-start(bf16[3,32,32]{2,1,0:T(8,128)(2,1)} %param.24) | copy-start | bytes 18436
  87.0 12.0 %copy-start.15 = (f32[32]{0:T(128)S(1)}, f32[32]{0:T(128)}, u32[]{:S(2)}) copy-start(f32[32]{0:T(128)} %param.25) | copy-start | bytes 388
  87.0 64.4 %all-to-all-start.1 = ((bf16[32,2,64,128]{3,2,1,0:T(8,128)(2,1)}), bf16[32,2,64,128]{3,2,1,0:T(8,128)(2,1)}, u32[]{:S(2)}, u32[]{:S(2)}) async-start(bf16[32,2,64,128]{3,2,1,0:T(8,128)(2,1)} %bitcast.135), calls=%async_computation.1 | async-start | bytes 2097152 | tf_op jit(solution)/shard_map/all_to_all | solution.py:225
  98.2 1.1 copy-start
  99.4 32.2 %collective-permute-start.4 = (bf16[1,4,64,128]{3,2,1,0:T(8,128)(2,1)S(1)}, bf16[1,4,64,128]{3,2,1,0:T(8,128)(2,1)S(1)}, u32[]{:S(2)}, u32[]{:S(2)}) collective-permute-start(bf16[1,4,64,128]{3,2,1,0:T(8,128)(2,1)S(1)} %get-tuple-element.20), channel_id=1, source_target_pairs={{0,16},{16,32},{32,48},{48,64},{64,80},{80,96},{96,112},{112,128},... | collective-permute-start | bytes 196616 | tf_op jit(solution)/shard_map/ppermute | solution.py:65
  102.5 15.7 %collective-permute-start.6 = (bf16[4,1,64,128]{3,2,1,0:T(8,128)(2,1)S(1)}, bf16[4,1,64,128]{3,2,1,0:T(8,128)(2,1)S(1)}, u32[]{:S(2)}, u32[]{:S(2)}) collective-permute-start(bf16[4,1,64,128]{3,2,1,0:T(8,128)(2,1)S(1)} %get-tuple-element.21), channel_id=1, source_target_pairs={{0,1},{1,2},{2,3},{3,4},{4,5},{5,6},{6,7},{7,8},{8,9},{9,10},{10,1... | collective-permute-start | bytes 196616 | tf_op jit(solution)/shard_map/ppermute | solution.py:67
  112.5 16.9 %collective-permute-start.7 = (bf16[4,1,64,128]{3,2,1,0:T(8,128)(2,1)S(1)}, bf16[4,1,64,128]{3,2,1,0:T(8,128)(2,1)S(1)}, u32[]{:S(2)}, u32[]{:S(2)}) collective-permute-start(bf16[4,1,64,128]{3,2,1,0:T(8,128)(2,1)S(1)} %get-tuple-element.22), channel_id=1, source_target_pairs={{1,0},{2,1},{3,2},{4,3},{5,4},{6,5},{7,6},{8,7},{9,8},{10,9},{11,1... | collective-permute-start | bytes 196616 | tf_op jit(solution)/shard_map/ppermute | solution.py:68
  114.4 39.2 %collective-permute-start.5 = (bf16[1,4,64,128]{3,2,1,0:T(8,128)(2,1)S(1)}, bf16[1,4,64,128]{3,2,1,0:T(8,128)(2,1)S(1)}, u32[]{:S(2)}, u32[]{:S(2)}) collective-permute-start(bf16[1,4,64,128]{3,2,1,0:T(8,128)(2,1)S(1)} %get-tuple-element.19), channel_id=1, source_target_pairs={{16,0},{32,16},{48,32},{64,48},{80,64},{96,80},{112,96},{128,112},... | collective-permute-start | bytes 196616 | tf_op jit(solution)/shard_map/ppermute | solution.py:66
  152.8 1.0 copy-start.3
  152.8 1.2 copy-start.5
  154.0 1.0 copy-start.2
  154.2 1.4 copy-start.7

commit v10 on v9

--- a/solution.py
+++ b/solution.py
@@ -171,11 +171,11 @@
 
 
 def far_terms(received, targets, nblocks):
-    senders, cap = received.shape[0], received.shape[1]
-    received = received.reshape(senders, cap, -1)
     onehot = (targets[None] == jnp.arange(nblocks, dtype=jnp.int32)[:, None, None]).astype(
         jnp.bfloat16
     )
+    if received.ndim == 4:
+        return jnp.einsum("nrc,rcaf->naf", onehot, received, preferred_element_type=jnp.float32)
     return jnp.einsum("nrc,rck->nk", onehot, received, preferred_element_type=jnp.float32)
 
 
@@ -215,9 +215,8 @@
     halo_one = fetch_halo(gated)
     recv_one = lax.all_to_all(send_one, "rx", split_axis=0, concat_axis=0, tiled=True)
     targets = recv_one[:, :, block_len].astype(jnp.int32) - 1
-    recv_one = recv_one[:, :, :block_len]
     near_one = local_terms(gated, tiles, halo_one)
-    far_one = far_terms(recv_one, targets, nblocks)
+    far_one = far_terms(recv_one, targets, nblocks)[:, :block_len]
     first_hop = (near_one + far_one.reshape(gated.shape)).astype(jnp.bfloat16)
 
     send_two = send_products(first_hop, edge_tiles, sources, slots, select)

time: 157 us -> 159 us (1.013)
  starting transfers between devices: 59.6 us -> 70.3 us
  waiting for transfers between devices: 60.7 us -> 52.5 us
    ppermute x2, waiting for transfers between devices: 18.1 us -> 0.01 us  [fetch_halo(): right = lax.ppermute(signal[:, :1], 'ry', shift_pairs(n_ry, -1))]
    ppermute x2, waiting for transfers between devices: 5.82 us -> 16.5 us  [fetch_halo(): above = lax.ppermute(signal[-1:], 'rx', shift_pairs(n_rx, 1))]
    ppermute x2, starting transfers between devices: 19 us -> 27.7 us  [fetch_halo(): left = lax.ppermute(signal[:, -1:], 'ry', shift_pairs(n_ry, 1))]
    slice x1 -> x0, local copies, waits for them, and re-layouts: 2.07 us -> none  [local(): recv_one = recv_one[:, :, :block_len]]
    dot_general x0 -> x1, matrix products: none -> 1.96 us  [far_terms(): jnp.einsum('nrc,rcaf->naf', onehot, received, preferred_element_type=jnp....]
    reshape x1, local copies, waits for them, and re-layouts: 1.33 us -> 3.28 us  [send_products(): return products.reshape(lax.axis_size('rx'), CAP, block_size, features)]
    dot_general x8, matrix products: 6.48 us -> 4.89 us  [local_terms(): jnp.einsum('ijab,ijbf->ijaf', tiles[:, :, offset], neighbours[offset], pr...]
    unnamed x41 -> x38, local copies, waits for them, and re-layouts: 3.27 us -> 2.7 us
  transfers between devices with their start and end apart: 10 -> 10, of which waited for: 6 -> 4; matrix products, arithmetic and copies ran while one was open for 12% -> 10% of each run, Pallas kernels for 0% -> 0%
where the time goes in v10:
time: 159 us; the launch traced here: 158 us
  starting transfers between devices  70.3 us (44%)
  waiting for transfers between devices  52.5 us (33%)
  local copies, waits for them, and re-layouts  16.1 us (10%)
  matrix products  11.2 us (7%)
  other arithmetic  3.93 us (2%)
  Pallas kernels  3.31 us (2%)
    ppermute x2, starting transfers between devices, fetch_halo(): left = lax.ppermute(signal[:, -1:], 'ry', shift_pairs(n_ry, 1))  27.7 us
    all_to_all x1, waiting for transfers between devices, local(): lax.all_to_all(send_two, 'rx', split_axis=0, concat_axis=0, tiled=True)  19.6 us
    all_to_all x1, waiting for transfers between devices, local(): lax.all_to_all(send_one, 'rx', split_axis=0, concat_axis=0, tiled=True)  16.5 us
    ppermute x2, waiting for transfers between devices, fetch_halo(): above = lax.ppermute(signal[-1:], 'rx', shift_pairs(n_rx, 1))  16.5 us
    all_to_all x1, starting transfers between devices, local(): lax.all_to_all(send_one, 'rx', split_axis=0, concat_axis=0, tiled=True)  14.9 us
    all_to_all x1, starting transfers between devices, local(): lax.all_to_all(send_two, 'rx', split_axis=0, concat_axis=0, tiled=True)  11.3 us
    ppermute x2, starting transfers between devices, fetch_halo(): above = lax.ppermute(signal[-1:], 'rx', shift_pairs(n_rx, 1))  6.17 us
    ppermute x2, starting transfers between devices, fetch_halo(): below = lax.ppermute(signal[:1], 'rx', shift_pairs(n_rx, -1))  5.17 us
  transfers between devices with their start and end apart: 10, of which 4 were waited for; matrix products, arithmetic and copies ran while one was open for 10% of the time, Pallas kernels for 0%

profile of v10, /device:TPU:57, one launch (start us, length us, event | category | flops | bytes accessed | tf_op | source)
XLA Modules:
  0.0 158.1 jit_solution(8905034882078439003)
XLA Ops:
  0.7 0.8 slice_bitcast_fusion.19
  3.7 0.8 reshape.383.tile_ref
  5.9 0.7 gather_fusion
  7.9 1.2 reshape.386
  9.1 14.9 %all-to-all-start = ((bf16[32,2,8320]{2,1,0:T(2,128)(2,1)}), bf16[32,2,8320]{2,1,0:T(2,128)(2,1)}, u32[]{:S(2)}, u32[]{:S(2)}) async-start(bf16[32,2,8320]{2,1,0:T(2,128)(2,1)} %reshape.386), calls=%async_computation | async-start | bytes 2129920 | tf_op jit(solution)/shard_map/all_to_all | solution.py:216
  24.7 3.1 %collective-permute-start.3 = (bf16[4,1,64,128]{3,2,1,0:T(8,128)(2,1)}, bf16[4,1,64,128]{3,2,1,0:T(8,128)(2,1)S(1)}, u32[]{:S(2)}, u32[]{:S(2)}) collective-permute-start(bf16[4,1,64,128]{3,2,1,0:T(8,128)(2,1)} %get-tuple-element.30), channel_id=1, source_target_pairs={{1,0},{2,1},{3,2},{4,3},{5,4},{6,5},{7,6},{8,7},{9,8},{10,9},{11,1... | collective-permute-start | bytes 196616 | tf_op jit(solution)/shard_map/ppermute | solution.py:68
  27.8 13.2 %collective-permute-start.2 = (bf16[4,1,64,128]{3,2,1,0:T(8,128)(2,1)}, bf16[4,1,64,128]{3,2,1,0:T(8,128)(2,1)S(1)}, u32[]{:S(2)}, u32[]{:S(2)}) collective-permute-start(bf16[4,1,64,128]{3,2,1,0:T(8,128)(2,1)} %get-tuple-element.29), channel_id=1, source_target_pairs={{0,1},{1,2},{2,3},{3,4},{4,5},{5,6},{6,7},{7,8},{8,9},{9,10},{10,1... | collective-permute-start | bytes 196616 | tf_op jit(solution)/shard_map/ppermute | solution.py:67
  41.2 3.1 %collective-permute-start = (bf16[1,4,64,128]{3,2,1,0:T(8,128)(2,1)S(1)}, bf16[1,4,64,128]{3,2,1,0:T(8,128)(2,1)}, u32[]{:S(2)}, u32[]{:S(2)}) collective-permute-start(bf16[1,4,64,128]{3,2,1,0:T(8,128)(2,1)S(1)} %bitcast.129), channel_id=1, source_target_pairs={{0,16},{16,32},{32,48},{48,64},{64,80},{80,96},{96,112},{112,128},... | collective-permute-start | bytes 196616 | tf_op jit(solution)/shard_map/ppermute | solution.py:65
  44.3 0.7 copy.62
  45.0 2.8 %collective-permute-start.1 = (bf16[1,4,64,128]{3,2,1,0:T(8,128)(2,1)}, bf16[1,4,64,128]{3,2,1,0:T(8,128)(2,1)S(1)}, u32[]{:S(2)}, u32[]{:S(2)}) collective-permute-start(bf16[1,4,64,128]{3,2,1,0:T(8,128)(2,1)} %bitcast.15), channel_id=1, source_target_pairs={{16,0},{32,16},{48,32},{64,48},{80,64},{96,80},{112,96},{128,112},... | collective-permute-start | bytes 196616 | tf_op jit(solution)/shard_map/ppermute | solution.py:66
  48.2 1.0 reshape.381
  50.3 0.8 copy.61
  51.3 1.0 fusion.34
  52.3 8.5 %collective-permute-done = bf16[1,4,64,128]{3,2,1,0:T(8,128)(2,1)} collective-permute-done((bf16[1,4,64,128]{3,2,1,0:T(8,128)(2,1)S(1)}, bf16[1,4,64,128]{3,2,1,0:T(8,128)(2,1)}, u32[]{:S(2)}, u32[]{:S(2)}) %collective-permute-start) | collective-permute-done | bytes 65568 | tf_op jit(solution)/shard_map/ppermute | solution.py:65
  60.8 1.0 convolution_add_fusion.4
  61.9 16.5 %all-to-all-done = bf16[32,2,8320]{2,1,0:T(2,128)(2,1)} async-done(((bf16[32,2,8320]{2,1,0:T(2,128)(2,1)}), bf16[32,2,8320]{2,1,0:T(2,128)(2,1)}, u32[]{:S(2)}, u32[]{:S(2)}) %all-to-all-start) | async-done | bytes 1064992 | tf_op jit(solution)/shard_map/all_to_all | solution.py:216
  78.3 0.7 slice.183
  79.2 1.6 convolution_bitcast_fusion
  80.9 0.9 copy-done.2
  81.8 0.9 fusion.12
  82.7 3.3 %shard_map.118 = bf16[64,64,128]{2,1,0:T(8,128)(2,1)} custom-call(s32[48]{0:T(128)} %bitcast.133, s32[48]{0:T(128)} %multiply_add_fusion.2.slot_ref, bf16[16,64,128]{2,1,0:T(8,128)(2,1)} %bitcast.113, bf16[48,64,64]{2,1,0:T(8,128)(2,1)} %copy-done.1), custom_call_target="tpu_custom_call" | custom-call | flops 50331648 | bytes 1703936 | tf_op jit(solution)/shard_map/pallas_call | solution.py:132
  86.1 3.3 %copy.68 = bf16[32,2,64,128]{3,1,2,0:T(2,128)(2,1)} copy(bf16[32,2,64,128]{3,2,1,0:T(8,128)(2,1)} %bitcast.119) | data formatting | bytes 2097152 | tf_op jit(solution)/shard_map/reshape | solution.py:152
  89.3 11.3 %all-to-all-start.1 = ((bf16[32,2,64,128]{3,1,2,0:T(2,128)(2,1)}), bf16[32,2,64,128]{3,1,2,0:T(2,128)(2,1)}, u32[]{:S(2)}, u32[]{:S(2)}) async-start(bf16[32,2,64,128]{3,1,2,0:T(2,128)(2,1)} %copy.68), calls=%async_computation.1 | async-start | bytes 2097152 | tf_op jit(solution)/shard_map/all_to_all | solution.py:224
  101.8 1.9 %collective-permute-start.7 = (bf16[4,1,64,128]{3,2,1,0:T(8,128)(2,1)S(1)}, bf16[4,1,64,128]{3,2,1,0:T(8,128)(2,1)S(1)}, u32[]{:S(2)}, u32[]{:S(2)}) collective-permute-start(bf16[4,1,64,128]{3,2,1,0:T(8,128)(2,1)S(1)} %get-tuple-element.22), channel_id=1, source_target_pairs={{1,0},{2,1},{3,2},{4,3},{5,4},{6,5},{7,6},{8,7},{9,8},{10,9},{11,1... | collective-permute-start | bytes 196616 | tf_op jit(solution)/shard_map/ppermute | solution.py:68
  103.8 14.5 %collective-permute-start.6 = (bf16[4,1,64,128]{3,2,1,0:T(8,128)(2,1)S(1)}, bf16[4,1,64,128]{3,2,1,0:T(8,128)(2,1)S(1)}, u32[]{:S(2)}, u32[]{:S(2)}) collective-permute-start(bf16[4,1,64,128]{3,2,1,0:T(8,128)(2,1)S(1)} %get-tuple-element.21), channel_id=1, source_target_pairs={{0,1},{1,2},{2,3},{3,4},{4,5},{5,6},{6,7},{7,8},{8,9},{9,10},{10,1... | collective-permute-start | bytes 196616 | tf_op jit(solution)/shard_map/ppermute | solution.py:67
  118.9 3.1 %collective-permute-start.4 = (bf16[1,4,64,128]{3,2,1,0:T(8,128)(2,1)S(1)}, bf16[1,4,64,128]{3,2,1,0:T(8,128)(2,1)S(1)}, u32[]{:S(2)}, u32[]{:S(2)}) collective-permute-start(bf16[1,4,64,128]{3,2,1,0:T(8,128)(2,1)S(1)} %get-tuple-element.20), channel_id=1, source_target_pairs={{0,16},{16,32},{32,48},{48,64},{64,80},{80,96},{96,112},{112,128},... | collective-permute-start | bytes 196616 | tf_op jit(solution)/shard_map/ppermute | solution.py:65
  122.0 2.4 %collective-permute-start.5 = (bf16[1,4,64,128]{3,2,1,0:T(8,128)(2,1)}, bf16[1,4,64,128]{3,2,1,0:T(8,128)(2,1)S(1)}, u32[]{:S(2)}, u32[]{:S(2)}) collective-permute-start(bf16[1,4,64,128]{3,2,1,0:T(8,128)(2,1)} %get-tuple-element.19), channel_id=1, source_target_pairs={{16,0},{32,16},{48,32},{64,48},{80,64},{96,80},{112,96},{128,112},... | collective-permute-start | bytes 196616 | tf_op jit(solution)/shard_map/ppermute | solution.py:66
  125.1 1.0 fusion.48
  126.2 8.0 %collective-permute-done.4 = bf16[1,4,64,128]{3,2,1,0:T(8,128)(2,1)S(1)} collective-permute-done((bf16[1,4,64,128]{3,2,1,0:T(8,128)(2,1)S(1)}, bf16[1,4,64,128]{3,2,1,0:T(8,128)(2,1)S(1)}, u32[]{:S(2)}, u32[]{:S(2)}) %collective-permute-start.4) | collective-permute-done | bytes 65568 | tf_op jit(solution)/shard_map/ppermute | solution.py:65
  134.3 19.6 %all-to-all-done.1 = bf16[32,2,64,128]{3,1,2,0:T(2,128)(2,1)} async-done(((bf16[32,2,64,128]{3,1,2,0:T(2,128)(2,1)}), bf16[32,2,64,128]{3,1,2,0:T(2,128)(2,1)}, u32[]{:S(2)}, u32[]{:S(2)}) %all-to-all-start.1) | async-done | bytes 1048608 | tf_op jit(solution)/shard_map/all_to_all | solution.py:224
  153.9 2.0 %convolution_bitcast_fusion.2 = f32[16,64,128]{2,0,1:T(8,128)S(1)} fusion(bf16[32,2,64,128]{3,1,2,0:T(2,128)(2,1)} %all-to-all-done.1, s32[32,2]{0,1:T(2,128)S(1)} %add_bitcast_fusion), kind=kOutput, calls=%fused_computation.24 | convolution fusion | flops 16778240 | bytes 1573120 | tf_op jit(solution)/shard_map/nrc,rcaf->naf/dot_general | solution.py:178
  157.3 0.8 add_convert_fusion
  (104 shorter events, 12.1 us)
Async XLA Ops:
  0.0 2.3 %copy-start.11 = (f32[32]{0:T(128)S(1)}, f32[32]{0:T(128)}, u32[]{:S(2)}) copy-start(f32[32]{0:T(128)} %param.18) | copy-start | bytes 388
  0.0 2.4 %copy-start.12 = (f32[32]{0:T(128)S(1)}, f32[32]{0:T(128)}, u32[]{:S(2)}) copy-start(f32[32]{0:T(128)} %param.17) | copy-start | bytes 388
  0.0 2.5 %copy-start.10 = (s32[1,1,48,1]{2,3,1,0:T(1,128)S(1)}, s32[1,1,48,1]{2,3,1,0:T(1,128)}, u32[]{:S(2)}) copy-start(s32[1,1,48,1]{2,3,1,0:T(1,128)} %param.21) | copy-start | bytes 580
  0.0 2.9 %copy-start.15 = (s32[1,1,48]{2,1,0:T(1,128)S(1)}, s32[1,1,48]{2,1,0:T(1,128)}, u32[]{:S(2)}) copy-start(s32[1,1,48]{2,1,0:T(1,128)} %param.22) | copy-start | bytes 580
  0.0 3.7 %copy-start.8 = (bf16[1,1,48,4096]{3,2,1,0:T(8,128)(2,1)S(1)}, bf16[1,1,48,4096]{3,2,1,0:T(8,128)(2,1)}, u32[]{:S(2)}) copy-start(bf16[1,1,48,4096]{3,2,1,0:T(8,128)(2,1)} %param.23) | copy-start | bytes 1179652
  2.1 2.7 %copy-start.4 = (bf16[4,4,64,128]{3,2,1,0:T(8,128)(2,1)S(1)}, bf16[4,4,64,128]{3,2,1,0:T(8,128)(2,1)}, u32[]{:S(2)}) copy-start(bf16[4,4,64,128]{3,2,1,0:T(8,128)(2,1)} %param.14) | copy-start | bytes 786436
  4.5 2.0 %copy-start.1 = (bf16[48,64,64]{2,1,0:T(8,128)(2,1)}, bf16[48,64,64]{2,1,0:T(8,128)(2,1)S(1)}, u32[]{:S(2)}) copy-start(bf16[48,64,64]{2,1,0:T(8,128)(2,1)S(1)} %reshape.383.tile_ref) | copy-start | bytes 1179652
  5.2 0.7 copy-start.14
  9.1 38.7 %copy-start.7 = (bf16[4,4,5,4096]{3,1,2,0:T(4,128)(2,1)S(1)}, bf16[4,4,5,4096]{3,1,2,0:T(4,128)(2,1)}, u32[]{:S(2)}) copy-start(bf16[4,4,5,4096]{3,1,2,0:T(4,128)(2,1)} %param.19) | copy-start | bytes 1966084
  9.1 69.2 %all-to-all-start = ((bf16[32,2,8320]{2,1,0:T(2,128)(2,1)}), bf16[32,2,8320]{2,1,0:T(2,128)(2,1)}, u32[]{:S(2)}, u32[]{:S(2)}) async-start(bf16[32,2,8320]{2,1,0:T(2,128)(2,1)} %reshape.386), calls=%async_computation | async-start | bytes 2129920 | tf_op jit(solution)/shard_map/all_to_all | solution.py:216
  24.7 26.4 %collective-permute-start.3 = (bf16[4,1,64,128]{3,2,1,0:T(8,128)(2,1)}, bf16[4,1,64,128]{3,2,1,0:T(8,128)(2,1)S(1)}, u32[]{:S(2)}, u32[]{:S(2)}) collective-permute-start(bf16[4,1,64,128]{3,2,1,0:T(8,128)(2,1)} %get-tuple-element.30), channel_id=1, source_target_pairs={{1,0},{2,1},{3,2},{4,3},{5,4},{6,5},{7,6},{8,7},{9,8},{10,9},{11,1... | collective-permute-start | bytes 196616 | tf_op jit(solution)/shard_map/ppermute | solution.py:68
  27.8 23.5 %collective-permute-start.2 = (bf16[4,1,64,128]{3,2,1,0:T(8,128)(2,1)}, bf16[4,1,64,128]{3,2,1,0:T(8,128)(2,1)S(1)}, u32[]{:S(2)}, u32[]{:S(2)}) collective-permute-start(bf16[4,1,64,128]{3,2,1,0:T(8,128)(2,1)} %get-tuple-element.29), channel_id=1, source_target_pairs={{0,1},{1,2},{2,3},{3,4},{4,5},{5,6},{6,7},{7,8},{8,9},{9,10},{10,1... | collective-permute-start | bytes 196616 | tf_op jit(solution)/shard_map/ppermute | solution.py:67
  41.2 19.6 %collective-permute-start = (bf16[1,4,64,128]{3,2,1,0:T(8,128)(2,1)S(1)}, bf16[1,4,64,128]{3,2,1,0:T(8,128)(2,1)}, u32[]{:S(2)}, u32[]{:S(2)}) collective-permute-start(bf16[1,4,64,128]{3,2,1,0:T(8,128)(2,1)S(1)} %bitcast.129), channel_id=1, source_target_pairs={{0,16},{16,32},{32,48},{48,64},{64,80},{80,96},{96,112},{112,128},... | collective-permute-start | bytes 196616 | tf_op jit(solution)/shard_map/ppermute | solution.py:65
  45.0 35.9 %collective-permute-start.1 = (bf16[1,4,64,128]{3,2,1,0:T(8,128)(2,1)}, bf16[1,4,64,128]{3,2,1,0:T(8,128)(2,1)S(1)}, u32[]{:S(2)}, u32[]{:S(2)}) collective-permute-start(bf16[1,4,64,128]{3,2,1,0:T(8,128)(2,1)} %bitcast.15), channel_id=1, source_target_pairs={{16,0},{32,16},{48,32},{64,48},{80,64},{96,80},{112,96},{128,112},... | collective-permute-start | bytes 196616 | tf_op jit(solution)/shard_map/ppermute | solution.py:66
  80.7 1.1 copy-start.2
  80.7 1.1 copy-start.6
  89.3 11.4 %copy-start.9 = (bf16[3,32,32]{2,1,0:T(8,128)(2,1)S(1)}, bf16[3,32,32]{2,1,0:T(8,128)(2,1)}, u32[]{:S(2)}) copy-start(bf16[3,32,32]{2,1,0:T(8,128)(2,1)} %param.24) | copy-start | bytes 18436
  89.3 12.1 %copy-start.13 = (f32[32]{0:T(128)S(1)}, f32[32]{0:T(128)}, u32[]{:S(2)}) copy-start(f32[32]{0:T(128)} %param.25) | copy-start | bytes 388
  89.3 64.6 %all-to-all-start.1 = ((bf16[32,2,64,128]{3,1,2,0:T(2,128)(2,1)}), bf16[32,2,64,128]{3,1,2,0:T(2,128)(2,1)}, u32[]{:S(2)}, u32[]{:S(2)}) async-start(bf16[32,2,64,128]{3,1,2,0:T(2,128)(2,1)} %copy.68), calls=%async_computation.1 | async-start | bytes 2097152 | tf_op jit(solution)/shard_map/all_to_all | solution.py:224
  100.7 1.1 copy-start
  101.8 23.1 %collective-permute-start.7 = (bf16[4,1,64,128]{3,2,1,0:T(8,128)(2,1)S(1)}, bf16[4,1,64,128]{3,2,1,0:T(8,128)(2,1)S(1)}, u32[]{:S(2)}, u32[]{:S(2)}) collective-permute-start(bf16[4,1,64,128]{3,2,1,0:T(8,128)(2,1)S(1)} %get-tuple-element.22), channel_id=1, source_target_pairs={{1,0},{2,1},{3,2},{4,3},{5,4},{6,5},{7,6},{8,7},{9,8},{10,9},{11,1... | collective-permute-start | bytes 196616 | tf_op jit(solution)/shard_map/ppermute | solution.py:68
  103.8 21.4 %collective-permute-start.6 = (bf16[4,1,64,128]{3,2,1,0:T(8,128)(2,1)S(1)}, bf16[4,1,64,128]{3,2,1,0:T(8,128)(2,1)S(1)}, u32[]{:S(2)}, u32[]{:S(2)}) collective-permute-start(bf16[4,1,64,128]{3,2,1,0:T(8,128)(2,1)S(1)} %get-tuple-element.21), channel_id=1, source_target_pairs={{0,1},{1,2},{2,3},{3,4},{4,5},{5,6},{6,7},{7,8},{8,9},{9,10},{10,1... | collective-permute-start | bytes 196616 | tf_op jit(solution)/shard_map/ppermute | solution.py:67
  118.9 15.3 %collective-permute-start.4 = (bf16[1,4,64,128]{3,2,1,0:T(8,128)(2,1)S(1)}, bf16[1,4,64,128]{3,2,1,0:T(8,128)(2,1)S(1)}, u32[]{:S(2)}, u32[]{:S(2)}) collective-permute-start(bf16[1,4,64,128]{3,2,1,0:T(8,128)(2,1)S(1)} %get-tuple-element.20), channel_id=1, source_target_pairs={{0,16},{16,32},{32,48},{48,64},{64,80},{80,96},{96,112},{112,128},... | collective-permute-start | bytes 196616 | tf_op jit(solution)/shard_map/ppermute | solution.py:65
  122.0 34.1 %collective-permute-start.5 = (bf16[1,4,64,128]{3,2,1,0:T(8,128)(2,1)}, bf16[1,4,64,128]{3,2,1,0:T(8,128)(2,1)S(1)}, u32[]{:S(2)}, u32[]{:S(2)}) collective-permute-start(bf16[1,4,64,128]{3,2,1,0:T(8,128)(2,1)} %get-tuple-element.19), channel_id=1, source_target_pairs={{16,0},{32,16},{48,32},{64,48},{80,64},{96,80},{112,96},{128,112},... | collective-permute-start | bytes 196616 | tf_op jit(solution)/shard_map/ppermute | solution.py:66
  153.9 2.1 %copy-start.3 = (f32[4,4,128,64]{2,3,1,0:T(8,128)S(1)}, f32[4,4,128,64]{2,3,1,0:T(8,128)}, u32[]{:S(2)}) copy-start(f32[4,4,128,64]{2,3,1,0:T(8,128)} %fusion.48) | copy-start | bytes 1572868
  156.3 1.0 copy-start.5

commit v11 on v10

--- a/solution.py
+++ b/solution.py
@@ -174,8 +174,7 @@
     onehot = (targets[None] == jnp.arange(nblocks, dtype=jnp.int32)[:, None, None]).astype(
         jnp.bfloat16
     )
-    if received.ndim == 4:
-        return jnp.einsum("nrc,rcaf->naf", onehot, received, preferred_element_type=jnp.float32)
+    received = received.reshape(received.shape[0], received.shape[1], -1)
     return jnp.einsum("nrc,rck->nk", onehot, received, preferred_element_type=jnp.float32)
 
 

time: 159 us -> 157 us (0.987)
  starting transfers between devices: 70.3 us -> 59.6 us
  waiting for transfers between devices: 52.5 us -> 60.7 us
    ppermute x2, waiting for transfers between devices: 0.01 us -> 18 us  [fetch_halo(): right = lax.ppermute(signal[:, :1], 'ry', shift_pairs(n_ry, -1))]
    ppermute x2, waiting for transfers between devices: 16.5 us -> 5.82 us  [fetch_halo(): above = lax.ppermute(signal[-1:], 'rx', shift_pairs(n_rx, 1))]
    ppermute x2, starting transfers between devices: 27.7 us -> 19 us  [fetch_halo(): left = lax.ppermute(signal[:, -1:], 'ry', shift_pairs(n_ry, 1))]
    dot_general x1 -> x0, matrix products: 1.96 us -> none  [far_terms(): jnp.einsum('nrc,rcaf->naf', onehot, received, preferred_element_type=jnp....]
    reshape x1, local copies, waits for them, and re-layouts: 3.28 us -> 1.33 us  [far_terms(): received = received.reshape(received.shape[0], received.shape[1], -1)]
    dot_general x8, matrix products: 4.89 us -> 6.48 us  [local_terms(): jnp.einsum('ijab,ijbf->ijaf', tiles[:, :, offset], neighbours[offset], pr...]
    unnamed x38 -> x42, local copies, waits for them, and re-layouts: 2.7 us -> 3.95 us
  transfers between devices with their start and end apart: 10 -> 10, of which waited for: 4 -> 6; matrix products, arithmetic and copies ran while one was open for 10% -> 11% of each run, Pallas kernels for 0% -> 0%
where the time goes in v11:
time: 157 us; the launch traced here: 156 us
  waiting for transfers between devices  60.7 us (39%)
  starting transfers between devices  59.6 us (38%)
  local copies, waits for them, and re-layouts  15.2 us (10%)
  matrix products  12.5 us (8%)
  other arithmetic  3.95 us (3%)
  Pallas kernels  3.31 us (2%)
    all_to_all x1, waiting for transfers between devices, local(): lax.all_to_all(send_two, 'rx', split_axis=0, concat_axis=0, tiled=True)  19.6 us
    ppermute x2, starting transfers between devices, fetch_halo(): left = lax.ppermute(signal[:, -1:], 'ry', shift_pairs(n_ry, 1))  19 us
    ppermute x2, waiting for transfers between devices, fetch_halo(): right = lax.ppermute(signal[:, :1], 'ry', shift_pairs(n_ry, -1))  18 us
    all_to_all x1, waiting for transfers between devices, local(): lax.all_to_all(send_one, 'rx', split_axis=0, concat_axis=0, tiled=True)  17.2 us
    all_to_all x1, starting transfers between devices, local(): lax.all_to_all(send_one, 'rx', split_axis=0, concat_axis=0, tiled=True)  14.9 us
    all_to_all x1, starting transfers between devices, local(): lax.all_to_all(send_two, 'rx', split_axis=0, concat_axis=0, tiled=True)  11.2 us
    dot_general x8, matrix products, local_terms(): jnp.einsum('ijab,ijbf->ijaf', tiles[:, :, offset], neighbours[offset], pr...  6.48 us
    ppermute x2, starting transfers between devices, fetch_halo(): above = lax.ppermute(signal[-1:], 'rx', shift_pairs(n_rx, 1))  6.17 us
  transfers between devices with their start and end apart: 10, of which 6 were waited for; matrix products, arithmetic and copies ran while one was open for 11% of the time, Pallas kernels for 0%

profile of v11, /device:TPU:57, one launch (start us, length us, event | category | flops | bytes accessed | tf_op | source)
XLA Modules:
  0.0 155.9 jit_solution(17732048705142044975)
XLA Ops:
  4.1 0.8 reshape.388.tile_ref
  8.3 1.2 reshape.391
  9.6 14.9 %all-to-all-start = ((bf16[32,2,8320]{2,1,0:T(2,128)(2,1)}), bf16[32,2,8320]{2,1,0:T(2,128)(2,1)}, u32[]{:S(2)}, u32[]{:S(2)}) async-start(bf16[32,2,8320]{2,1,0:T(2,128)(2,1)} %reshape.391), calls=%async_computation | async-start | bytes 2129920 | tf_op jit(solution)/shard_map/all_to_all | solution.py:215
  25.2 3.1 %collective-permute-start = (bf16[1,4,64,128]{3,2,1,0:T(8,128)(2,1)}, bf16[1,4,64,128]{3,2,1,0:T(8,128)(2,1)S(1)}, u32[]{:S(2)}, u32[]{:S(2)}) collective-permute-start(bf16[1,4,64,128]{3,2,1,0:T(8,128)(2,1)} %bitcast.11), channel_id=1, source_target_pairs={{0,16},{16,32},{32,48},{48,64},{64,80},{80,96},{96,112},{112,128},... | collective-permute-start | bytes 196616 | tf_op jit(solution)/shard_map/ppermute | solution.py:65
  28.9 9.0 %collective-permute-start.2 = (bf16[4,1,64,128]{3,2,1,0:T(8,128)(2,1)S(1)}, bf16[4,1,64,128]{3,2,1,0:T(8,128)(2,1)}, u32[]{:S(2)}, u32[]{:S(2)}) collective-permute-start(bf16[4,1,64,128]{3,2,1,0:T(8,128)(2,1)S(1)} %get-tuple-element.29), channel_id=1, source_target_pairs={{0,1},{1,2},{2,3},{3,4},{4,5},{5,6},{6,7},{7,8},{8,9},{9,10},{10,1... | collective-permute-start | bytes 196616 | tf_op jit(solution)/shard_map/ppermute | solution.py:67
  37.9 1.9 %collective-permute-start.3 = (bf16[4,1,64,128]{3,2,1,0:T(8,128)(2,1)}, bf16[4,1,64,128]{3,2,1,0:T(8,128)(2,1)}, u32[]{:S(2)}, u32[]{:S(2)}) collective-permute-start(bf16[4,1,64,128]{3,2,1,0:T(8,128)(2,1)} %get-tuple-element.30), channel_id=1, source_target_pairs={{1,0},{2,1},{3,2},{4,3},{5,4},{6,5},{7,6},{8,7},{9,8},{10,9},{11,1... | collective-permute-start | bytes 196616 | tf_op jit(solution)/shard_map/ppermute | solution.py:68
  40.6 2.2 %collective-permute-start.1 = (bf16[1,4,64,128]{3,2,1,0:T(8,128)(2,1)}, bf16[1,4,64,128]{3,2,1,0:T(8,128)(2,1)S(1)}, u32[]{:S(2)}, u32[]{:S(2)}) collective-permute-start(bf16[1,4,64,128]{3,2,1,0:T(8,128)(2,1)} %bitcast.15), channel_id=1, source_target_pairs={{16,0},{32,16},{48,32},{64,48},{80,64},{96,80},{112,96},{128,112},... | collective-permute-start | bytes 196616 | tf_op jit(solution)/shard_map/ppermute | solution.py:66
  43.1 1.0 reshape.386
  45.2 0.8 copy.61
  46.0 1.0 fusion.34
  47.1 7.9 %collective-permute-done.3 = bf16[4,1,64,128]{3,2,1,0:T(8,128)(2,1)} collective-permute-done((bf16[4,1,64,128]{3,2,1,0:T(8,128)(2,1)}, bf16[4,1,64,128]{3,2,1,0:T(8,128)(2,1)}, u32[]{:S(2)}, u32[]{:S(2)}) %collective-permute-start.3) | collective-permute-done | bytes 65568 | tf_op jit(solution)/shard_map/ppermute | solution.py:68
  54.9 1.8 %fusion.38 = f32[4,4,128,64]{2,3,1,0:T(8,128)} fusion(bf16[4,1,64,128]{3,2,1,0:T(8,128)(2,1)} %collective-permute-done.3, bf16[4,3,64,128]{3,2,1,0:T(8,128)(2,1)S(1)} %get-tuple-element.32, bf16[4,4,5,64,64]{4,3,1,0,2:T(8,128)(2,1)S(1)} %reshape.386), kind=kOutput, calls=%fused_computation.62 | convolution fusion | flops 17301504 | bytes 1048576 | tf_op jit(solution)/shard_map/ijab,ijbf->ijaf/dot_general | solution.py:85
  56.8 4.6 %collective-permute-done = bf16[1,4,64,128]{3,2,1,0:T(8,128)(2,1)S(1)} collective-permute-done((bf16[1,4,64,128]{3,2,1,0:T(8,128)(2,1)}, bf16[1,4,64,128]{3,2,1,0:T(8,128)(2,1)S(1)}, u32[]{:S(2)}, u32[]{:S(2)}) %collective-permute-start) | collective-permute-done | bytes 65568 | tf_op jit(solution)/shard_map/ppermute | solution.py:65
  61.6 17.2 %all-to-all-done = bf16[32,2,8320]{2,1,0:T(2,128)(2,1)} async-done(((bf16[32,2,8320]{2,1,0:T(2,128)(2,1)}), bf16[32,2,8320]{2,1,0:T(2,128)(2,1)}, u32[]{:S(2)}, u32[]{:S(2)}) %all-to-all-start) | async-done | bytes 1064992 | tf_op jit(solution)/shard_map/all_to_all | solution.py:215
  79.6 1.6 convolution_bitcast_fusion
  81.3 0.9 copy-done.4
  82.2 0.9 fusion.12
  83.2 3.3 %shard_map.118 = bf16[64,64,128]{2,1,0:T(8,128)(2,1)} custom-call(s32[48]{0:T(128)} %bitcast.148, s32[48]{0:T(128)} %multiply_add_fusion.3.slot_ref, bf16[16,64,128]{2,1,0:T(8,128)(2,1)} %bitcast.130, bf16[48,64,64]{2,1,0:T(8,128)(2,1)} %copy-done.1), custom_call_target="tpu_custom_call" | custom-call | flops 50331648 | bytes 1703936 | tf_op jit(solution)/shard_map/pallas_call | solution.py:132
  86.5 11.2 %all-to-all-start.1 = ((bf16[32,2,64,128]{3,2,1,0:T(8,128)(2,1)}), bf16[32,2,64,128]{3,2,1,0:T(8,128)(2,1)}, u32[]{:S(2)}, u32[]{:S(2)}) async-start(bf16[32,2,64,128]{3,2,1,0:T(8,128)(2,1)} %bitcast.136), calls=%async_computation.1 | async-start | bytes 2097152 | tf_op jit(solution)/shard_map/all_to_all | solution.py:223
  98.9 3.1 %collective-permute-start.4 = (bf16[1,4,64,128]{3,2,1,0:T(8,128)(2,1)S(1)}, bf16[1,4,64,128]{3,2,1,0:T(8,128)(2,1)S(1)}, u32[]{:S(2)}, u32[]{:S(2)}) collective-permute-start(bf16[1,4,64,128]{3,2,1,0:T(8,128)(2,1)S(1)} %get-tuple-element.20), channel_id=1, source_target_pairs={{0,16},{16,32},{32,48},{48,64},{64,80},{80,96},{96,112},{112,128},... | collective-permute-start | bytes 196616 | tf_op jit(solution)/shard_map/ppermute | solution.py:65
  102.0 10.0 %collective-permute-start.6 = (bf16[4,1,64,128]{3,2,1,0:T(8,128)(2,1)S(1)}, bf16[4,1,64,128]{3,2,1,0:T(8,128)(2,1)S(1)}, u32[]{:S(2)}, u32[]{:S(2)}) collective-permute-start(bf16[4,1,64,128]{3,2,1,0:T(8,128)(2,1)S(1)} %get-tuple-element.21), channel_id=1, source_target_pairs={{0,1},{1,2},{2,3},{3,4},{4,5},{5,6},{6,7},{7,8},{8,9},{9,10},{10,1... | collective-permute-start | bytes 196616 | tf_op jit(solution)/shard_map/ppermute | solution.py:67
  112.0 1.9 %collective-permute-start.7 = (bf16[4,1,64,128]{3,2,1,0:T(8,128)(2,1)S(1)}, bf16[4,1,64,128]{3,2,1,0:T(8,128)(2,1)S(1)}, u32[]{:S(2)}, u32[]{:S(2)}) collective-permute-start(bf16[4,1,64,128]{3,2,1,0:T(8,128)(2,1)S(1)} %get-tuple-element.22), channel_id=1, source_target_pairs={{1,0},{2,1},{3,2},{4,3},{5,4},{6,5},{7,6},{8,7},{9,8},{10,9},{11,1... | collective-permute-start | bytes 196616 | tf_op jit(solution)/shard_map/ppermute | solution.py:68
  113.9 2.4 %collective-permute-start.5 = (bf16[1,4,64,128]{3,2,1,0:T(8,128)(2,1)S(1)}, bf16[1,4,64,128]{3,2,1,0:T(8,128)(2,1)S(1)}, u32[]{:S(2)}, u32[]{:S(2)}) collective-permute-start(bf16[1,4,64,128]{3,2,1,0:T(8,128)(2,1)S(1)} %get-tuple-element.19), channel_id=1, source_target_pairs={{16,0},{32,16},{48,32},{64,48},{80,64},{96,80},{112,96},{128,112},... | collective-permute-start | bytes 196616 | tf_op jit(solution)/shard_map/ppermute | solution.py:66
  116.6 1.0 convolution_add_fusion
  117.7 1.0 fusion.48
  118.7 10.2 %collective-permute-done.7 = bf16[4,1,64,128]{3,2,1,0:T(8,128)(2,1)S(1)} collective-permute-done((bf16[4,1,64,128]{3,2,1,0:T(8,128)(2,1)S(1)}, bf16[4,1,64,128]{3,2,1,0:T(8,128)(2,1)S(1)}, u32[]{:S(2)}, u32[]{:S(2)}) %collective-permute-start.7) | collective-permute-done | bytes 65568 | tf_op jit(solution)/shard_map/ppermute | solution.py:68
  128.9 1.0 fusion.52
  129.9 1.2 collective-permute-done.4
  131.3 19.6 %all-to-all-done.1 = bf16[32,2,64,128]{3,2,1,0:T(8,128)(2,1)} async-done(((bf16[32,2,64,128]{3,2,1,0:T(8,128)(2,1)}), bf16[32,2,64,128]{3,2,1,0:T(8,128)(2,1)}, u32[]{:S(2)}, u32[]{:S(2)}) %all-to-all-start.1) | async-done | bytes 1048608 | tf_op jit(solution)/shard_map/all_to_all | solution.py:223
  150.9 1.3 reshape.413
  152.3 0.8 convolution_bitcast_fusion.2
  153.7 0.8 copy-done.2
  (108 shorter events, 15.6 us)
Async XLA Ops:
  0.0 2.3 %copy-start.13 = (f32[32]{0:T(128)S(1)}, f32[32]{0:T(128)}, u32[]{:S(2)}) copy-start(f32[32]{0:T(128)} %param.17) | copy-start | bytes 388
  0.0 2.4 %copy-start.14 = (f32[32]{0:T(128)S(1)}, f32[32]{0:T(128)}, u32[]{:S(2)}) copy-start(f32[32]{0:T(128)} %param.18) | copy-start | bytes 388
  0.0 2.8 %copy-start.6 = (bf16[4,4,64,128]{3,2,1,0:T(8,128)(2,1)S(1)}, bf16[4,4,64,128]{3,2,1,0:T(8,128)(2,1)}, u32[]{:S(2)}) copy-start(bf16[4,4,64,128]{3,2,1,0:T(8,128)(2,1)} %param.14) | copy-start | bytes 786436
  3.1 0.7 copy-start.16
  3.1 1.0 copy-start.10
  5.0 1.1 copy-start.1
  6.0 0.7 copy-start.12
  6.1 1.1 copy-start.17
  9.6 33.2 %copy-start.9 = (bf16[4,4,5,4096]{3,1,2,0:T(4,128)(2,1)S(1)}, bf16[4,4,5,4096]{3,1,2,0:T(4,128)(2,1)}, u32[]{:S(2)}) copy-start(bf16[4,4,5,4096]{3,1,2,0:T(4,128)(2,1)} %param.19) | copy-start | bytes 1966084
  9.6 69.2 %all-to-all-start = ((bf16[32,2,8320]{2,1,0:T(2,128)(2,1)}), bf16[32,2,8320]{2,1,0:T(2,128)(2,1)}, u32[]{:S(2)}, u32[]{:S(2)}) async-start(bf16[32,2,8320]{2,1,0:T(2,128)(2,1)} %reshape.391), calls=%async_computation | async-start | bytes 2129920 | tf_op jit(solution)/shard_map/all_to_all | solution.py:215
  25.2 36.2 %collective-permute-start = (bf16[1,4,64,128]{3,2,1,0:T(8,128)(2,1)}, bf16[1,4,64,128]{3,2,1,0:T(8,128)(2,1)S(1)}, u32[]{:S(2)}, u32[]{:S(2)}) collective-permute-start(bf16[1,4,64,128]{3,2,1,0:T(8,128)(2,1)} %bitcast.11), channel_id=1, source_target_pairs={{0,16},{16,32},{32,48},{48,64},{64,80},{80,96},{96,112},{112,128},... | collective-permute-start | bytes 196616 | tf_op jit(solution)/shard_map/ppermute | solution.py:65
  28.9 17.1 %collective-permute-start.2 = (bf16[4,1,64,128]{3,2,1,0:T(8,128)(2,1)S(1)}, bf16[4,1,64,128]{3,2,1,0:T(8,128)(2,1)}, u32[]{:S(2)}, u32[]{:S(2)}) collective-permute-start(bf16[4,1,64,128]{3,2,1,0:T(8,128)(2,1)S(1)} %get-tuple-element.29), channel_id=1, source_target_pairs={{0,1},{1,2},{2,3},{3,4},{4,5},{5,6},{6,7},{7,8},{8,9},{9,10},{10,1... | collective-permute-start | bytes 196616 | tf_op jit(solution)/shard_map/ppermute | solution.py:67
  37.9 17.0 %collective-permute-start.3 = (bf16[4,1,64,128]{3,2,1,0:T(8,128)(2,1)}, bf16[4,1,64,128]{3,2,1,0:T(8,128)(2,1)}, u32[]{:S(2)}, u32[]{:S(2)}) collective-permute-start(bf16[4,1,64,128]{3,2,1,0:T(8,128)(2,1)} %get-tuple-element.30), channel_id=1, source_target_pairs={{1,0},{2,1},{3,2},{4,3},{5,4},{6,5},{7,6},{8,7},{9,8},{10,9},{11,1... | collective-permute-start | bytes 196616 | tf_op jit(solution)/shard_map/ppermute | solution.py:68
  40.6 40.8 %collective-permute-start.1 = (bf16[1,4,64,128]{3,2,1,0:T(8,128)(2,1)}, bf16[1,4,64,128]{3,2,1,0:T(8,128)(2,1)S(1)}, u32[]{:S(2)}, u32[]{:S(2)}) collective-permute-start(bf16[1,4,64,128]{3,2,1,0:T(8,128)(2,1)} %bitcast.15), channel_id=1, source_target_pairs={{16,0},{32,16},{48,32},{64,48},{80,64},{96,80},{112,96},{128,112},... | collective-permute-start | bytes 196616 | tf_op jit(solution)/shard_map/ppermute | solution.py:66
  81.1 1.1 copy-start.4
  81.2 1.1 copy-start.8
  86.5 11.3 %copy-start.11 = (bf16[3,32,32]{2,1,0:T(8,128)(2,1)S(1)}, bf16[3,32,32]{2,1,0:T(8,128)(2,1)}, u32[]{:S(2)}) copy-start(bf16[3,32,32]{2,1,0:T(8,128)(2,1)} %param.24) | copy-start | bytes 18436
  86.5 12.0 %copy-start.15 = (f32[32]{0:T(128)S(1)}, f32[32]{0:T(128)}, u32[]{:S(2)}) copy-start(f32[32]{0:T(128)} %param.25) | copy-start | bytes 388
  86.5 64.4 %all-to-all-start.1 = ((bf16[32,2,64,128]{3,2,1,0:T(8,128)(2,1)}), bf16[32,2,64,128]{3,2,1,0:T(8,128)(2,1)}, u32[]{:S(2)}, u32[]{:S(2)}) async-start(bf16[32,2,64,128]{3,2,1,0:T(8,128)(2,1)} %bitcast.136), calls=%async_computation.1 | async-start | bytes 2097152 | tf_op jit(solution)/shard_map/all_to_all | solution.py:223
  97.7 1.1 copy-start
  98.9 32.2 %collective-permute-start.4 = (bf16[1,4,64,128]{3,2,1,0:T(8,128)(2,1)S(1)}, bf16[1,4,64,128]{3,2,1,0:T(8,128)(2,1)S(1)}, u32[]{:S(2)}, u32[]{:S(2)}) collective-permute-start(bf16[1,4,64,128]{3,2,1,0:T(8,128)(2,1)S(1)} %get-tuple-element.20), channel_id=1, source_target_pairs={{0,16},{16,32},{32,48},{48,64},{64,80},{80,96},{96,112},{112,128},... | collective-permute-start | bytes 196616 | tf_op jit(solution)/shard_map/ppermute | solution.py:65
  102.0 15.7 %collective-permute-start.6 = (bf16[4,1,64,128]{3,2,1,0:T(8,128)(2,1)S(1)}, bf16[4,1,64,128]{3,2,1,0:T(8,128)(2,1)S(1)}, u32[]{:S(2)}, u32[]{:S(2)}) collective-permute-start(bf16[4,1,64,128]{3,2,1,0:T(8,128)(2,1)S(1)} %get-tuple-element.21), channel_id=1, source_target_pairs={{0,1},{1,2},{2,3},{3,4},{4,5},{5,6},{6,7},{7,8},{8,9},{9,10},{10,1... | collective-permute-start | bytes 196616 | tf_op jit(solution)/shard_map/ppermute | solution.py:67
  112.0 16.9 %collective-permute-start.7 = (bf16[4,1,64,128]{3,2,1,0:T(8,128)(2,1)S(1)}, bf16[4,1,64,128]{3,2,1,0:T(8,128)(2,1)S(1)}, u32[]{:S(2)}, u32[]{:S(2)}) collective-permute-start(bf16[4,1,64,128]{3,2,1,0:T(8,128)(2,1)S(1)} %get-tuple-element.22), channel_id=1, source_target_pairs={{1,0},{2,1},{3,2},{4,3},{5,4},{6,5},{7,6},{8,7},{9,8},{10,9},{11,1... | collective-permute-start | bytes 196616 | tf_op jit(solution)/shard_map/ppermute | solution.py:68
  113.9 39.2 %collective-permute-start.5 = (bf16[1,4,64,128]{3,2,1,0:T(8,128)(2,1)S(1)}, bf16[1,4,64,128]{3,2,1,0:T(8,128)(2,1)S(1)}, u32[]{:S(2)}, u32[]{:S(2)}) collective-permute-start(bf16[1,4,64,128]{3,2,1,0:T(8,128)(2,1)S(1)} %get-tuple-element.19), channel_id=1, source_target_pairs={{16,0},{32,16},{48,32},{64,48},{80,64},{96,80},{112,96},{128,112},... | collective-permute-start | bytes 196616 | tf_op jit(solution)/shard_map/ppermute | solution.py:66
  152.3 1.0 copy-start.3
  152.3 1.2 copy-start.5
  153.5 1.0 copy-start.2
  153.7 1.4 copy-start.7

commit v12 on v11

--- a/solution.py
+++ b/solution.py
@@ -170,6 +170,46 @@
     return slots.reshape(lax.axis_size("rx"), CAP, -1)
 
 
+def gather_kernel(tgt_ref, near_ref, recv_ref, out_ref):
+    out_ref[...] = near_ref[...]
+
+    def body(slot, carry):
+        target = tgt_ref[slot]
+
+        @pl.when(target >= 0)
+        def _():
+            row = jnp.maximum(target, 0)
+            out_ref[row] = out_ref[row] + recv_ref[slot].astype(jnp.float32)
+
+        return carry
+
+    lax.fori_loop(0, recv_ref.shape[0], body, 0, unroll=True)
+
+
+def add_far(near, received, targets):
+    nblocks, block_size, features = near.shape
+    nslots = targets.shape[0]
+    whole = lambda i, t: (0, 0, 0)
+    return pl.pallas_call(
+        gather_kernel,
+        out_shape=jax.ShapeDtypeStruct(near.shape, jnp.float32),
+        grid_spec=pltpu.PrefetchScalarGridSpec(
+            num_scalar_prefetch=1,
+            grid=(1,),
+            in_specs=[
+                pl.BlockSpec((nblocks, block_size, features), whole),
+                pl.BlockSpec((nslots, block_size, features), whole),
+            ],
+            out_specs=pl.BlockSpec((nblocks, block_size, features), whole),
+        ),
+        cost_estimate=pl.CostEstimate(
+            flops=nslots * block_size * features,
+            bytes_accessed=(8 * nblocks + 2 * nslots) * block_size * features,
+            transcendentals=0,
+        ),
+    )(targets, near, received.reshape(nslots, block_size, features))
+
+
 def far_terms(received, targets, nblocks):
     onehot = (targets[None] == jnp.arange(nblocks, dtype=jnp.int32)[:, None, None]).astype(
         jnp.bfloat16
@@ -222,8 +262,9 @@
     halo_two = fetch_halo(first_hop)
     recv_two = lax.all_to_all(send_two, "rx", split_axis=0, concat_axis=0, tiled=True)
     near_two = local_terms(first_hop, tiles, halo_two)
-    far_two = far_terms(recv_two, targets, nblocks)
-    second_hop = near_two + far_two.reshape(gated.shape)
+    second_hop = add_far(
+        near_two.reshape(nblocks, block_size, features), recv_two, targets.reshape(-1)
+    ).reshape(gated.shape)
 
     input_signals, output_signals = group_eye(channels)
     diagonal = (input_signals == output_signals).astype(jnp.float32)

time: 157 us -> 159 us (1.013)
  Pallas kernels: 3.31 us -> 6.96 us
  waiting for transfers between devices: 60.7 us -> 59 us
    ppermute x2, waiting for transfers between devices: 5.82 us -> 17.6 us  [fetch_halo(): above = lax.ppermute(signal[-1:], 'rx', shift_pairs(n_rx, 1))]
    ppermute x2, waiting for transfers between devices: 18 us -> 8.57 us  [fetch_halo(): right = lax.ppermute(signal[:, :1], 'ry', shift_pairs(n_ry, -1))]
    all_to_all x1, waiting for transfers between devices: 19.6 us -> 15.5 us  [local(): lax.all_to_all(send_two, 'rx', split_axis=0, concat_axis=0, tiled=True)]
    pallas_call x0 -> x1, Pallas kernels: none -> 3.64 us  [add_far(): pl.pallas_call(gather_kernel, out_shape=jax.ShapeDtypeStruct(near.shape,...]
    unnamed x42 -> x37, local copies, waits for them, and re-layouts: 3.95 us -> 2.67 us
  transfers between devices with their start and end apart: 10 -> 10, of which waited for: 6 -> 5; matrix products, arithmetic and copies ran while one was open for 11% -> 12% of each run, Pallas kernels for 0% -> 0%
where the time goes in v12:
time: 159 us; the launch traced here: 158 us
  starting transfers between devices  59.1 us (37%)
  waiting for transfers between devices  59 us (37%)
  local copies, waits for them, and re-layouts  13.9 us (9%)
  matrix products  12.9 us (8%)
  Pallas kernels  6.96 us (4%)
  other arithmetic  5.21 us (3%)
    ppermute x2, starting transfers between devices, fetch_halo(): left = lax.ppermute(signal[:, -1:], 'ry', shift_pairs(n_ry, 1))  18 us
    ppermute x2, waiting for transfers between devices, fetch_halo(): above = lax.ppermute(signal[-1:], 'rx', shift_pairs(n_rx, 1))  17.6 us
    all_to_all x1, waiting for transfers between devices, local(): lax.all_to_all(send_one, 'rx', split_axis=0, concat_axis=0, tiled=True)  17.3 us
    all_to_all x1, waiting for transfers between devices, local(): lax.all_to_all(send_two, 'rx', split_axis=0, concat_axis=0, tiled=True)  15.5 us
    all_to_all x1, starting transfers between devices, local(): lax.all_to_all(send_one, 'rx', split_axis=0, concat_axis=0, tiled=True)  14.9 us
    all_to_all x1, starting transfers between devices, local(): lax.all_to_all(send_two, 'rx', split_axis=0, concat_axis=0, tiled=True)  11.2 us
    ppermute x2, waiting for transfers between devices, fetch_halo(): right = lax.ppermute(signal[:, :1], 'ry', shift_pairs(n_ry, -1))  8.57 us
    dot_general x8, matrix products, local_terms(): jnp.einsum('ijab,ijbf->ijaf', tiles[:, :, offset], neighbours[offset], pr...  7.39 us
  transfers between devices with their start and end apart: 10, of which 5 were waited for; matrix products, arithmetic and copies ran while one was open for 12% of the time, Pallas kernels for 0%

profile of v12, /device:TPU:57, one launch (start us, length us, event | category | flops | bytes accessed | tf_op | source)
XLA Modules:
  0.0 157.6 jit_solution(15991068484256938992)
XLA Ops:
  4.1 0.8 reshape.390.tile_ref
  8.3 1.2 reshape.393
  9.6 14.9 %all-to-all-start = ((bf16[32,2,8320]{2,1,0:T(2,128)(2,1)}), bf16[32,2,8320]{2,1,0:T(2,128)(2,1)}, u32[]{:S(2)}, u32[]{:S(2)}) async-start(bf16[32,2,8320]{2,1,0:T(2,128)(2,1)} %reshape.393), calls=%async_computation | async-start | bytes 2129920 | tf_op jit(solution)/shard_map/all_to_all | solution.py:255
  24.6 3.1 %collective-permute-start = (bf16[1,4,64,128]{3,2,1,0:T(8,128)(2,1)S(1)}, bf16[1,4,64,128]{3,2,1,0:T(8,128)(2,1)S(1)}, u32[]{:S(2)}, u32[]{:S(2)}) collective-permute-start(bf16[1,4,64,128]{3,2,1,0:T(8,128)(2,1)S(1)} %bitcast.121), channel_id=1, source_target_pairs={{0,16},{16,32},{32,48},{48,64},{64,80},{80,96},{96,112},{112,128},... | collective-permute-start | bytes 196616 | tf_op jit(solution)/shard_map/ppermute | solution.py:65
  28.4 9.0 %collective-permute-start.2 = (bf16[4,1,64,128]{3,2,1,0:T(8,128)(2,1)}, bf16[4,1,64,128]{3,2,1,0:T(8,128)(2,1)S(1)}, u32[]{:S(2)}, u32[]{:S(2)}) collective-permute-start(bf16[4,1,64,128]{3,2,1,0:T(8,128)(2,1)} %get-tuple-element.31), channel_id=1, source_target_pairs={{0,1},{1,2},{2,3},{3,4},{4,5},{5,6},{6,7},{7,8},{8,9},{9,10},{10,1... | collective-permute-start | bytes 196616 | tf_op jit(solution)/shard_map/ppermute | solution.py:67
  37.4 1.9 %collective-permute-start.3 = (bf16[4,1,64,128]{3,2,1,0:T(8,128)(2,1)}, bf16[4,1,64,128]{3,2,1,0:T(8,128)(2,1)}, u32[]{:S(2)}, u32[]{:S(2)}) collective-permute-start(bf16[4,1,64,128]{3,2,1,0:T(8,128)(2,1)} %get-tuple-element.32), channel_id=1, source_target_pairs={{1,0},{2,1},{3,2},{4,3},{5,4},{6,5},{7,6},{8,7},{9,8},{10,9},{11,1... | collective-permute-start | bytes 196616 | tf_op jit(solution)/shard_map/ppermute | solution.py:68
  40.0 2.2 %collective-permute-start.1 = (bf16[1,4,64,128]{3,2,1,0:T(8,128)(2,1)}, bf16[1,4,64,128]{3,2,1,0:T(8,128)(2,1)S(1)}, u32[]{:S(2)}, u32[]{:S(2)}) collective-permute-start(bf16[1,4,64,128]{3,2,1,0:T(8,128)(2,1)} %bitcast.15), channel_id=1, source_target_pairs={{16,0},{32,16},{48,32},{64,48},{80,64},{96,80},{112,96},{128,112},... | collective-permute-start | bytes 196616 | tf_op jit(solution)/shard_map/ppermute | solution.py:66
  42.5 1.0 reshape.388
  44.6 0.8 copy.44
  45.6 8.6 %collective-permute-done.3 = bf16[4,1,64,128]{3,2,1,0:T(8,128)(2,1)} collective-permute-done((bf16[4,1,64,128]{3,2,1,0:T(8,128)(2,1)}, bf16[4,1,64,128]{3,2,1,0:T(8,128)(2,1)}, u32[]{:S(2)}, u32[]{:S(2)}) %collective-permute-start.3) | collective-permute-done | bytes 65568 | tf_op jit(solution)/shard_map/ppermute | solution.py:68
  54.2 1.8 %fusion.35 = f32[4,4,128,64]{2,3,1,0:T(8,128)} fusion(bf16[4,1,64,128]{3,2,1,0:T(8,128)(2,1)} %collective-permute-done.3, bf16[4,3,64,128]{3,2,1,0:T(8,128)(2,1)S(1)} %get-tuple-element.34, bf16[4,4,5,64,64]{4,3,1,0,2:T(8,128)(2,1)S(1)} %reshape.388), kind=kOutput, calls=%fused_computation.56 | convolution fusion | flops 17301504 | bytes 1048576 | tf_op jit(solution)/shard_map/ijab,ijbf->ijaf/dot_general | solution.py:85
  56.0 5.2 %collective-permute-done = bf16[1,4,64,128]{3,2,1,0:T(8,128)(2,1)S(1)} collective-permute-done((bf16[1,4,64,128]{3,2,1,0:T(8,128)(2,1)S(1)}, bf16[1,4,64,128]{3,2,1,0:T(8,128)(2,1)S(1)}, u32[]{:S(2)}, u32[]{:S(2)}) %collective-permute-start) | collective-permute-done | bytes 65568 | tf_op jit(solution)/shard_map/ppermute | solution.py:65
  61.5 17.3 %all-to-all-done = bf16[32,2,8320]{2,1,0:T(2,128)(2,1)} async-done(((bf16[32,2,8320]{2,1,0:T(2,128)(2,1)}), bf16[32,2,8320]{2,1,0:T(2,128)(2,1)}, u32[]{:S(2)}, u32[]{:S(2)}) %all-to-all-start) | async-done | bytes 1064992 | tf_op jit(solution)/shard_map/all_to_all | solution.py:255
  78.8 1.3 fusion.88
  80.2 1.6 convolution_bitcast_fusion
  81.9 0.9 copy-done.2
  82.8 0.9 fusion.10
  83.8 3.3 %shard_map.118 = bf16[64,64,128]{2,1,0:T(8,128)(2,1)} custom-call(s32[48]{0:T(128)} %bitcast.126, s32[48]{0:T(128)} %multiply_add_fusion.2.slot_ref, bf16[16,64,128]{2,1,0:T(8,128)(2,1)} %bitcast.105, bf16[48,64,64]{2,1,0:T(8,128)(2,1)} %copy-done.1), custom_call_target="tpu_custom_call" | custom-call | flops 50331648 | bytes 1703936 | tf_op jit(solution)/shard_map/pallas_call | solution.py:132
  87.1 11.2 %all-to-all-start.1 = ((bf16[32,2,64,128]{3,2,1,0:T(8,128)(2,1)}), bf16[32,2,64,128]{3,2,1,0:T(8,128)(2,1)}, u32[]{:S(2)}, u32[]{:S(2)}) async-start(bf16[32,2,64,128]{3,2,1,0:T(8,128)(2,1)} %bitcast.111), calls=%async_computation.1 | async-start | bytes 2097152 | tf_op jit(solution)/shard_map/all_to_all | solution.py:263
  100.7 3.1 %collective-permute-start.4 = (bf16[1,4,64,128]{3,2,1,0:T(8,128)(2,1)}, bf16[1,4,64,128]{3,2,1,0:T(8,128)(2,1)}, u32[]{:S(2)}, u32[]{:S(2)}) collective-permute-start(bf16[1,4,64,128]{3,2,1,0:T(8,128)(2,1)} %get-tuple-element.22), channel_id=1, source_target_pairs={{0,16},{16,32},{32,48},{48,64},{64,80},{80,96},{96,112},{112,128},... | collective-permute-start | bytes 196616 | tf_op jit(solution)/shard_map/ppermute | solution.py:65
  104.5 9.0 %collective-permute-start.6 = (bf16[4,1,64,128]{3,2,1,0:T(8,128)(2,1)}, bf16[4,1,64,128]{3,2,1,0:T(8,128)(2,1)}, u32[]{:S(2)}, u32[]{:S(2)}) collective-permute-start(bf16[4,1,64,128]{3,2,1,0:T(8,128)(2,1)} %get-tuple-element.23), channel_id=1, source_target_pairs={{0,1},{1,2},{2,3},{3,4},{4,5},{5,6},{6,7},{7,8},{8,9},{9,10},{10,1... | collective-permute-start | bytes 196616 | tf_op jit(solution)/shard_map/ppermute | solution.py:67
  113.5 1.9 %collective-permute-start.7 = (bf16[4,1,64,128]{3,2,1,0:T(8,128)(2,1)}, bf16[4,1,64,128]{3,2,1,0:T(8,128)(2,1)}, u32[]{:S(2)}, u32[]{:S(2)}) collective-permute-start(bf16[4,1,64,128]{3,2,1,0:T(8,128)(2,1)} %get-tuple-element.24), channel_id=1, source_target_pairs={{1,0},{2,1},{3,2},{4,3},{5,4},{6,5},{7,6},{8,7},{9,8},{10,9},{11,1... | collective-permute-start | bytes 196616 | tf_op jit(solution)/shard_map/ppermute | solution.py:68
  115.4 2.8 %collective-permute-start.5 = (bf16[1,4,64,128]{3,2,1,0:T(8,128)(2,1)}, bf16[1,4,64,128]{3,2,1,0:T(8,128)(2,1)S(1)}, u32[]{:S(2)}, u32[]{:S(2)}) collective-permute-start(bf16[1,4,64,128]{3,2,1,0:T(8,128)(2,1)} %get-tuple-element.21), channel_id=1, source_target_pairs={{16,0},{32,16},{48,32},{64,48},{80,64},{96,80},{112,96},{128,112},... | collective-permute-start | bytes 196616 | tf_op jit(solution)/shard_map/ppermute | solution.py:66
  119.4 12.4 %collective-permute-done.4 = bf16[1,4,64,128]{3,2,1,0:T(8,128)(2,1)} collective-permute-done((bf16[1,4,64,128]{3,2,1,0:T(8,128)(2,1)}, bf16[1,4,64,128]{3,2,1,0:T(8,128)(2,1)}, u32[]{:S(2)}, u32[]{:S(2)}) %collective-permute-start.4) | collective-permute-done | bytes 65568 | tf_op jit(solution)/shard_map/ppermute | solution.py:65
  131.8 1.0 convolution_add_fusion.2
  132.9 1.1 fusion.45
  134.0 1.1 fusion.49
  135.0 1.0 fusion.4
  136.1 15.5 %all-to-all-done.1 = bf16[32,2,64,128]{3,2,1,0:T(8,128)(2,1)} async-done(((bf16[32,2,64,128]{3,2,1,0:T(8,128)(2,1)}), bf16[32,2,64,128]{3,2,1,0:T(8,128)(2,1)}, u32[]{:S(2)}, u32[]{:S(2)}) %all-to-all-start.1) | async-done | bytes 1048608 | tf_op jit(solution)/shard_map/all_to_all | solution.py:263
  151.5 3.6 %shard_map.119 = f32[16,64,128]{2,1,0:T(8,128)} custom-call(s32[64]{0:T(128)} %sub.22.tgt_ref, f32[16,64,128]{2,1,0:T(8,128)} %bitcast.113, bf16[64,64,128]{2,1,0:T(8,128)(2,1)} %bitcast.36.recv_ref), custom_call_target="tpu_custom_call" | custom-call | flops 524288 | bytes 2097152 | tf_op jit(solution)/shard_map/pallas_call | solution.py:193
  155.2 1.6 %fusion.9 = f32[1024,128]{1,0:T(8,128)S(1)} fusion(f32[1024,128]{1,0:T(8,128)S(1)} %convolution_add_fusion, f32[1024,128]{1,0:T(8,128)} %bitcast.114, f32[128,128]{1,0:T(8,128)S(1)} %mul.258, f32[128]{0:T(128)S(1)} %copy-done.9), kind=kOutput, calls=%fused_computation.21 | convolution fusion | flops 201588736 | bytes 1638912 | tf_op jit(solution)/shard_map/ngk,kj->ngj/dot_general | solution.py:285
  156.8 0.8 add_convert_fusion
  (102 shorter events, 14.9 us)
Async XLA Ops:
  0.0 2.3 %copy-start.11 = (f32[32]{0:T(128)S(1)}, f32[32]{0:T(128)}, u32[]{:S(2)}) copy-start(f32[32]{0:T(128)} %param.17) | copy-start | bytes 388
  0.0 2.4 %copy-start.12 = (f32[32]{0:T(128)S(1)}, f32[32]{0:T(128)}, u32[]{:S(2)}) copy-start(f32[32]{0:T(128)} %param.18) | copy-start | bytes 388
  0.0 2.8 %copy-start.3 = (bf16[4,4,64,128]{3,2,1,0:T(8,128)(2,1)S(1)}, bf16[4,4,64,128]{3,2,1,0:T(8,128)(2,1)}, u32[]{:S(2)}) copy-start(bf16[4,4,64,128]{3,2,1,0:T(8,128)(2,1)} %param.14) | copy-start | bytes 786436
  3.1 0.7 copy-start.14
  3.1 1.0 copy-start.7
  5.0 1.1 copy-start.1
  6.0 0.7 copy-start.10
  6.1 1.1 copy-start.15
  9.6 32.6 %copy-start.6 = (bf16[4,4,5,4096]{3,1,2,0:T(4,128)(2,1)S(1)}, bf16[4,4,5,4096]{3,1,2,0:T(4,128)(2,1)}, u32[]{:S(2)}) copy-start(bf16[4,4,5,4096]{3,1,2,0:T(4,128)(2,1)} %param.19) | copy-start | bytes 1966084
  9.6 69.2 %all-to-all-start = ((bf16[32,2,8320]{2,1,0:T(2,128)(2,1)}), bf16[32,2,8320]{2,1,0:T(2,128)(2,1)}, u32[]{:S(2)}, u32[]{:S(2)}) async-start(bf16[32,2,8320]{2,1,0:T(2,128)(2,1)} %reshape.393), calls=%async_computation | async-start | bytes 2129920 | tf_op jit(solution)/shard_map/all_to_all | solution.py:255
  24.6 36.7 %collective-permute-start = (bf16[1,4,64,128]{3,2,1,0:T(8,128)(2,1)S(1)}, bf16[1,4,64,128]{3,2,1,0:T(8,128)(2,1)S(1)}, u32[]{:S(2)}, u32[]{:S(2)}) collective-permute-start(bf16[1,4,64,128]{3,2,1,0:T(8,128)(2,1)S(1)} %bitcast.121), channel_id=1, source_target_pairs={{0,16},{16,32},{32,48},{48,64},{64,80},{80,96},{96,112},{112,128},... | collective-permute-start | bytes 196616 | tf_op jit(solution)/shard_map/ppermute | solution.py:65
  28.4 17.0 %collective-permute-start.2 = (bf16[4,1,64,128]{3,2,1,0:T(8,128)(2,1)}, bf16[4,1,64,128]{3,2,1,0:T(8,128)(2,1)S(1)}, u32[]{:S(2)}, u32[]{:S(2)}) collective-permute-start(bf16[4,1,64,128]{3,2,1,0:T(8,128)(2,1)} %get-tuple-element.31), channel_id=1, source_target_pairs={{0,1},{1,2},{2,3},{3,4},{4,5},{5,6},{6,7},{7,8},{8,9},{9,10},{10,1... | collective-permute-start | bytes 196616 | tf_op jit(solution)/shard_map/ppermute | solution.py:67
  37.4 16.8 %collective-permute-start.3 = (bf16[4,1,64,128]{3,2,1,0:T(8,128)(2,1)}, bf16[4,1,64,128]{3,2,1,0:T(8,128)(2,1)}, u32[]{:S(2)}, u32[]{:S(2)}) collective-permute-start(bf16[4,1,64,128]{3,2,1,0:T(8,128)(2,1)} %get-tuple-element.32), channel_id=1, source_target_pairs={{1,0},{2,1},{3,2},{4,3},{5,4},{6,5},{7,6},{8,7},{9,8},{10,9},{11,1... | collective-permute-start | bytes 196616 | tf_op jit(solution)/shard_map/ppermute | solution.py:68
  40.0 41.9 %collective-permute-start.1 = (bf16[1,4,64,128]{3,2,1,0:T(8,128)(2,1)}, bf16[1,4,64,128]{3,2,1,0:T(8,128)(2,1)S(1)}, u32[]{:S(2)}, u32[]{:S(2)}) collective-permute-start(bf16[1,4,64,128]{3,2,1,0:T(8,128)(2,1)} %bitcast.15), channel_id=1, source_target_pairs={{16,0},{32,16},{48,32},{64,48},{80,64},{96,80},{112,96},{128,112},... | collective-permute-start | bytes 196616 | tf_op jit(solution)/shard_map/ppermute | solution.py:66
  81.7 1.1 copy-start.2
  81.7 1.1 copy-start.5
  87.1 11.3 %copy-start.8 = (bf16[3,32,32]{2,1,0:T(8,128)(2,1)S(1)}, bf16[3,32,32]{2,1,0:T(8,128)(2,1)}, u32[]{:S(2)}) copy-start(bf16[3,32,32]{2,1,0:T(8,128)(2,1)} %param.24) | copy-start | bytes 18436
  87.1 12.0 %copy-start.13 = (f32[32]{0:T(128)S(1)}, f32[32]{0:T(128)}, u32[]{:S(2)}) copy-start(f32[32]{0:T(128)} %param.25) | copy-start | bytes 388
  87.1 64.4 %all-to-all-start.1 = ((bf16[32,2,64,128]{3,2,1,0:T(8,128)(2,1)}), bf16[32,2,64,128]{3,2,1,0:T(8,128)(2,1)}, u32[]{:S(2)}, u32[]{:S(2)}) async-start(bf16[32,2,64,128]{3,2,1,0:T(8,128)(2,1)} %bitcast.111), calls=%async_computation.1 | async-start | bytes 2097152 | tf_op jit(solution)/shard_map/all_to_all | solution.py:263
  98.3 1.7 %copy-start = (bf16[4,4,64,128]{3,2,1,0:T(8,128)(2,1)S(1)}, bf16[4,4,64,128]{3,2,1,0:T(8,128)(2,1)}, u32[]{:S(2)}) copy-start(bf16[4,4,64,128]{3,2,1,0:T(8,128)(2,1)} %fusion.10) | copy-start | bytes 786436
  100.7 31.1 %collective-permute-start.4 = (bf16[1,4,64,128]{3,2,1,0:T(8,128)(2,1)}, bf16[1,4,64,128]{3,2,1,0:T(8,128)(2,1)}, u32[]{:S(2)}, u32[]{:S(2)}) collective-permute-start(bf16[1,4,64,128]{3,2,1,0:T(8,128)(2,1)} %get-tuple-element.22), channel_id=1, source_target_pairs={{0,16},{16,32},{32,48},{48,64},{64,80},{80,96},{96,112},{112,128},... | collective-permute-start | bytes 196616 | tf_op jit(solution)/shard_map/ppermute | solution.py:65
  104.5 28.4 %collective-permute-start.6 = (bf16[4,1,64,128]{3,2,1,0:T(8,128)(2,1)}, bf16[4,1,64,128]{3,2,1,0:T(8,128)(2,1)}, u32[]{:S(2)}, u32[]{:S(2)}) collective-permute-start(bf16[4,1,64,128]{3,2,1,0:T(8,128)(2,1)} %get-tuple-element.23), channel_id=1, source_target_pairs={{0,1},{1,2},{2,3},{3,4},{4,5},{5,6},{6,7},{7,8},{8,9},{9,10},{10,1... | collective-permute-start | bytes 196616 | tf_op jit(solution)/shard_map/ppermute | solution.py:67
  113.5 20.5 %collective-permute-start.7 = (bf16[4,1,64,128]{3,2,1,0:T(8,128)(2,1)}, bf16[4,1,64,128]{3,2,1,0:T(8,128)(2,1)}, u32[]{:S(2)}, u32[]{:S(2)}) collective-permute-start(bf16[4,1,64,128]{3,2,1,0:T(8,128)(2,1)} %get-tuple-element.24), channel_id=1, source_target_pairs={{1,0},{2,1},{3,2},{4,3},{5,4},{6,5},{7,6},{8,7},{9,8},{10,9},{11,1... | collective-permute-start | bytes 196616 | tf_op jit(solution)/shard_map/ppermute | solution.py:68
  115.4 19.6 %collective-permute-start.5 = (bf16[1,4,64,128]{3,2,1,0:T(8,128)(2,1)}, bf16[1,4,64,128]{3,2,1,0:T(8,128)(2,1)S(1)}, u32[]{:S(2)}, u32[]{:S(2)}) collective-permute-start(bf16[1,4,64,128]{3,2,1,0:T(8,128)(2,1)} %get-tuple-element.21), channel_id=1, source_target_pairs={{16,0},{32,16},{48,32},{64,48},{80,64},{96,80},{112,96},{128,112},... | collective-permute-start | bytes 196616 | tf_op jit(solution)/shard_map/ppermute | solution.py:66
  136.1 19.1 %copy-start.9 = (f32[128]{0:T(128)S(1)}, f32[128]{0:T(128)}, u32[]{:S(2)}) copy-start(f32[128]{0:T(128)} %add.197) | copy-start | bytes 1540
  155.2 1.7 %copy-start.4 = (bf16[4,4,64,128]{3,2,1,0:T(8,128)(2,1)S(1)}, bf16[4,4,64,128]{3,2,1,0:T(8,128)(2,1)}, u32[]{:S(2)}) copy-start(bf16[4,4,64,128]{3,2,1,0:T(8,128)(2,1)} %param.14) | copy-start | bytes 786436
